TPU v7x, 32 devices: a whole 2x2x4 slice. The times are simulated.
32 devices in a mesh: comp: 8 (over y, x, core), tile: 4 (over z).
Axes of the slice: x: 2, y: 2, z: 4, core: 2. Of those that a mesh axis runs over, the one named last changes fastest.
Arguments:
- atm_state: float32 [128, 128, 512], P(None, 'comp', 'tile'), may hold values from -6 to 6
- ocean_state: float32 [48, 128, 512], P(None, 'comp', 'tile'), may hold values from -6 to 6
- atm_rate: float32 [128], replicated, may hold values from 0.02 to 0.24
- ocean_rate: float32 [48], replicated, may hold values from 0.02 to 0.24
- ocean_mask: int32 [128, 4], P('comp', 'tile'), may hold values 0 or 1
- remap_weight: bfloat16 [8, 192, 128, 128], P('comp', 'tile'), may hold values from -0.5 to 0.5
- pair_src: int32 [8, 192], P('comp', 'tile'), may hold values from 0 to 63, as said below
- pair_tgt: int32 [8, 192], P('comp', 'tile'), may hold values from 0 to 63, as said below
- pair_count: int32 [8, 4], P('comp', 'tile'), may hold values from 24 to 48, as said below
Outputs:
- atm_next: float32 [128, 128, 512], P(None, 'comp', 'tile')
- ocean_next: float32 [48, 128, 512], P(None, 'comp', 'tile')
Inputs may be any that keep to these rules, and one draw needn't show every extreme that they name: `pair_src`: entry d * 48 + j of row b names atmosphere tile e * 16 + y of band b. Among the first pair_count[b, d] entries of device d at most 13 have the same e, and every device has 13 live entries with one same e. `pair_tgt`: entry d * 48 + j of row b names ocean tile e * 16 + y of band b. Among the first pair_count[b, d] entries of device d at most 13 have the same e, and every device has 13 live entries with one same e. `pair_count`: each row b has some device with 48 live slots.
All inputs are finite; a program needn't handle non-finite values. No bound on the sum of `ocean_mask` on one device may be relied on, other than what follows from the above.
Results may differ from a plain program's by a relative error of at most 0.002.
Values may be sent and summed in bfloat16 or wider, within the bound.
No kernel may reach another device: no remote copies, remote signals or barrier semaphores. Data moves between devices by JAX's collectives and lax.ppermute only.
A program may use at most 64 MiB of HBM per device.

v0:
```python
import jax
import jax.numpy as jnp
from jax import lax
from jax.sharding import PartitionSpec as P

SURF = 8


def padded_2(block, sides, width):
    for axis, dim in sides:
        count = lax.axis_size(axis)
        forward = [(i, i + 1) for i in range(count - 1)]
        forward.append((count - 1, 0))
        backward = [(target, source) for source, target in forward]
        low = lax.ppermute(
            lax.slice_in_dim(block, block.shape[dim] - width, None, axis=dim), axis, forward
        )
        high = lax.ppermute(lax.slice_in_dim(block, 0, width, axis=dim), axis, backward)
        block = jnp.concatenate([low, block, high], axis=dim)
    return block


def relax(padded, spread):
    center = padded[:, 1:-1, 1:-1]
    beside_all = (
        padded[:, 2:, 1:-1] + padded[:, :-2, 1:-1] + padded[:, 1:-1, 2:] + padded[:, 1:-1, :-2]
    )
    return center + spread[:, None, None] * (beside_all - 4.0 * center)


def ghosts(padded, width):
    row_total = padded.shape[1]
    row_index = jnp.arange(row_total)
    position = lax.axis_index("comp")
    at_first = jnp.logical_and(row_index < width, position == 0)
    at_last = jnp.logical_and(row_index >= row_total - width, position == lax.axis_size("comp") - 1)
    retain = jnp.logical_not(jnp.logical_or(at_first, at_last)).astype(jnp.float32)
    return padded * retain[None, :, None]


def shards(
    atm_state,
    ocean_state,
    atm_rate,
    ocean_rate,
    ocean_mask,
    remap_weight,
    pair_src,
    pair_tgt,
    pair_count,
):
    atm_rows = atm_state.shape[1]
    ocean_rows = ocean_state.shape[1]
    cell_total = atm_state.shape[2]
    pair_total = pair_src.shape[1]
    wet_rows = ocean_mask[:, 0].astype(jnp.float32)
    atm_source = atm_state[:SURF].astype(jnp.bfloat16)
    ocean_source = (ocean_state[:SURF] * wet_rows[None, :, None]).astype(jnp.bfloat16)
    atm_band, ocean_band = (
        lax.all_gather(atm_source, "tile", axis=1, tiled=True),
        lax.all_gather(ocean_source, "tile", axis=1, tiled=True),
    )
    anchor = pair_src[0]
    target = pair_tgt[0]
    active = jnp.arange(pair_total) < pair_count[0, 0]
    active_float = active.astype(jnp.float32)[:, None, None]
    weights = remap_weight[0]
    forward = (
        jnp.einsum(
            "fpt,pts->pfs",
            jnp.take(atm_band, anchor, axis=1),
            weights,
            preferred_element_type=jnp.float32,
        )
        * active_float
    )
    reverse = (
        jnp.einsum(
            "fps,pts->pft",
            jnp.take(ocean_band, target, axis=1),
            weights,
            preferred_element_type=jnp.float32,
        )
        * active_float
    )
    band_rows = atm_rows + ocean_rows
    ahead_codes = jnp.where(
        active, target // ocean_rows * band_rows + atm_rows + target % ocean_rows, -1
    )
    back_codes = jnp.where(active, anchor // atm_rows * band_rows + anchor % atm_rows, -1)
    ahead_flat = forward.reshape(pair_total, -1)
    back_flat = reverse.reshape(pair_total, -1)
    row_codes = jnp.arange(band_rows * lax.axis_size("tile"))
    ahead_hot = (row_codes[:, None] == ahead_codes[None, :]).astype(jnp.float32)
    back_hot = (row_codes[:, None] == back_codes[None, :]).astype(jnp.float32)
    summed = lax.psum_scatter(
        jnp.dot(
            ahead_hot,
            ahead_flat,
            precision=lax.Precision.HIGHEST,
            preferred_element_type=jnp.float32,
        )
        + jnp.dot(
            back_hot, back_flat, precision=lax.Precision.HIGHEST, preferred_element_type=jnp.float32
        ),
        "tile",
        scatter_dimension=0,
        tiled=True,
    )
    atm_force = summed[:atm_rows].reshape(atm_rows, SURF, cell_total)
    ocean_force = summed[atm_rows:].reshape(ocean_rows, SURF, cell_total)
    atm_padded = ghosts(padded_2(atm_state, (("comp", 1), ("tile", 2)), 2), 2)
    atm_stepped = relax(ghosts(relax(atm_padded, atm_rate), 1), atm_rate)
    ocean_padded = ghosts(padded_2(ocean_state, (("comp", 1), ("tile", 2)), 2), 2)
    ocean_stepped = relax(ghosts(relax(ocean_padded, ocean_rate), 1), ocean_rate)
    atm_next = atm_stepped.at[:SURF].add(jnp.transpose(atm_force, (1, 0, 2)))
    ocean_next = ocean_stepped.at[:SURF].add(
        jnp.transpose(ocean_force, (1, 0, 2)) * wet_rows[None, :, None]
    )
    return (atm_next, ocean_next)


def solution(mesh):
    return jax.shard_map(
        shards,
        mesh=mesh,
        in_specs=(
            P(None, "comp", "tile"),
            P(None, "comp", "tile"),
            P(),
            P(),
            P("comp", "tile"),
            P("comp", "tile", None, None),
            P("comp", "tile"),
            P("comp", "tile"),
            P("comp", "tile"),
        ),
        out_specs=(P(None, "comp", "tile"), P(None, "comp", "tile")),
        check_vma=False,
    )
```

profile of v0, /device:TPU:0, one launch (start us, length us, event | category | flops | bytes accessed | tf_op | source)
XLA Modules:
  0.0 102.0 jit_solution(3758282511293976926)
XLA Ops:
  7.2 0.0 copy-start
  7.2 0.0 reduce-scatter.2.cloned.1.call-start
  7.3 2.0 %copy.67 = f32[128,16,128]{0,1,2:T(8,128)S(1)} copy(f32[128,16,128]{2,1,0:T(8,128)} %param.15) | data formatting | bytes 2097152 | tf_op args[0]
  9.2 0.8 fusion.48
  10.1 0.5 collective-permute-start
  10.6 2.9 %collective-permute-start.1 = (f32[128,2,128]{0,1,2:T(2,128)}, f32[128,2,128]{0,1,2:T(2,128)}, u32[]{:S(2)}, u32[]{:S(2)}) collective-permute-start(f32[128,2,128]{0,1,2:T(2,128)} %get-tuple-element.38), channel_id=1, source_target_pairs={{4,0},{8,4},{12,8},{16,12},{20,16},{24,20},{28,24},{0,28},{5,1},{9... | collective-permute-start | bytes 393224 | tf_op jit(solution)/shard_map/ppermute | solution.py:18
  13.4 0.8 slice.198
  15.0 14.4 %all_gather.6 = bf16[8,64,128]{2,0,1:T(8,128)(2,1)S(1)} all-gather(bf16[8,16,128]{2,0,1:T(8,128)(2,1)S(1)} %copy.100), channel_id=1, replica_groups=mesh['comp'=8,'tile'=4] {'tile'}, dimensions={1}, use_global_device_ids=true | all-gather | bytes 163840 | tf_op jit(solution)/shard_map/all_gather | solution.py:60
  29.4 0.6 fusion.43
  29.9 0.1 copy.74
  30.1 0.0 copy-start.2
  30.1 0.7 copy-done.2
  30.8 0.1 fusion.36
  30.9 14.3 %all_gather.7 = bf16[8,64,128]{2,0,1:T(8,128)(2,1)} all-gather(bf16[8,16,128]{2,0,1:T(8,128)(2,1)S(1)} %fusion.36), channel_id=1, replica_groups=mesh['comp'=8,'tile'=4] {'tile'}, dimensions={1}, use_global_device_ids=true | all-gather | bytes 163840 | tf_op jit(solution)/shard_map/all_gather | solution.py:61
  45.2 0.6 fusion.44
  45.8 0.6 gather_fusion
  46.4 0.6 fusion.8
  47.0 0.1 copy-done.5
  47.0 0.4 fusion.26
  47.4 2.1 %gather_fusion.1 = bf16[48,8,128]{2,1,0:T(8,128)(2,1)} fusion(bf16[8,64,128]{2,0,1:T(8,128)(2,1)} %all_gather.7, s32[1024]{0:T(1024)S(1)} %pad_clamp_fusion), kind=kCustom, calls=%fused_computation.1.clone | custom fusion | bytes 196800 | tf_op jit(solution)/shard_map/jit(_take)/gather | solution.py:80
  49.6 1.8 %fusion.11 = f32[48,8,128]{2,1,0:T(8,128)S(1)} fusion(bf16[1,48,128,128]{3,2,1,0:T(8,128)(2,1)S(1)} %copy-done, bf16[48,8,128]{2,1,0:T(8,128)(2,1)} %gather_fusion.1, f32[48]{0:T(128)S(1)} %compare_convert_fusion, pred[48]{0:T(512)(128)(4,1)S(1)} %compare_and_fusion), kind=kOutput, calls=%fused_computation.17 | convolution fusion | flops 12681216 | bytes 1868016 | tf_op jit(solution)/shard_map/fps,pts->pft/dot_general | solution.py:78
  51.4 1.9 %convolution_add_fusion = f32[128,1024]{1,0:T(8,128)} fusion(f32[128,1024]{1,0:T(8,128)S(1)} %fusion.26, f32[6,8,8,128]{3,2,1,0:T(8,128)S(1)} %bitcast.52, s32[48]{0:T(128)} %fusion.44), kind=kOutput, calls=%fused_computation.15 | convolution fusion | flops 75634688 | bytes 1245376 | tf_op jit(solution)/shard_map/dot_general | solution.py:103
  53.3 0.0 reduce-scatter.2.cloned.1.call-update
  53.3 1.4 %fusion.50 = (f32[48,2,128]{2,0,1:T(8,128)}, f32[48,2,128]{2,0,1:T(8,128)S(1)}) fusion(f32[48,16,128]{2,0,1:T(8,128)} %copy-done.2), kind=kLoop, calls=%fused_computation.98 | loop fusion | bytes 196608 | tf_op jit(solution)/shard_map/slice | solution.py:18
  54.8 0.0 collective-permute-start.4
  54.8 2.6 %collective-permute-start.5 = (f32[48,2,128]{2,0,1:T(8,128)}, f32[48,2,128]{2,0,1:T(8,128)}, u32[]{:S(2)}, u32[]{:S(2)}) collective-permute-start(f32[48,2,128]{2,0,1:T(8,128)} %get-tuple-element.41), channel_id=1, source_target_pairs={{4,0},{8,4},{12,8},{16,12},{20,16},{24,20},{28,24},{0,28},{5,1},{9... | collective-permute-start | bytes 147464 | tf_op jit(solution)/shard_map/ppermute | solution.py:18
  57.4 1.9 %collective-permute-done.4 = f32[48,2,128]{2,0,1:T(8,128)} collective-permute-done((f32[48,2,128]{2,0,1:T(8,128)S(1)}, f32[48,2,128]{2,0,1:T(8,128)}, u32[]{:S(2)}, u32[]{:S(2)}) %collective-permute-start.4) | collective-permute-done | bytes 49184 | tf_op jit(solution)/shard_map/ppermute | solution.py:15
  59.3 0.8 constant_dynamic-update-slice_fusion.2
  60.1 0.1 constant_dynamic-update-slice_fusion.1
  60.2 0.0 collective-permute-done.5
  60.2 0.8 constant_dynamic-update-slice_fusion
  61.0 1.1 %fusion.49 = (f32[48,20,2]{2,0,1:T(8,128)}, f32[48,20,2]{2,0,1:T(8,128)}) fusion(f32[48,20,128]{2,0,1:T(8,128)S(1)} %constant_dynamic-update-slice_fusion), kind=kLoop, calls=%fused_computation.97 | loop fusion | bytes 30720 | tf_op jit(solution)/shard_map/slice | solution.py:16
  62.1 1.3 %copy.79 = f32[48,20,2]{0,1,2:T(8,128)S(1)} copy(f32[48,20,2]{2,0,1:T(8,128)} %get-tuple-element.39) | data formatting | bytes 15360 | tf_op jit(solution)/shard_map/slice | solution.py:16
  63.3 1.5 %collective-permute-start.6 = (f32[48,20,2]{0,1,2:T(8,128)S(1)}, f32[48,20,2]{0,1,2:T(8,128)S(1)}, u32[]{:S(2)}, u32[]{:S(2)}) collective-permute-start(f32[48,20,2]{0,1,2:T(8,128)S(1)} %copy.79), channel_id=1, source_target_pairs={{0,1},{1,2},{2,3},{3,0},{4,5},{5,6},{6,7},{7,4},{8,9},{9,10},{10,1... | collective-permute-start | bytes 23048 | tf_op jit(solution)/shard_map/ppermute | solution.py:15
  64.9 1.3 %copy.80 = f32[48,20,2]{0,1,2:T(8,128)S(1)} copy(f32[48,20,2]{2,0,1:T(8,128)} %get-tuple-element.40) | data formatting | bytes 15360 | tf_op jit(solution)/shard_map/slice | solution.py:18
  66.1 2.4 %collective-permute-start.7 = (f32[48,20,2]{0,1,2:T(8,128)S(1)}, f32[48,20,2]{0,1,2:T(8,128)S(1)}, u32[]{:S(2)}, u32[]{:S(2)}) collective-permute-start(f32[48,20,2]{0,1,2:T(8,128)S(1)} %copy.80), channel_id=1, source_target_pairs={{1,0},{2,1},{3,2},{0,3},{5,4},{6,5},{7,6},{4,7},{9,8},{10,9},{11,1... | collective-permute-start | bytes 23048 | tf_op jit(solution)/shard_map/ppermute | solution.py:18
  68.5 0.8 collective-permute-done.6
  69.4 1.0 %copy.81 = f32[48,20,2]{2,0,1:T(8,128)} copy(f32[48,20,2]{0,1,2:T(8,128)S(1)} %collective-permute-done.6) | data formatting | bytes 15360 | tf_op jit(solution)/shard_map/ppermute | solution.py:15
  70.4 0.1 collective-permute-done.7
  70.5 1.0 %copy.82 = f32[48,20,2]{2,0,1:T(8,128)} copy(f32[48,20,2]{0,1,2:T(8,128)S(1)} %collective-permute-done.7) | data formatting | bytes 15360 | tf_op jit(solution)/shard_map/ppermute | solution.py:18
  71.5 1.6 %maximum_multiply_fusion.1 = f32[48,20,132]{2,0,1:T(8,128)S(1)} fusion(f32[48,20,2]{2,0,1:T(8,128)} %copy.82, f32[48,20,128]{2,0,1:T(8,128)S(1)} %constant_dynamic-update-slice_fusion, f32[48,20,2]{2,0,1:T(8,128)} %copy.81, f32[20]{0:T(128)S(1)} %not_convert_fusion.1), kind=kLoop, calls=%fused_computation.25 | loop fusion | flops 380160 | bytes 1013840 | tf_op jit(solution)/shard_map/mul | solution.py:38
  73.1 1.0 fusion.20
  74.1 0.0 collective-permute-done
  74.2 0.0 collective-permute-done.1
  74.2 1.2 %pad_maximum_fusion = f32[128,20,128]{0,1,2:T(8,128)S(1)} fusion(f32[128,2,128]{0,1,2:T(2,128)} %collective-permute-done.1, f32[128,16,128]{0,1,2:T(8,128)S(1)} %copy.67, f32[128,2,128]{0,1,2:T(2,128)} %collective-permute-done), kind=kLoop, calls=%fused_computation.2 | loop fusion | flops 655360 | bytes 2621440 | tf_op jit(solution)/shard_map/concatenate | solution.py:19
  75.4 1.3 %collective-permute-start.2 = (f32[128,20,2]{0,1,2:T(8,128)S(1)}, f32[128,20,2]{0,1,2:T(8,128)S(1)}, u32[]{:S(2)}, u32[]{:S(2)}) collective-permute-start(f32[128,20,2]{0,1,2:T(8,128)S(1)} %get-tuple-element.35), channel_id=1, source_target_pairs={{0,1},{1,2},{2,3},{3,0},{4,5},{5,6},{6,7},{7,4},{8,9},{9,10},{10,1... | collective-permute-start | bytes 61448 | tf_op jit(solution)/shard_map/ppermute | solution.py:15
  76.7 3.1 %collective-permute-start.3 = (f32[128,20,2]{0,1,2:T(8,128)S(1)}, f32[128,20,2]{0,1,2:T(8,128)S(1)}, u32[]{:S(2)}, u32[]{:S(2)}) collective-permute-start(f32[128,20,2]{0,1,2:T(8,128)S(1)} %get-tuple-element.36), channel_id=1, source_target_pairs={{1,0},{2,1},{3,2},{0,3},{5,4},{6,5},{7,6},{4,7},{9,8},{10,9},{11,1... | collective-permute-start | bytes 61448 | tf_op jit(solution)/shard_map/ppermute | solution.py:18
  79.8 0.5 fusion.23
  80.3 0.3 copy.71
  80.5 1.0 collective-permute-done.2
  81.6 0.0 copy-start.4
  81.6 0.0 collective-permute-done.3
  81.6 0.2 maximum_multiply_fusion
  81.8 0.4 copy-done.4
  82.2 0.5 fusion.7
  82.7 0.4 fusion.16
  83.1 0.0 reduce-scatter.2.cloned.1.call-done
  83.1 0.9 slice_bitcast_fusion
  84.0 1.3 %copy.75 = f32[16,8,128]{1,2,0:T(8,128)} copy(f32[16,8,128]{2,1,0:T(8,128)S(1)} %bitcast.54) | data formatting | bytes 131072 | tf_op jit(solution)/shard_map/reshape | solution.py:110
  85.4 2.3 %slice_add_fusion.3 = f32[8,16,128]{0,2,1:T(8,128)} fusion(f32[128,16,128]{0,2,1:T(8,128)S(1)} %fusion.16, f32[16,8,128]{1,2,0:T(8,128)} %copy.75), kind=kLoop, calls=%fused_computation.18 | loop fusion | flops 16384 | bytes 196608 | tf_op jit(solution)/shard_map/add | solution.py:116
  87.7 5.1 %scatter-add.6 = f32[128,16,128]{0,2,1:T(8,128)S(1)} dynamic-update-slice(f32[128,16,128]{0,2,1:T(8,128)S(1)} %fusion.16, f32[8,16,128]{0,2,1:T(8,128)} %slice_add_fusion.3, s32[]{:T(128)} %constant.113.clone.1, s32[]{:T(128)} %constant.113.clone.1, s32[]{:T(128)} %constant.113.clone.1) | dynamic-update-slice | bytes 131076 | tf_op jit(solution)/shard_map/scatter-add | solution.py:116
  92.8 1.4 %copy.83 = f32[128,16,128]{2,1,0:T(8,128)} copy(f32[128,16,128]{0,2,1:T(8,128)S(1)} %scatter-add.6) | data formatting | bytes 2097152
  94.2 0.1 fusion.35
  94.3 0.9 copy.84
  (28 shorter events, 0.1 us)
Async XLA Ops:
  7.2 39.2 %copy-start = (bf16[1,48,128,128]{3,2,1,0:T(8,128)(2,1)S(1)}, bf16[1,48,128,128]{3,2,1,0:T(8,128)(2,1)}, u32[]{:S(2)}) copy-start(bf16[1,48,128,128]{3,2,1,0:T(8,128)(2,1)} %param.20) | copy-start | bytes 4718596
  7.2 7.1 %copy-start.8 = (s32[1,48]{1,0:T(1,128)S(1)}, s32[1,48]{1,0:T(1,128)}, u32[]{:S(2)}) copy-start(s32[1,48]{1,0:T(1,128)} %param.21) | copy-start | bytes 580
  7.2 7.1 %copy-start.6 = (s32[1,48]{1,0:T(1,128)S(1)}, s32[1,48]{1,0:T(1,128)}, u32[]{:S(2)}) copy-start(s32[1,48]{1,0:T(1,128)} %param.22) | copy-start | bytes 580
  7.2 22.7 %copy-start.1 = (f32[48,16,128]{2,1,0:T(8,128)S(1)}, f32[48,16,128]{2,1,0:T(8,128)}, u32[]{:S(2)}) copy-start(f32[48,16,128]{2,1,0:T(8,128)} %param.16) | copy-start | bytes 1179652
  7.2 22.9 %copy-start.7 = (s32[16,1]{0,1:T(1,128)S(1)}, s32[16,1]{0,1:T(1,128)}, u32[]{:S(2)}) copy-start(s32[16,1]{0,1:T(1,128)} %param.19) | copy-start | bytes 196
  7.2 75.9 %reduce-scatter.2.cloned.1.call-start = ((), (), s32[]{:S(2)}) async-start(), calls=%async_computation.1 | async-start | bytes 655360 | tf_op jit(solution)/shard_map/reduce_scatter | solution.py:96
  10.1 64.1 %collective-permute-start = (f32[128,2,128]{0,1,2:T(2,128)}, f32[128,2,128]{0,1,2:T(2,128)}, u32[]{:S(2)}, u32[]{:S(2)}) collective-permute-start(f32[128,2,128]{0,1,2:T(2,128)} %get-tuple-element.37), channel_id=1, source_target_pairs={{0,4},{4,8},{8,12},{12,16},{16,20},{20,24},{24,28},{28,0},{1,5},{5... | collective-permute-start | bytes 393224 | tf_op jit(solution)/shard_map/ppermute | solution.py:15
  10.6 63.6 %collective-permute-start.1 = (f32[128,2,128]{0,1,2:T(2,128)}, f32[128,2,128]{0,1,2:T(2,128)}, u32[]{:S(2)}, u32[]{:S(2)}) collective-permute-start(f32[128,2,128]{0,1,2:T(2,128)} %get-tuple-element.38), channel_id=1, source_target_pairs={{4,0},{8,4},{12,8},{16,12},{20,16},{24,20},{28,24},{0,28},{5,1},{9... | collective-permute-start | bytes 393224 | tf_op jit(solution)/shard_map/ppermute | solution.py:18
  30.1 0.7 copy-start.2
  46.4 0.6 copy-start.5
  54.8 4.5 %collective-permute-start.4 = (f32[48,2,128]{2,0,1:T(8,128)S(1)}, f32[48,2,128]{2,0,1:T(8,128)}, u32[]{:S(2)}, u32[]{:S(2)}) collective-permute-start(f32[48,2,128]{2,0,1:T(8,128)S(1)} %get-tuple-element.42), channel_id=1, source_target_pairs={{0,4},{4,8},{8,12},{12,16},{16,20},{20,24},{24,28},{28,0},{1,5},{5... | collective-permute-start | bytes 147464 | tf_op jit(solution)/shard_map/ppermute | solution.py:15
  54.8 5.4 %collective-permute-start.5 = (f32[48,2,128]{2,0,1:T(8,128)}, f32[48,2,128]{2,0,1:T(8,128)}, u32[]{:S(2)}, u32[]{:S(2)}) collective-permute-start(f32[48,2,128]{2,0,1:T(8,128)} %get-tuple-element.41), channel_id=1, source_target_pairs={{4,0},{8,4},{12,8},{16,12},{20,16},{24,20},{28,24},{0,28},{5,1},{9... | collective-permute-start | bytes 147464 | tf_op jit(solution)/shard_map/ppermute | solution.py:18
  63.3 6.0 %collective-permute-start.6 = (f32[48,20,2]{0,1,2:T(8,128)S(1)}, f32[48,20,2]{0,1,2:T(8,128)S(1)}, u32[]{:S(2)}, u32[]{:S(2)}) collective-permute-start(f32[48,20,2]{0,1,2:T(8,128)S(1)} %copy.79), channel_id=1, source_target_pairs={{0,1},{1,2},{2,3},{3,0},{4,5},{5,6},{6,7},{7,4},{8,9},{9,10},{10,1... | collective-permute-start | bytes 23048 | tf_op jit(solution)/shard_map/ppermute | solution.py:15
  66.1 4.3 %collective-permute-start.7 = (f32[48,20,2]{0,1,2:T(8,128)S(1)}, f32[48,20,2]{0,1,2:T(8,128)S(1)}, u32[]{:S(2)}, u32[]{:S(2)}) collective-permute-start(f32[48,20,2]{0,1,2:T(8,128)S(1)} %copy.80), channel_id=1, source_target_pairs={{1,0},{2,1},{3,2},{0,3},{5,4},{6,5},{7,6},{4,7},{9,8},{10,9},{11,1... | collective-permute-start | bytes 23048 | tf_op jit(solution)/shard_map/ppermute | solution.py:18
  70.4 2.7 %copy-start.3 = (f32[48]{0:T(128)S(1)}, f32[48]{0:T(128)}, u32[]{:S(2)}) copy-start(f32[48]{0:T(128)} %param.18) | copy-start | bytes 580
  75.4 6.1 %collective-permute-start.2 = (f32[128,20,2]{0,1,2:T(8,128)S(1)}, f32[128,20,2]{0,1,2:T(8,128)S(1)}, u32[]{:S(2)}, u32[]{:S(2)}) collective-permute-start(f32[128,20,2]{0,1,2:T(8,128)S(1)} %get-tuple-element.35), channel_id=1, source_target_pairs={{0,1},{1,2},{2,3},{3,0},{4,5},{5,6},{6,7},{7,4},{8,9},{9,10},{10,1... | collective-permute-start | bytes 61448 | tf_op jit(solution)/shard_map/ppermute | solution.py:15
  76.7 4.9 %collective-permute-start.3 = (f32[128,20,2]{0,1,2:T(8,128)S(1)}, f32[128,20,2]{0,1,2:T(8,128)S(1)}, u32[]{:S(2)}, u32[]{:S(2)}) collective-permute-start(f32[128,20,2]{0,1,2:T(8,128)S(1)} %get-tuple-element.36), channel_id=1, source_target_pairs={{1,0},{2,1},{3,2},{0,3},{5,4},{6,5},{7,6},{4,7},{9,8},{10,9},{11,1... | collective-permute-start | bytes 61448 | tf_op jit(solution)/shard_map/ppermute | solution.py:18
  81.6 0.7 copy-start.4
Sparse Core Ops, SparseCore 0:
  53.4 22.3 reduce-scatter.1
where the time goes:
time: 103 us; the launch traced here: 102 us
  blocking collectives  28.6 us (28%)
  local copies, waits for them, and re-layouts  26.5 us (26%)
  between operations  15 us (15%)
  starting transfers between devices  14.4 us (14%)
  other arithmetic  9.11 us (9%)
  matrix products  4.66 us (5%)
  waiting for transfers between devices  3.77 us (4%)
    all_gather x1, blocking collectives, shards(): lax.all_gather(atm_source, 'tile', axis=1, tiled=True)  14.4 us
    all_gather x1, blocking collectives, shards(): lax.all_gather(ocean_source, 'tile', axis=1, tiled=True)  14.3 us
    ppermute x4, starting transfers between devices, padded_2(): lax.ppermute(lax.slice_in_dim(block, 0, width, axis=dim), axis, backward)  11 us
    unnamed x28, local copies, waits for them, and re-layouts  7.44 us
    scatter-add x1, local copies, waits for them, and re-layouts, shards(): atm_next = atm_stepped.at[:SURF].add(jnp.transpose(atm_force, (1, 0, 2)))  5.1 us
    ppermute x4, waiting for transfers between devices, padded_2(): lax.ppermute(lax.slice_in_dim(block, block.shape[dim] - width, None, axis...  3.67 us
    mul x4, other arithmetic, ghosts(): return padded * retain[None, :, None]  3.33 us
    ppermute x4, starting transfers between devices, padded_2(): lax.ppermute(lax.slice_in_dim(block, block.shape[dim] - width, None, axis...  3.33 us
  transfers between devices with their start and end apart: 9, of which 4 were waited for; matrix products, arithmetic and copies ran while one was open for 24% of the time, Pallas kernels for 0%

commit v1 on v0

v1 whole, which is shorter than its diff:
```python
import functools

import jax
import jax.numpy as jnp
from jax import lax
from jax.experimental import pallas as pl
from jax.experimental.pallas import tpu as pltpu
from jax.sharding import PartitionSpec as P

SURF = 8
F32 = jnp.float32
BF16 = jnp.bfloat16
VMEM = pl.BlockSpec(memory_space=pltpu.VMEM)
SMEM = pl.BlockSpec(memory_space=pltpu.SMEM)


def beside_even(index):
    return index + 1 - 2 * (index % 2)


def beside_odd(index, count):
    return (index - 1 + 2 * (index % 2) + count) % count


def tile_pairs(count):
    routes = [
        [(i, beside_even(i)) for i in range(count)],
        [(i, beside_odd(i, count)) for i in range(count)],
    ]
    routes += [[(i, (i + s) % count) for i in range(count)] for s in range(2, count - 1)]
    return routes


def peers(me, count):
    a = beside_even(me)
    b = beside_odd(me, count)
    far = range(2, count - 1)
    sources = [a, b] + [lax.rem(me - s + count, count) for s in far]
    targets = [a, b] + [lax.rem(me + s, count) for s in far]
    return sources, targets


def comp_pairs(count):
    even = [(i, beside_even(i)) for i in range(count)]
    odd = [(i, i + 1) for i in range(1, count - 1, 2)] + [(i + 1, i) for i in range(1, count - 1, 2)]
    return even, odd


def pack_surface(mask, atm, ocean, out):
    rows_a = atm.shape[1]
    rows_o = ocean.shape[1]
    for y in range(rows_a):
        out[y] = atm[:, y, :].astype(BF16)
    for y in range(rows_o):
        out[rows_a + y] = (ocean[:, y, :] * mask[y, 0].astype(F32)).astype(BF16)


def pack_rows(rows, atm, ocean, even_out, odd_out):
    parity = lax.rem(lax.axis_index("comp"), 2)
    at = 0
    for ref in (atm, ocean):
        channels = ref.shape[0] // rows
        for c in range(0, channels, 8):
            for r in range(2):
                low = ref[pl.ds(c * rows + r, 8, stride=rows), :]
                high = ref[pl.ds(c * rows + rows - 2 + r, 8, stride=rows), :]
                even_out[r, at + c : at + c + 8, :] = jnp.where(parity == 0, high, low).astype(BF16)
                odd_out[r, at + c : at + c + 8, :] = jnp.where(parity == 0, low, high).astype(BF16)
        at += channels


def halo_rows(parity, even_in, odd_in, at):
    e = [even_in[r, at : at + 8, :].astype(F32) for r in range(2)]
    o = [odd_in[r, at : at + 8, :].astype(F32) for r in range(2)]
    north = [jnp.where(parity == 0, o[r], e[r]) for r in range(2)]
    south = [jnp.where(parity == 0, e[r], o[r]) for r in range(2)]
    return north, south


def pack_columns(rows, atm, ocean, atm_rate, ocean_rate, even_in, odd_in, out_a, out_b, edge, inner, stage):
    parity = lax.rem(lax.axis_index("comp"), 2)
    tile_parity = lax.rem(lax.axis_index("tile"), 2)
    lanes = atm.shape[1]
    row = lax.broadcasted_iota(jnp.int32, (8, lanes), 0)
    lane = lax.broadcasted_iota(jnp.int32, (8, lanes), 1)
    east = lax.div(row, 2) == tile_parity
    outer_lane = jnp.where(east, lanes - 1, 0)
    inner_lane = jnp.where(east, lanes - 2, 1)
    first = lax.rem(row, 2) == 0
    live = row < 4
    pick_edge = jnp.where(live & first & (lane == outer_lane), 1.0, 0.0).astype(BF16)
    pick_inner = jnp.where(
        live & (lane == jnp.where(first, inner_lane, outer_lane)), 1.0, 0.0
    ).astype(BF16)
    dims = (((1,), (1,)), ((), ()))
    stage[...] = jnp.zeros_like(stage)
    at = 0
    for ref, rate in ((atm, atm_rate), (ocean, ocean_rate)):
        channels = ref.shape[0] // rows
        for c in range(0, channels, 8):
            rho = rate[c : c + 8, :]
            north, south = halo_rows(parity, even_in, odd_in, at + c)
            q = [north[1]]
            q += [ref[pl.ds(c * rows + r, 8, stride=rows), :] for r in range(rows)]
            q += [south[0]]
            for r in range(rows):
                mid = (1.0 - 4.0 * rho) * q[r + 1] + rho * (q[r] + q[r + 2])
                edge[pl.ds(r, 8, stride=rows), :] = 2.0 * rho * mid
                inner[pl.ds(r, 8, stride=rows), :] = rho * rho * q[r + 1]
            found = lax.dot_general(
                pick_edge, edge[...].astype(BF16), dims, preferred_element_type=F32
            ) + lax.dot_general(
                pick_inner, inner[...].astype(BF16), dims, preferred_element_type=F32
            )
            j = (at + c) // 8
            stage[0, 2 * j : 2 * j + 2, :] = found[0:2, :]
            stage[1, 2 * j : 2 * j + 2, :] = found[2:4, :]
        at += channels
    out_a[...] = stage[0].astype(BF16)
    out_b[...] = stage[1].astype(BF16)


def remap(tile_count, rows_a, rows_o, *refs):
    src, tgt, number, weights, own = refs[:5]
    got = refs[5 : 5 + tile_count - 1]
    own_out = refs[5 + tile_count - 1]
    outs = refs[6 + tile_count - 1 : 6 + 2 * (tile_count - 1)]
    band, total = refs[6 + 2 * (tile_count - 1) :]
    me = lax.axis_index("tile")
    block = rows_a + rows_o
    sources, targets = peers(me, tile_count)
    band[pl.ds(me * block, block)] = own[...]
    for e, ref in zip(sources, got):
        band[pl.ds(e * block, block)] = ref[...]
    total[...] = jnp.zeros_like(total)
    pairs = weights.shape[0]
    live_count = number[0, 0]
    trans = (((1,), (1,)), ((), ()))
    plain = (((1,), (0,)), ((), ()))
    group = 8
    for start in range(0, pairs, group):
        made = []
        for k in range(start, min(start + group, pairs)):
            a = src[0, k]
            o = tgt[0, k]
            at_a = lax.div(a, rows_a) * block + lax.rem(a, rows_a)
            at_o = lax.div(o, rows_o) * block + rows_a + lax.rem(o, rows_o)
            live = k < live_count
            w = weights[k]
            ta = band[at_a]
            to = band[at_o]
            ta = jnp.where(live, ta, jnp.zeros_like(ta))
            to = jnp.where(live, to, jnp.zeros_like(to))
            ahead = lax.dot_general(ta, w, plain, preferred_element_type=F32)
            back = lax.dot_general(to, w, trans, preferred_element_type=F32)
            made.append((at_a, at_o, ahead, back))
        for at_a, at_o, ahead, back in made:
            total[at_o] += ahead
            total[at_a] += back
    own_out[...] = total[pl.ds(me * block, block)]
    for e, ref in zip(targets, outs):
        ref[...] = total[pl.ds(e * block, block)].astype(BF16)


def stencil(rows, atm, ocean, atm_rate, ocean_rate, even_in, odd_in, atm_out, ocean_out):
    comp = lax.axis_index("comp")
    parity = lax.rem(comp, 2)
    lanes = atm.shape[1]
    lane = lax.broadcasted_iota(jnp.int32, (8, lanes), 1)
    at_west = lane == 0
    at_east = lane == lanes - 1
    keep_north = jnp.where(comp == 0, 0.0, 1.0).astype(F32)
    keep_south = jnp.where(comp == lax.axis_size("comp") - 1, 0.0, 1.0).astype(F32)
    at = 0
    for ref, rate, out in ((atm, atm_rate, atm_out), (ocean, ocean_rate, ocean_out)):
        channels = ref.shape[0] // rows
        for c in range(0, channels, 8):
            rho = jnp.broadcast_to(rate[c : c + 8, :], (8, lanes))
            own = 1.0 - 4.0 * rho
            north, south = halo_rows(parity, even_in, odd_in, at + c)
            q = north + [ref[pl.ds(c * rows + r, 8, stride=rows), :] for r in range(rows)] + south
            p = []
            for i in range(1, rows + 3):
                west = jnp.where(at_west, 0.0, pltpu.roll(q[i], 1, 1))
                east = jnp.where(at_east, 0.0, pltpu.roll(q[i], lanes - 1, 1))
                p.append(own * q[i] + rho * ((q[i - 1] + q[i + 1]) + (west + east)))
            p[0] = p[0] * keep_north
            p[rows + 1] = p[rows + 1] * keep_south
            for r in range(rows):
                ghost = rho * q[r + 2]
                west = jnp.where(at_west, ghost, pltpu.roll(p[r + 1], 1, 1))
                east = jnp.where(at_east, ghost, pltpu.roll(p[r + 1], lanes - 1, 1))
                out[pl.ds(c * rows + r, 8, stride=rows), :] = own * p[r + 1] + rho * (
                    (p[r] + p[r + 2]) + (west + east)
                )
        at += channels


def final(tile_count, rows_a, rows_o, message, *refs):
    mask, atm, ocean, own = refs[:4]
    got = refs[4 : 4 + tile_count - 1]
    atm_out, ocean_out, force = refs[4 + tile_count - 1 :]
    lanes = atm.shape[1]
    tile_parity = lax.rem(lax.axis_index("tile"), 2)
    row = lax.broadcasted_iota(jnp.int32, (8, lanes), 0)
    lane = lax.broadcasted_iota(jnp.int32, (8, lanes), 1)
    east = lax.div(row, 2) == tile_parity
    spot = jnp.where(
        lax.rem(row, 2) == 0,
        jnp.where(east, lanes - 1, 0),
        jnp.where(east, lanes - 2, 1),
    )
    place = jnp.where((row < 4) & (lane == spot), 1.0, 0.0).astype(BF16)
    block = rows_a + rows_o
    for y in range(block):
        total = own[y]
        for ref in got:
            total = total + ref[8 * y : 8 * y + 8, :].astype(F32)
        if y >= rows_a:
            total = total * mask[y - rows_a, 0].astype(F32)
        start = y if y < rows_a else SURF * rows_a + y - rows_a
        force[pl.ds(start, SURF, stride=rows_a if y < rows_a else rows_o), :] = total
    dims = (((0,), (0,)), ((), ()))
    at = 0
    for ref, out, rows, add in (
        (atm, atm_out, rows_a, 0),
        (ocean, ocean_out, rows_o, SURF * rows_a),
    ):
        for c in range(0, ref.shape[0] // rows, 8):
            j = message + 2 * ((at + c) // 8)
            sides = jnp.concatenate(
                [
                    got[0][j : j + 2, :].astype(F32),
                    got[1][j : j + 2, :].astype(F32),
                    jnp.zeros((4, lanes), F32),
                ],
                axis=0,
            ).astype(BF16)
            value = ref[c * rows : (c + 8) * rows, :] + lax.dot_general(
                sides, place, dims, preferred_element_type=F32
            )
            if c == 0:
                value = value + force[add : add + SURF * rows, :]
            out[c * rows : (c + 8) * rows, :] = value
        at += ref.shape[0] // rows


def params(limit=None):
    return pltpu.CompilerParams(vmem_limit_bytes=limit)


def shards(
    atm_state,
    ocean_state,
    atm_rate,
    ocean_rate,
    ocean_mask,
    remap_weight,
    pair_src,
    pair_tgt,
    pair_count,
):
    channels_a, rows_a, lanes = atm_state.shape
    channels_o, rows_o, _ = ocean_state.shape
    channels = channels_a + channels_o
    tile_count = lax.axis_size("tile")
    block = rows_a + rows_o
    message = block * SURF
    extra = -(-2 * channels // 8 // 16) * 16
    atm = atm_state.reshape(channels_a * rows_a, lanes)
    ocean = ocean_state.reshape(channels_o * rows_o, lanes)
    rate_a = atm_rate.reshape(channels_a, 1)
    rate_o = ocean_rate.reshape(channels_o, 1)
    routes = tile_pairs(tile_count)
    even_pairs, odd_pairs = comp_pairs(lax.axis_size("comp"))

    surface = pl.pallas_call(
        pack_surface,
        grid=(1,),
        in_specs=[
            SMEM,
            pl.BlockSpec((SURF, rows_a, lanes), lambda i: (0, 0, 0)),
            pl.BlockSpec((SURF, rows_o, lanes), lambda i: (0, 0, 0)),
        ],
        out_specs=pl.BlockSpec((block, SURF, lanes), lambda i: (0, 0, 0)),
        out_shape=jax.ShapeDtypeStruct((block, SURF, lanes), BF16),
        compiler_params=params(4 << 20),
    )(ocean_mask, atm_state, ocean_state)
    far_first = list(range(len(routes)))[::-1]
    received = {}
    for i in far_first:
        received[i] = lax.ppermute(surface, "tile", routes[i])

    halo = jax.ShapeDtypeStruct((2, channels, lanes), BF16)
    even_rows, odd_rows = pl.pallas_call(
        functools.partial(pack_rows, rows_a),
        in_specs=[VMEM, VMEM],
        out_specs=[VMEM, VMEM],
        out_shape=[halo, halo],
        compiler_params=params(8 << 20),
    )(atm, ocean)
    even_in = lax.ppermute(even_rows, "comp", even_pairs)
    odd_in = lax.ppermute(odd_rows, "comp", odd_pairs)

    part = jax.ShapeDtypeStruct((block, SURF, lanes), BF16)
    results = pl.pallas_call(
        functools.partial(remap, tile_count, rows_a, rows_o),
        in_specs=[SMEM, SMEM, SMEM] + [VMEM] * (1 + tile_count),
        out_specs=[VMEM] * tile_count,
        out_shape=[jax.ShapeDtypeStruct((block, SURF, lanes), F32)] + [part] * (tile_count - 1),
        scratch_shapes=[
            pltpu.VMEM((tile_count * block, SURF, lanes), BF16),
            pltpu.VMEM((tile_count * block, SURF, lanes), F32),
        ],
        compiler_params=params(12 << 20),
    )(
        pair_src,
        pair_tgt,
        pair_count,
        remap_weight[0],
        surface,
        *[received[i] for i in range(tile_count - 1)],
    )
    own_part, parts = results[0], [p.reshape(message, lanes) for p in results[1:]]

    col_a, col_b = pl.pallas_call(
        functools.partial(pack_columns, rows_a),
        in_specs=[VMEM] * 6,
        out_specs=[VMEM, VMEM],
        out_shape=[jax.ShapeDtypeStruct((extra, lanes), BF16)] * 2,
        scratch_shapes=[
            pltpu.VMEM((8 * rows_a, lanes), F32),
            pltpu.VMEM((8 * rows_a, lanes), F32),
            pltpu.VMEM((2, extra, lanes), F32),
        ],
        compiler_params=params(8 << 20),
    )(atm, ocean, rate_a, rate_o, even_in, odd_in)
    send = [
        jnp.concatenate([parts[0], col_a], axis=0),
        jnp.concatenate([parts[1], col_b], axis=0),
    ] + parts[2:]
    returned = {}
    for i in far_first:
        returned[i] = lax.ppermute(send[i], "tile", routes[i])

    atm_base, ocean_base = pl.pallas_call(
        functools.partial(stencil, rows_a),
        in_specs=[VMEM] * 6,
        out_specs=[VMEM, VMEM],
        out_shape=[
            jax.ShapeDtypeStruct(atm.shape, F32),
            jax.ShapeDtypeStruct(ocean.shape, F32),
        ],
        compiler_params=params(8 << 20),
    )(atm, ocean, rate_a, rate_o, even_in, odd_in)

    atm_next, ocean_next = pl.pallas_call(
        functools.partial(final, tile_count, rows_a, rows_o, message),
        in_specs=[SMEM] + [VMEM] * (2 + tile_count),
        out_specs=[VMEM, VMEM],
        out_shape=[
            jax.ShapeDtypeStruct(atm.shape, F32),
            jax.ShapeDtypeStruct(ocean.shape, F32),
        ],
        scratch_shapes=[pltpu.VMEM((SURF * block, lanes), F32)],
        compiler_params=params(12 << 20),
    )(ocean_mask, atm_base, ocean_base, own_part, *[returned[i] for i in range(tile_count - 1)])
    return (
        atm_next.reshape(channels_a, rows_a, lanes),
        ocean_next.reshape(channels_o, rows_o, lanes),
    )


def solution(mesh):
    return jax.shard_map(
        shards,
        mesh=mesh,
        in_specs=(
            P(None, "comp", "tile"),
            P(None, "comp", "tile"),
            P(),
            P(),
            P("comp", "tile"),
            P("comp", "tile", None, None),
            P("comp", "tile"),
            P("comp", "tile"),
            P("comp", "tile"),
        ),
        out_specs=(P(None, "comp", "tile"), P(None, "comp", "tile")),
        check_vma=False,
    )
```

time: 103 us -> 35.3 us (0.34)
  blocking collectives: 28.6 us -> 0 us
  local copies, waits for them, and re-layouts: 26.5 us -> 5.13 us
  between operations: 15 us -> 1.38 us
  Pallas kernels: 0 us -> 10.4 us
  other arithmetic: 9.11 us -> 0.03 us
  matrix products: 4.66 us -> 0 us
  starting transfers between devices: 14.4 us -> 11 us
  waiting for transfers between devices: 3.77 us -> 6.9 us
    all_gather x2 -> x0, blocking collectives: 28.6 us -> none  [the longest x1 14.4 us: shards(): lax.all_gather(atm_source, 'tile', axis=1, tiled=True)]
    pallas_call x0 -> x6, Pallas kernels: none -> 10.4 us  [the longest x1 2.51 us: shards(): pl.pallas_call(functools.partial(stencil, rows_a), in_specs=[VMEM] * 6, o...]
    slice x7 -> x0, local copies, waits for them, and re-layouts: 6.7 us -> none  [the longest x4 3.16 us: padded_2(): lax.slice_in_dim(block, block.shape[dim] - width, None, axis=dim)]
    scatter-add x1 -> x0, local copies, waits for them, and re-layouts: 5.1 us -> none  [shards(): atm_next = atm_stepped.at[:SURF].add(jnp.transpose(atm_force, (1, 0, 2)))]
    dot_general x4 -> x0, matrix products: 4.66 us -> none  [the longest x1 1.88 us: shards(): jnp.dot(back_hot, back_flat, precision=lax.Precision.HIGHEST, preferred_e...]
    ppermute x8, starting transfers between devices: 14.3 us -> 11 us  [the longest x3 5.35 us: shards(): received[i] = lax.ppermute(surface, 'tile', routes[i])]
    mul x4 -> x0, other arithmetic: 3.33 us -> none  [ghosts(): return padded * retain[None, :, None]]
    add x3 -> x0, other arithmetic: 3.19 us -> none  [the longest x1 2.33 us: shards(): atm_next = atm_stepped.at[:SURF].add(jnp.transpose(atm_force, (1, 0, 2)))]
  transfers between devices with their start and end apart: 9 -> 8, of which waited for: 4 -> 2; matrix products, arithmetic and copies ran while one was open for 24% -> 5% of each run, Pallas kernels for 0% -> 15%
where the time goes in v1:
time: 35.3 us; the launch traced here: 34.8 us
  starting transfers between devices  11 us (31%)
  Pallas kernels  10.4 us (29%)
  waiting for transfers between devices  6.9 us (20%)
  local copies, waits for them, and re-layouts  5.13 us (15%)
  between operations  1.38 us (4%)
    ppermute x3, starting transfers between devices, shards(): received[i] = lax.ppermute(surface, 'tile', routes[i])  5.35 us
    ppermute x3, starting transfers between devices, shards(): returned[i] = lax.ppermute(send[i], 'tile', routes[i])  4.45 us
    unnamed x17, local copies, waits for them, and re-layouts  4.28 us
    ppermute x3, waiting for transfers between devices, shards(): returned[i] = lax.ppermute(send[i], 'tile', routes[i])  3.67 us
    ppermute x3, waiting for transfers between devices, shards(): received[i] = lax.ppermute(surface, 'tile', routes[i])  3.23 us
    pallas_call x1, Pallas kernels, shards(): pl.pallas_call(functools.partial(stencil, rows_a), in_specs=[VMEM] * 6, o...  2.51 us
    pallas_call x1, Pallas kernels, shards(): pl.pallas_call(functools.partial(pack_columns, rows_a), in_specs=[VMEM] *...  2.16 us
    pallas_call x1, Pallas kernels, shards(): pl.pallas_call(functools.partial(final, tile_count, rows_a, rows_o, messa...  2.1 us
  transfers between devices with their start and end apart: 8, of which 2 were waited for; matrix products, arithmetic and copies ran while one was open for 5% of the time, Pallas kernels for 15%

profile of v1, /device:TPU:0, one launch (start us, length us, event | category | flops | bytes accessed | tf_op | source)
XLA Modules:
  0.0 34.8 jit_solution(5717294809408319397)
XLA Ops:
  0.6 0.0 copy-start.7
  0.6 0.0 copy-start
  0.7 1.2 %copy-done = f32[128,16,128]{2,1,0:T(8,128)S(1)} copy-done((f32[128,16,128]{2,1,0:T(8,128)S(1)}, f32[128,16,128]{2,1,0:T(8,128)}, u32[]{:S(2)}) %copy-start) | copy-done | bytes 1048600
  1.9 0.0 copy-start.2
  1.9 1.0 %copy-done.2 = f32[48,16,128]{2,1,0:T(8,128)S(1)} copy-done((f32[48,16,128]{2,1,0:T(8,128)S(1)}, f32[48,16,128]{2,1,0:T(8,128)}, u32[]{:S(2)}) %copy-start.2) | copy-done | bytes 393240
  2.9 0.0 copy-start.1
  2.9 0.0 copy-start.3
  2.9 0.0 copy-start.4
  2.9 0.8 %shard_map.104 = (bf16[2,176,128]{2,1,0:T(8,128)(2,1)}, bf16[2,176,128]{2,1,0:T(8,128)(2,1)}) custom-call(f32[2048,128]{1,0:T(8,128)S(1)} %bitcast.10, f32[768,128]{1,0:T(8,128)S(1)} %bitcast.13), custom_call_target="tpu_custom_call" | custom-call | tf_op jit(solution)/shard_map/pallas_call | solution.py:295
  3.7 0.5 %collective-permute-start = (bf16[2,176,128]{2,1,0:T(8,128)(2,1)}, bf16[2,176,128]{2,1,0:T(8,128)(2,1)S(1)}, u32[]{:S(2)}, u32[]{:S(2)}) collective-permute-start(bf16[2,176,128]{2,1,0:T(8,128)(2,1)} %get-tuple-element.14), channel_id=1, source_target_pairs={{0,4},{4,0},{8,12},{12,8},{16,20},{20,16},{24,28},{28,24},{1,5},{5... | collective-permute-start | bytes 270344 | tf_op jit(solution)/shard_map/ppermute | solution.py:302
  4.2 0.7 %collective-permute-start.1 = (bf16[2,176,128]{2,1,0:T(8,128)(2,1)}, bf16[2,176,128]{2,1,0:T(8,128)(2,1)S(1)}, u32[]{:S(2)}, u32[]{:S(2)}) collective-permute-start(bf16[2,176,128]{2,1,0:T(8,128)(2,1)} %get-tuple-element.15), channel_id=1, source_target_pairs={{4,8},{12,16},{20,24},{8,4},{16,12},{24,20},{5,9},{13,17},{21,25},... | collective-permute-start | bytes 270344 | tf_op jit(solution)/shard_map/ppermute | solution.py:303
  4.8 0.7 %copy.16.mask.refs_0_ = s32[16,1]{1,0:T(8,128)S(1)} copy(s32[16,1]{0,1:T(1,128)} %param.13) | data formatting | bytes 128 | tf_op args[4]
  5.6 0.0 copy-done.1
  5.6 0.0 copy-done.3
  5.6 0.8 %shard_map.106.refs_4_ = bf16[32,8,128]{2,1,0:T(8,128)(2,1)S(1)} custom-call(s32[16,1]{1,0:T(8,128)S(1)} %copy.16.mask.refs_0_, f32[128,16,128]{2,1,0:T(8,128)S(1)} %copy-done.1, f32[48,16,128]{2,1,0:T(8,128)S(1)} %copy-done.3), custom_call_target="tpu_custom_call" | custom-call | tf_op jit(solution)/shard_map/pallas_call | solution.py:277
  6.4 3.8 %collective-permute-start.4 = (bf16[32,8,128]{2,1,0:T(8,128)(2,1)S(1)}, bf16[32,8,128]{2,1,0:T(8,128)(2,1)S(1)}, u32[]{:S(2)}, u32[]{:S(2)}) collective-permute-start(bf16[32,8,128]{2,1,0:T(8,128)(2,1)S(1)} %shard_map.106.refs_4_), channel_id=1, source_target_pairs={{0,2},{1,3},{2,0},{3,1},{4,6},{5,7},{6,4},{7,5},{8,10},{9,11},{10,... | collective-permute-start | bytes 196616 | tf_op jit(solution)/shard_map/ppermute | solution.py:292
  10.2 1.3 %collective-permute-start.3 = (bf16[32,8,128]{2,1,0:T(8,128)(2,1)S(1)}, bf16[32,8,128]{2,1,0:T(8,128)(2,1)S(1)}, u32[]{:S(2)}, u32[]{:S(2)}) collective-permute-start(bf16[32,8,128]{2,1,0:T(8,128)(2,1)S(1)} %shard_map.106.refs_4_), channel_id=1, source_target_pairs={{0,3},{1,2},{2,1},{3,0},{4,7},{5,6},{6,5},{7,4},{8,11},{9,10},{10,... | collective-permute-start | bytes 196616 | tf_op jit(solution)/shard_map/ppermute | solution.py:292
  11.5 0.2 collective-permute-start.2
  12.4 0.0 copy-done.7
  12.4 0.1 copy.12.ocean_rate
  12.5 0.8 %copy.11.atm_rate = f32[128,1]{1,0:T(8,128)S(1)} copy(f32[128,1]{0,1:T(1,128)} %bitcast.20) | data formatting | bytes 1024 | tf_op jit(solution)/shard_map/reshape | solution.py:272
  13.3 0.0 collective-permute-done.4.refs_7_
  13.3 3.2 %collective-permute-done.3.refs_6_ = bf16[32,8,128]{2,1,0:T(8,128)(2,1)S(1)} collective-permute-done((bf16[32,8,128]{2,1,0:T(8,128)(2,1)S(1)}, bf16[32,8,128]{2,1,0:T(8,128)(2,1)S(1)}, u32[]{:S(2)}, u32[]{:S(2)}) %collective-permute-start.3) | collective-permute-done | bytes 65568 | tf_op jit(solution)/shard_map/ppermute | solution.py:292
  16.5 0.0 collective-permute-done.2.refs_5_
  16.5 0.0 copy-done.4
  16.5 0.0 copy-start.5
  16.5 0.7 %copy-done.5 = s32[1,48]{1,0:T(1,128)S(1)} copy-done((s32[1,48]{1,0:T(1,128)S(1)}, s32[1,48]{1,0:T(1,128)}, u32[]{:S(2)}) %copy-start.5) | copy-done | bytes 216
  17.1 0.0 copy-start.6
  17.2 0.7 %copy-done.6 = s32[1,48]{1,0:T(1,128)S(1)} copy-done((s32[1,48]{1,0:T(1,128)S(1)}, s32[1,48]{1,0:T(1,128)}, u32[]{:S(2)}) %copy-start.6) | copy-done | bytes 216
  17.8 2.0 %shard_map.107 = (f32[32,8,128]{2,1,0:T(8,128)S(1)}, bf16[32,8,128]{2,1,0:T(8,128)(2,1)S(1)}, bf16[32,8,128]{2,1,0:T(8,128)(2,1)S(1)}, bf16[32,8,128]{2,1,0:T(8,128)(2,1)S(1)}) custom-call(s32[1,48]{1,0:T(1,128)S(1)} %copy-done.5, s32[1,48]{1,0:T(1,128)S(1)} %copy-done.6, s32[1,1]{1,0:T(1,128)S(6)} %copy.17.refs_2_, bf16[48,128,128]{2,1,0:T(8,128)(2,1)S(1)} %bitcast.16, ...), custom_call_target="tpu_custom_call" | custom-call | tf_op jit(solution)/shard_map/pallas_call | solution.py:306
  19.8 0.0 collective-permute-done.even_in
  19.8 0.0 collective-permute-done.1.odd_in
  19.8 2.2 %shard_map.108 = (bf16[48,128]{1,0:T(8,128)(2,1)S(1)}, bf16[48,128]{1,0:T(8,128)(2,1)S(1)}) custom-call(f32[2048,128]{1,0:T(8,128)S(1)} %bitcast.11, f32[768,128]{1,0:T(8,128)S(1)} %bitcast.14, f32[128,1]{1,0:T(8,128)S(1)} %copy.11.atm_rate, f32[48,1]{1,0:T(8,128)S(1)} %copy.12.ocean_rate, bf16[2,176,128]{2,1,0:T(8,128)(2,1)S(1)} %collective-permute-done.even_in, ...), custom_call_target="tpu_custom_call" | custom-call | tf_op jit(solution)/shard_map/pallas_call | solution.py:326
  22.0 2.1 %collective-permute-start.6 = (bf16[304,128]{1,0:T(8,128)(2,1)S(1)}, bf16[304,128]{1,0:T(8,128)(2,1)S(1)}, u32[]{:S(2)}, u32[]{:S(2)}) collective-permute-start(bf16[304,128]{1,0:T(8,128)(2,1)S(1)} %pad_maximum_fusion.1), channel_id=1, source_target_pairs={{0,3},{1,2},{2,1},{3,0},{4,7},{5,6},{6,5},{7,4},{8,11},{9,10},{10,... | collective-permute-start | bytes 233480 | tf_op jit(solution)/shard_map/ppermute | solution.py:344
  24.2 1.5 %collective-permute-start.5 = (bf16[304,128]{1,0:T(8,128)(2,1)S(1)}, bf16[304,128]{1,0:T(8,128)(2,1)S(1)}, u32[]{:S(2)}, u32[]{:S(2)}) collective-permute-start(bf16[304,128]{1,0:T(8,128)(2,1)S(1)} %pad_maximum_fusion), channel_id=1, source_target_pairs={{0,1},{1,0},{2,3},{3,2},{4,5},{5,4},{6,7},{7,6},{8,9},{9,8},{10,11... | collective-permute-start | bytes 233480 | tf_op jit(solution)/shard_map/ppermute | solution.py:344
  25.7 0.8 %collective-permute-start.7 = (bf16[256,128]{1,0:T(8,128)(2,1)S(1)}, bf16[256,128]{1,0:T(8,128)(2,1)S(1)}, u32[]{:S(2)}, u32[]{:S(2)}) collective-permute-start(bf16[256,128]{1,0:T(8,128)(2,1)S(1)} %bitcast.19), channel_id=1, source_target_pairs={{0,2},{1,3},{2,0},{3,1},{4,6},{5,7},{6,4},{7,5},{8,10},{9,11},{10,... | collective-permute-start | bytes 196616 | tf_op jit(solution)/shard_map/ppermute | solution.py:344
  26.5 2.5 %shard_map.105 = (f32[2048,128]{1,0:T(8,128)S(1)}, f32[768,128]{1,0:T(8,128)S(1)}) custom-call(f32[2048,128]{1,0:T(8,128)S(1)} %bitcast.12, f32[768,128]{1,0:T(8,128)S(1)} %bitcast.15, f32[128,1]{1,0:T(8,128)S(1)} %copy.11.atm_rate, f32[48,1]{1,0:T(8,128)S(1)} %copy.12.ocean_rate, bf16[2,176,128]{2,1,0:T(8,128)(2,1)S(1)} %collective-permute-done.even_in, ...), custom_call_target="tpu_custom_call" | custom-call | tf_op jit(solution)/shard_map/pallas_call | solution.py:346
  29.0 3.7 %collective-permute-done.7.refs_6_ = bf16[256,128]{1,0:T(8,128)(2,1)S(1)} collective-permute-done((bf16[256,128]{1,0:T(8,128)(2,1)S(1)}, bf16[256,128]{1,0:T(8,128)(2,1)S(1)}, u32[]{:S(2)}, u32[]{:S(2)}) %collective-permute-start.7) | collective-permute-done | bytes 65568 | tf_op jit(solution)/shard_map/ppermute | solution.py:344
  32.7 0.0 collective-permute-done.6.refs_5_
  32.7 0.0 collective-permute-done.5.refs_4_
  32.7 2.1 %shard_map.109 = (f32[2048,128]{1,0:T(8,128)}, f32[768,128]{1,0:T(8,128)}) custom-call(s32[16,1]{1,0:T(8,128)S(1)} %copy.16.mask.refs_0_, f32[2048,128]{1,0:T(8,128)S(1)} %get-tuple-element.16.refs_1_, f32[768,128]{1,0:T(8,128)S(1)} %get-tuple-element.17.refs_2_, f32[32,8,128]{2,1,0:T(8,128)S(1)} %get-tuple-element.18.refs_3_, ...), custom_call_target="tpu_custom_call" | custom-call | tf_op jit(solution)/shard_map/pallas_call | solution.py:357
  (2 shorter events, 0.0 us)
Async XLA Ops:
  0.6 11.8 %copy-start.7 = (f32[48]{0:T(128)S(1)}, f32[48]{0:T(128)}, u32[]{:S(2)}) copy-start(f32[48]{0:T(128)} %param.12) | copy-start | bytes 580
  0.6 1.2 %copy-start = (f32[128,16,128]{2,1,0:T(8,128)S(1)}, f32[128,16,128]{2,1,0:T(8,128)}, u32[]{:S(2)}) copy-start(f32[128,16,128]{2,1,0:T(8,128)} %atm.1) | copy-start | bytes 3145732
  1.9 1.0 %copy-start.2 = (f32[48,16,128]{2,1,0:T(8,128)S(1)}, f32[48,16,128]{2,1,0:T(8,128)}, u32[]{:S(2)}) copy-start(f32[48,16,128]{2,1,0:T(8,128)} %ocean.1) | copy-start | bytes 1179652
  2.9 2.7 %copy-start.1 = (f32[128,16,128]{2,1,0:T(8,128)S(1)}, f32[128,16,128]{2,1,0:T(8,128)}, u32[]{:S(2)}) copy-start(f32[128,16,128]{2,1,0:T(8,128)} %atm.1) | copy-start | bytes 3145732
  2.9 2.7 %copy-start.3 = (f32[48,16,128]{2,1,0:T(8,128)S(1)}, f32[48,16,128]{2,1,0:T(8,128)}, u32[]{:S(2)}) copy-start(f32[48,16,128]{2,1,0:T(8,128)} %ocean.1) | copy-start | bytes 1179652
  2.9 13.6 %copy-start.4 = (bf16[1,48,128,128]{3,2,1,0:T(8,128)(2,1)S(1)}, bf16[1,48,128,128]{3,2,1,0:T(8,128)(2,1)}, u32[]{:S(2)}) copy-start(bf16[1,48,128,128]{3,2,1,0:T(8,128)(2,1)} %param.14) | copy-start | bytes 4718596
  3.7 16.2 %collective-permute-start = (bf16[2,176,128]{2,1,0:T(8,128)(2,1)}, bf16[2,176,128]{2,1,0:T(8,128)(2,1)S(1)}, u32[]{:S(2)}, u32[]{:S(2)}) collective-permute-start(bf16[2,176,128]{2,1,0:T(8,128)(2,1)} %get-tuple-element.14), channel_id=1, source_target_pairs={{0,4},{4,0},{8,12},{12,8},{16,20},{20,16},{24,28},{28,24},{1,5},{5... | collective-permute-start | bytes 270344 | tf_op jit(solution)/shard_map/ppermute | solution.py:302
  4.2 15.7 %collective-permute-start.1 = (bf16[2,176,128]{2,1,0:T(8,128)(2,1)}, bf16[2,176,128]{2,1,0:T(8,128)(2,1)S(1)}, u32[]{:S(2)}, u32[]{:S(2)}) collective-permute-start(bf16[2,176,128]{2,1,0:T(8,128)(2,1)} %get-tuple-element.15), channel_id=1, source_target_pairs={{4,8},{12,16},{20,24},{8,4},{16,12},{24,20},{5,9},{13,17},{21,25},... | collective-permute-start | bytes 270344 | tf_op jit(solution)/shard_map/ppermute | solution.py:303
  6.4 6.9 %collective-permute-start.4 = (bf16[32,8,128]{2,1,0:T(8,128)(2,1)S(1)}, bf16[32,8,128]{2,1,0:T(8,128)(2,1)S(1)}, u32[]{:S(2)}, u32[]{:S(2)}) collective-permute-start(bf16[32,8,128]{2,1,0:T(8,128)(2,1)S(1)} %shard_map.106.refs_4_), channel_id=1, source_target_pairs={{0,2},{1,3},{2,0},{3,1},{4,6},{5,7},{6,4},{7,5},{8,10},{9,11},{10,... | collective-permute-start | bytes 196616 | tf_op jit(solution)/shard_map/ppermute | solution.py:292
  10.2 6.3 %collective-permute-start.3 = (bf16[32,8,128]{2,1,0:T(8,128)(2,1)S(1)}, bf16[32,8,128]{2,1,0:T(8,128)(2,1)S(1)}, u32[]{:S(2)}, u32[]{:S(2)}) collective-permute-start(bf16[32,8,128]{2,1,0:T(8,128)(2,1)S(1)} %shard_map.106.refs_4_), channel_id=1, source_target_pairs={{0,3},{1,2},{2,1},{3,0},{4,7},{5,6},{6,5},{7,4},{8,11},{9,10},{10,... | collective-permute-start | bytes 196616 | tf_op jit(solution)/shard_map/ppermute | solution.py:292
  11.5 5.0 %collective-permute-start.2 = (bf16[32,8,128]{2,1,0:T(8,128)(2,1)S(1)}, bf16[32,8,128]{2,1,0:T(8,128)(2,1)S(1)}, u32[]{:S(2)}, u32[]{:S(2)}) collective-permute-start(bf16[32,8,128]{2,1,0:T(8,128)(2,1)S(1)} %shard_map.106.refs_4_), channel_id=1, source_target_pairs={{0,1},{1,0},{2,3},{3,2},{4,5},{5,4},{6,7},{7,6},{8,9},{9,8},{10,11... | collective-permute-start | bytes 196616 | tf_op jit(solution)/shard_map/ppermute | solution.py:292
  16.5 0.7 %copy-start.5 = (s32[1,48]{1,0:T(1,128)S(1)}, s32[1,48]{1,0:T(1,128)}, u32[]{:S(2)}) copy-start(s32[1,48]{1,0:T(1,128)} %refs_0_.2) | copy-start | bytes 580
  17.1 0.7 %copy-start.6 = (s32[1,48]{1,0:T(1,128)S(1)}, s32[1,48]{1,0:T(1,128)}, u32[]{:S(2)}) copy-start(s32[1,48]{1,0:T(1,128)} %refs_1_.1) | copy-start | bytes 580
  22.0 10.6 %collective-permute-start.6 = (bf16[304,128]{1,0:T(8,128)(2,1)S(1)}, bf16[304,128]{1,0:T(8,128)(2,1)S(1)}, u32[]{:S(2)}, u32[]{:S(2)}) collective-permute-start(bf16[304,128]{1,0:T(8,128)(2,1)S(1)} %pad_maximum_fusion.1), channel_id=1, source_target_pairs={{0,3},{1,2},{2,1},{3,0},{4,7},{5,6},{6,5},{7,4},{8,11},{9,10},{10,... | collective-permute-start | bytes 233480 | tf_op jit(solution)/shard_map/ppermute | solution.py:344
  24.2 8.5 %collective-permute-start.5 = (bf16[304,128]{1,0:T(8,128)(2,1)S(1)}, bf16[304,128]{1,0:T(8,128)(2,1)S(1)}, u32[]{:S(2)}, u32[]{:S(2)}) collective-permute-start(bf16[304,128]{1,0:T(8,128)(2,1)S(1)} %pad_maximum_fusion), channel_id=1, source_target_pairs={{0,1},{1,0},{2,3},{3,2},{4,5},{5,4},{6,7},{7,6},{8,9},{9,8},{10,11... | collective-permute-start | bytes 233480 | tf_op jit(solution)/shard_map/ppermute | solution.py:344
  25.7 7.0 %collective-permute-start.7 = (bf16[256,128]{1,0:T(8,128)(2,1)S(1)}, bf16[256,128]{1,0:T(8,128)(2,1)S(1)}, u32[]{:S(2)}, u32[]{:S(2)}) collective-permute-start(bf16[256,128]{1,0:T(8,128)(2,1)S(1)} %bitcast.19), channel_id=1, source_target_pairs={{0,2},{1,3},{2,0},{3,1},{4,6},{5,7},{6,4},{7,5},{8,10},{9,11},{10,... | collective-permute-start | bytes 196616 | tf_op jit(solution)/shard_map/ppermute | solution.py:344

commit v2 on v1

v2 whole, which is shorter than its diff:
```python
import functools

import jax
import jax.numpy as jnp
from jax import lax
from jax.experimental import pallas as pl
from jax.experimental.pallas import tpu as pltpu
from jax.sharding import PartitionSpec as P

SURF = 8
F32 = jnp.float32
BF16 = jnp.bfloat16
VMEM = pl.BlockSpec(memory_space=pltpu.VMEM)
SMEM = pl.BlockSpec(memory_space=pltpu.SMEM)
HBM = pl.BlockSpec(memory_space=pltpu.HBM)
ANY = pl.BlockSpec(memory_space=pl.ANY)


def beside_even(index):
    return index + 1 - 2 * (index % 2)


def beside_odd(index, count):
    return (index - 1 + 2 * (index % 2) + count) % count


def tile_pairs(count):
    routes = [
        [(i, beside_even(i)) for i in range(count)],
        [(i, beside_odd(i, count)) for i in range(count)],
    ]
    routes += [[(i, (i + s) % count) for i in range(count)] for s in range(2, count - 1)]
    return routes


def peers(me, count):
    a = beside_even(me)
    b = beside_odd(me, count)
    far = range(2, count - 1)
    sources = [a, b] + [lax.rem(me - s + count, count) for s in far]
    targets = [a, b] + [lax.rem(me + s, count) for s in far]
    return sources, targets


def comp_pairs(count):
    even = [(i, beside_even(i)) for i in range(count)]
    odd = [(i, i + 1) for i in range(1, count - 1, 2)] + [(i + 1, i) for i in range(1, count - 1, 2)]
    return even, odd


def pack_surface(rows_a, rows_o, mask, atm, ocean, out, wet, atm_part, ocean_part, done):
    copies = [
        pltpu.make_async_copy(mask, wet, done.at[0]),
        pltpu.make_async_copy(atm.at[0 : SURF * rows_a], atm_part, done.at[1]),
        pltpu.make_async_copy(ocean.at[0 : SURF * rows_o], ocean_part, done.at[2]),
    ]
    for copy in copies:
        copy.start()
    copies[1].wait()
    for y in range(rows_a):
        out[y] = atm_part[pl.ds(y, SURF, stride=rows_a), :].astype(BF16)
    copies[0].wait()
    copies[2].wait()
    for y in range(rows_o):
        tile = ocean_part[pl.ds(y, SURF, stride=rows_o), :]
        out[rows_a + y] = (tile * wet[0, y].astype(F32)).astype(BF16)


def prepare(rows_a, rows_o, anchor, atm, ocean, rate_a, rate_o, src, tgt, number, even_out, odd_out, table, rate):
    del anchor
    parity = lax.rem(lax.axis_index("comp"), 2)
    lanes = atm.shape[1]
    at = 0
    for ref, rows in ((atm, rows_a), (ocean, rows_o)):
        channels = ref.shape[0] // rows
        for c in range(0, channels, 8):
            for r in range(2):
                low = ref[pl.ds(c * rows + r, 8, stride=rows), :]
                high = ref[pl.ds(c * rows + rows - 2 + r, 8, stride=rows), :]
                even_out[r, at + c : at + c + 8, :] = jnp.where(parity == 0, high, low).astype(BF16)
                odd_out[r, at + c : at + c + 8, :] = jnp.where(parity == 0, low, high).astype(BF16)
        at += channels
    split = rate_a.shape[1]
    rate[0:split, :] = jnp.broadcast_to(rate_a[...], (lanes, split)).T
    rate[split:, :] = jnp.broadcast_to(rate_o[...], (lanes, rate_o.shape[1])).T
    block = rows_a + rows_o
    pairs = src.shape[1]
    table[0:1, 0:pairs] = lax.div(src[...], rows_a) * block + lax.rem(src[...], rows_a)
    table[1:2, 0:pairs] = lax.div(tgt[...], rows_o) * block + rows_a + lax.rem(tgt[...], rows_o)
    table[2:3, 0:1] = number[...]


def halo_rows(parity, even_in, odd_in, at):
    e = [even_in[r, at : at + 8, :].astype(F32) for r in range(2)]
    o = [odd_in[r, at : at + 8, :].astype(F32) for r in range(2)]
    north = [jnp.where(parity == 0, o[r], e[r]) for r in range(2)]
    south = [jnp.where(parity == 0, e[r], o[r]) for r in range(2)]
    return north, south


def pack_columns(rows_a, rows_o, atm, ocean, rate, even_in, odd_in, out_a, out_b, spread, stage):
    parity = lax.rem(lax.axis_index("comp"), 2)
    tile_parity = lax.rem(lax.axis_index("tile"), 2)
    lanes = atm.shape[1]
    row = lax.broadcasted_iota(jnp.int32, (8, lanes), 0)
    lane = lax.broadcasted_iota(jnp.int32, (8, lanes), 1)
    east = lax.div(row, 2) == tile_parity
    second = lax.rem(row, 2)
    spot = jnp.where(east, lanes - 1 - second, second)
    pick = jnp.where((row < 4) & (lane == spot), 1.0, 0.0).astype(BF16)
    outer = (lane == 0) | (lane == lanes - 1)
    turn = (lane == 1) | (lane == lanes - 1)
    dims = (((1,), (1,)), ((), ()))
    stage[...] = jnp.zeros_like(stage)
    at = 0
    for ref, rows in ((atm, rows_a), (ocean, rows_o)):
        channels = ref.shape[0] // rows
        for c in range(0, channels, 8):
            rho = rate[at + c : at + c + 8, :]
            own = 2.0 * rho * (1.0 - 4.0 * rho)
            square = rho * rho
            north, south = halo_rows(parity, even_in, odd_in, at + c)
            q = [north[1]]
            q += [ref[pl.ds(c * rows + r, 8, stride=rows), :] for r in range(rows)]
            q += [south[0]]
            for r in range(rows):
                far = square * q[r + 1]
                near = own * q[r + 1] + 2.0 * square * (q[r] + q[r + 2])
                moved = jnp.where(turn, pltpu.roll(far, 1, 1), pltpu.roll(far, lanes - 1, 1))
                value = moved + jnp.where(outer, near, 0.0)
                spread[pl.ds((at + c) * rows + r, 8, stride=rows), :] = value
        at += channels
    for j in range(at // 8):
        part = spread[j * 8 * rows_a : (j + 1) * 8 * rows_a, :].astype(BF16)
        found = lax.dot_general(pick, part, dims, preferred_element_type=F32)
        stage[0, 2 * j : 2 * j + 2, :] = found[0:2, :]
        stage[1, 2 * j : 2 * j + 2, :] = found[2:4, :]
    out_a[...] = stage[0].astype(BF16)
    out_b[...] = stage[1].astype(BF16)


def remap(tile_count, block, *refs):
    table, weights, own, col_a, col_b = refs[:5]
    got = refs[5 : 4 + tile_count]
    own_out = refs[4 + tile_count]
    outs = refs[5 + tile_count : 4 + 2 * tile_count]
    band, total = refs[4 + 2 * tile_count :]
    me = lax.axis_index("tile")
    sources, targets = peers(me, tile_count)
    band[pl.ds(me * block, block)] = own[...]
    for e, ref in zip(sources, got):
        band[pl.ds(e * block, block)] = ref[...]
    total[...] = jnp.zeros_like(total)
    pairs = weights.shape[0]
    live_count = table[2, 0]
    trans = (((1,), (1,)), ((), ()))
    plain = (((1,), (0,)), ((), ()))
    group = 8
    for start in range(0, pairs, group):
        made = []
        for k in range(start, min(start + group, pairs)):
            at_a = table[0, k]
            at_o = table[1, k]
            live = k < live_count
            w = weights[k]
            ta = band[at_a]
            to = band[at_o]
            ta = jnp.where(live, ta, jnp.zeros_like(ta))
            to = jnp.where(live, to, jnp.zeros_like(to))
            ahead = lax.dot_general(ta, w, plain, preferred_element_type=F32)
            back = lax.dot_general(to, w, trans, preferred_element_type=F32)
            made.append((at_a, at_o, ahead, back))
        for at_a, at_o, ahead, back in made:
            total[at_o] += ahead
            total[at_a] += back
    own_out[...] = total[pl.ds(me * block, block)]
    lanes = weights.shape[2]
    for e, ref in zip(targets, outs):
        part = total[pl.ds(e * block, block)].astype(BF16)
        ref[0 : block * SURF, :] = part.reshape(block * SURF, lanes)
    for ref, col in zip(outs, (col_a, col_b)):
        ref[block * SURF :, :] = col[...]


def stencil(rows_a, rows_o, atm, ocean, rate, even_in, odd_in, atm_out, ocean_out):
    comp = lax.axis_index("comp")
    parity = lax.rem(comp, 2)
    lanes = atm.shape[1]
    lane = lax.broadcasted_iota(jnp.int32, (8, lanes), 1)
    at_west = lane == 0
    at_east = lane == lanes - 1
    keep_north = jnp.where(comp == 0, 0.0, 1.0).astype(F32)
    keep_south = jnp.where(comp == lax.axis_size("comp") - 1, 0.0, 1.0).astype(F32)
    at = 0
    for ref, rows, out in ((atm, rows_a, atm_out), (ocean, rows_o, ocean_out)):
        channels = ref.shape[0] // rows
        for c in range(0, channels, 8):
            rho = rate[at + c : at + c + 8, :]
            own = 1.0 - 4.0 * rho
            north, south = halo_rows(parity, even_in, odd_in, at + c)
            q = north + [ref[pl.ds(c * rows + r, 8, stride=rows), :] for r in range(rows)] + south
            p = []
            for i in range(1, rows + 3):
                west = jnp.where(at_west, 0.0, pltpu.roll(q[i], 1, 1))
                east = jnp.where(at_east, 0.0, pltpu.roll(q[i], lanes - 1, 1))
                p.append(own * q[i] + rho * ((q[i - 1] + q[i + 1]) + (west + east)))
            p[0] = p[0] * keep_north
            p[rows + 1] = p[rows + 1] * keep_south
            for r in range(rows):
                ghost = rho * q[r + 2]
                west = jnp.where(at_west, ghost, pltpu.roll(p[r + 1], 1, 1))
                east = jnp.where(at_east, ghost, pltpu.roll(p[r + 1], lanes - 1, 1))
                out[pl.ds(c * rows + r, 8, stride=rows), :] = own * p[r + 1] + rho * (
                    (p[r] + p[r + 2]) + (west + east)
                )
        at += channels


def final(tile_count, rows_a, rows_o, *refs):
    mask, atm, ocean, own = refs[:4]
    got = refs[4 : 3 + tile_count]
    atm_out, ocean_out, force, value_a, value_o, done = refs[3 + tile_count :]
    lanes = atm.shape[1]
    block = rows_a + rows_o
    message = block * SURF
    tile_parity = lax.rem(lax.axis_index("tile"), 2)
    row = lax.broadcasted_iota(jnp.int32, (8, lanes), 0)
    lane = lax.broadcasted_iota(jnp.int32, (8, lanes), 1)
    east = lax.div(row, 2) == tile_parity
    second = lax.rem(row, 2)
    spot = jnp.where(east, lanes - 1 - second, second)
    place = jnp.where((row < 4) & (lane == spot), 1.0, 0.0).astype(BF16)
    for y in range(block):
        total = own[y]
        for ref in got:
            total = total + ref[SURF * y : SURF * y + SURF, :].astype(F32)
        if y >= rows_a:
            total = total * mask[0, y - rows_a].astype(F32)
        start = y if y < rows_a else SURF * rows_a + y - rows_a
        force[pl.ds(start, SURF, stride=rows_a if y < rows_a else rows_o), :] = total
    dims = (((0,), (0,)), ((), ()))
    group = 32
    at = 0
    copies = []
    for ref, keep, out, rows, add in (
        (atm, value_a, atm_out, rows_a, 0),
        (ocean, value_o, ocean_out, rows_o, SURF * rows_a),
    ):
        channels = ref.shape[0] // rows
        for c in range(0, channels, 8):
            j = message + 2 * ((at + c) // 8)
            sides = jnp.concatenate(
                [
                    got[0][j : j + 2, :].astype(F32),
                    got[1][j : j + 2, :].astype(F32),
                    jnp.zeros((4, lanes), F32),
                ],
                axis=0,
            ).astype(BF16)
            value = ref[c * rows : (c + 8) * rows, :] + lax.dot_general(
                sides, place, dims, preferred_element_type=F32
            )
            if c == 0:
                value = value + force[add : add + SURF * rows, :]
            keep[c * rows : (c + 8) * rows, :] = value
            if (c + 8) % group == 0 or c + 8 == channels:
                begin = c // group * group * rows
                end = (c + 8) * rows
                copies.append(
                    pltpu.make_async_copy(
                        keep.at[begin:end], out.at[begin:end], done.at[len(copies)]
                    )
                )
                copies[-1].start()
        at += channels
    for copy in copies:
        copy.wait()


def params(limit=None):
    return pltpu.CompilerParams(vmem_limit_bytes=limit)


def shards(
    atm_state,
    ocean_state,
    atm_rate,
    ocean_rate,
    ocean_mask,
    remap_weight,
    pair_src,
    pair_tgt,
    pair_count,
):
    channels_a, rows_a, lanes = atm_state.shape
    channels_o, rows_o, _ = ocean_state.shape
    channels = channels_a + channels_o
    tile_count = lax.axis_size("tile")
    block = rows_a + rows_o
    message = block * SURF
    extra = -(-2 * channels // 8 // 16) * 16
    atm = atm_state.reshape(channels_a * rows_a, lanes)
    ocean = ocean_state.reshape(channels_o * rows_o, lanes)
    mask = ocean_mask.reshape(1, rows_o)
    routes = tile_pairs(tile_count)
    even_pairs, odd_pairs = comp_pairs(lax.axis_size("comp"))

    surface = pl.pallas_call(
        functools.partial(pack_surface, rows_a, rows_o),
        in_specs=[HBM] * 3,
        out_specs=VMEM,
        out_shape=jax.ShapeDtypeStruct((block, SURF, lanes), BF16),
        scratch_shapes=[
            pltpu.SMEM((1, rows_o), jnp.int32),
            pltpu.VMEM((SURF * rows_a, lanes), F32),
            pltpu.VMEM((SURF * rows_o, lanes), F32),
            pltpu.SemaphoreType.DMA((3,)),
        ],
        compiler_params=params(4 << 20),
        name="pack_surface",
    )(mask, atm, ocean)
    received = [lax.ppermute(surface, "tile", route) for route in routes]

    halo = jax.ShapeDtypeStruct((2, channels, lanes), BF16)
    even_rows, odd_rows, table, rate = pl.pallas_call(
        functools.partial(prepare, rows_a, rows_o),
        in_specs=[ANY] + [VMEM] * 7,
        out_specs=[VMEM] * 4,
        out_shape=[
            halo,
            halo,
            jax.ShapeDtypeStruct((8, lanes), jnp.int32),
            jax.ShapeDtypeStruct((channels, lanes), F32),
        ],
        compiler_params=params(8 << 20),
        name="prepare",
    )(
        surface,
        atm,
        ocean,
        atm_rate.reshape(1, channels_a),
        ocean_rate.reshape(1, channels_o),
        pair_src,
        pair_tgt,
        pair_count,
    )
    even_in = lax.ppermute(even_rows, "comp", even_pairs)
    odd_in = lax.ppermute(odd_rows, "comp", odd_pairs)

    col_a, col_b = pl.pallas_call(
        functools.partial(pack_columns, rows_a, rows_o),
        in_specs=[VMEM] * 5,
        out_specs=[VMEM, VMEM],
        out_shape=[jax.ShapeDtypeStruct((extra, lanes), BF16)] * 2,
        scratch_shapes=[
            pltpu.VMEM((channels_a * rows_a + channels_o * rows_o, lanes), F32),
            pltpu.VMEM((2, extra, lanes), F32),
        ],
        compiler_params=params(8 << 20),
        name="pack_columns",
    )(atm, ocean, rate, even_in, odd_in)

    sends = [jax.ShapeDtypeStruct((message + extra, lanes), BF16)] * 2
    sends += [jax.ShapeDtypeStruct((message, lanes), BF16)] * (tile_count - 3)
    own_part, *parts = pl.pallas_call(
        functools.partial(remap, tile_count, block),
        in_specs=[SMEM] + [VMEM] * (3 + tile_count),
        out_specs=[VMEM] * tile_count,
        out_shape=[jax.ShapeDtypeStruct((block, SURF, lanes), F32)] + sends,
        scratch_shapes=[
            pltpu.VMEM((tile_count * block, SURF, lanes), BF16),
            pltpu.VMEM((tile_count * block, SURF, lanes), F32),
        ],
        compiler_params=params(12 << 20),
        name="remap",
    )(table, remap_weight[0], surface, col_a, col_b, *received)
    returned = [lax.ppermute(part, "tile", route) for part, route in zip(parts, routes)]

    atm_base, ocean_base = pl.pallas_call(
        functools.partial(stencil, rows_a, rows_o),
        in_specs=[VMEM] * 5,
        out_specs=[VMEM, VMEM],
        out_shape=[
            jax.ShapeDtypeStruct(atm.shape, F32),
            jax.ShapeDtypeStruct(ocean.shape, F32),
        ],
        compiler_params=params(8 << 20),
        name="stencil",
    )(atm, ocean, rate, even_in, odd_in)

    atm_next, ocean_next = pl.pallas_call(
        functools.partial(final, tile_count, rows_a, rows_o),
        in_specs=[SMEM] + [VMEM] * (2 + tile_count),
        out_specs=[HBM, HBM],
        out_shape=[
            jax.ShapeDtypeStruct(atm.shape, F32),
            jax.ShapeDtypeStruct(ocean.shape, F32),
        ],
        scratch_shapes=[
            pltpu.VMEM((SURF * block, lanes), F32),
            pltpu.VMEM(atm.shape, F32),
            pltpu.VMEM(ocean.shape, F32),
            pltpu.SemaphoreType.DMA((channels // 8,)),
        ],
        compiler_params=params(12 << 20),
        name="final",
    )(mask, atm_base, ocean_base, own_part, *returned)
    return (
        atm_next.reshape(channels_a, rows_a, lanes),
        ocean_next.reshape(channels_o, rows_o, lanes),
    )


def solution(mesh):
    return jax.shard_map(
        shards,
        mesh=mesh,
        in_specs=(
            P(None, "comp", "tile"),
            P(None, "comp", "tile"),
            P(),
            P(),
            P("comp", "tile"),
            P("comp", "tile", None, None),
            P("comp", "tile"),
            P("comp", "tile"),
            P("comp", "tile"),
        ),
        out_specs=(P(None, "comp", "tile"), P(None, "comp", "tile")),
        check_vma=False,
    )
```

time: 35.3 us -> 36.6 us (1.037)
  the two profiles are of different devices: /device:TPU:0 before, /device:TPU:3 now
where the time goes in v2:
time: 36.6 us; the launch traced here: 36.3 us
  starting transfers between devices  11.7 us (32%)
  waiting for transfers between devices  8.61 us (24%)
  Pallas kernels  8.46 us (23%)
  local copies, waits for them, and re-layouts  6.2 us (17%)
  between operations  1.34 us (4%)
    unnamed x22, local copies, waits for them, and re-layouts  6.2 us
    ppermute x3, waiting for transfers between devices, shards(): lax.ppermute(part, 'tile', route)  4.86 us
    ppermute x3, starting transfers between devices, shards(): lax.ppermute(part, 'tile', route)  4.16 us
    ppermute x3, starting transfers between devices, shards(): received = [lax.ppermute(surface, 'tile', route) for route in routes]  3.67 us
    ppermute x3, waiting for transfers between devices, shards(): received = [lax.ppermute(surface, 'tile', route) for route in routes]  3.3 us
    ppermute x1, starting transfers between devices, shards(): odd_in = lax.ppermute(odd_rows, 'comp', odd_pairs)  3.15 us
    pallas_call x1, Pallas kernels, shards(): pl.pallas_call(functools.partial(stencil, rows_a, rows_o), in_specs=[VMEM...  2.44 us
    pallas_call x1, Pallas kernels, shards(): pl.pallas_call(functools.partial(remap, tile_count, block), in_specs=[SME...  2.07 us
  transfers between devices with their start and end apart: 8, of which 4 were waited for; matrix products, arithmetic and copies ran while one was open for 0% of the time, Pallas kernels for 10%

profile of v2, /device:TPU:3, one launch (start us, length us, event | category | flops | bytes accessed | tf_op | source)
XLA Modules:
  0.0 36.3 jit_solution(93506688669674135)
XLA Ops:
  1.3 0.0 copy-start
  1.3 1.2 %copy-done = f32[128,16,128]{2,1,0:T(8,128)S(1)} copy-done((f32[128,16,128]{2,1,0:T(8,128)S(1)}, f32[128,16,128]{2,1,0:T(8,128)}, u32[]{:S(2)}) %copy-start) | copy-done | bytes 1048600
  2.5 0.0 copy-start.2
  2.5 1.0 %copy-done.2 = f32[48,16,128]{2,1,0:T(8,128)S(1)} copy-done((f32[48,16,128]{2,1,0:T(8,128)S(1)}, f32[48,16,128]{2,1,0:T(8,128)}, u32[]{:S(2)}) %copy-start.2) | copy-done | bytes 393240
  3.5 0.0 copy-start.5
  3.5 0.7 %copy-done.5 = s32[16,1]{0,1:T(1,128)S(1)} copy-done((s32[16,1]{0,1:T(1,128)S(1)}, s32[16,1]{0,1:T(1,128)}, u32[]{:S(2)}) %copy-start.5) | copy-done | bytes 88
  4.2 0.0 copy-start.1
  4.2 0.0 copy-start.3
  4.2 0.6 %pack_surface.1.anchor.refs_2_ = bf16[32,8,128]{2,1,0:T(8,128)(2,1)S(1)} custom-call(s32[1,16]{1,0:T(1,128)S(1)} %bitcast.17, f32[2048,128]{1,0:T(8,128)S(1)} %bitcast.8, f32[768,128]{1,0:T(8,128)S(1)} %bitcast.12), custom_call_target="tpu_custom_call" | custom-call | tf_op jit(solution)/shard_map/pack_surface/pallas_call | solution.py:308
  4.8 0.6 %copy-done.1 = f32[128,16,128]{2,1,0:T(8,128)S(1)} copy-done((f32[128,16,128]{2,1,0:T(8,128)S(1)}, f32[128,16,128]{2,1,0:T(8,128)}, u32[]{:S(2)}) %copy-start.1) | copy-done | bytes 1048600
  5.4 0.1 copy-done.3
  5.5 0.0 copy-start.7
  5.5 0.7 %copy-done.7 = f32[128]{0:T(128)S(1)} copy-done((f32[128]{0:T(128)S(1)}, f32[128]{0:T(128)}, u32[]{:S(2)}) %copy-start.7) | copy-done | bytes 536
  6.1 0.0 copy-start.8
  6.1 0.7 %copy-done.8 = f32[48]{0:T(128)S(1)} copy-done((f32[48]{0:T(128)S(1)}, f32[48]{0:T(128)}, u32[]{:S(2)}) %copy-start.8) | copy-done | bytes 216
  6.8 0.0 copy-start.9
  6.8 0.7 %copy-done.9 = s32[1,48]{1,0:T(1,128)S(1)} copy-done((s32[1,48]{1,0:T(1,128)S(1)}, s32[1,48]{1,0:T(1,128)}, u32[]{:S(2)}) %copy-start.9) | copy-done | bytes 216
  7.4 0.0 copy-start.10
  7.4 0.7 %copy-done.10 = s32[1,48]{1,0:T(1,128)S(1)} copy-done((s32[1,48]{1,0:T(1,128)S(1)}, s32[1,48]{1,0:T(1,128)}, u32[]{:S(2)}) %copy-start.10) | copy-done | bytes 216
  8.1 0.0 copy-start.4
  8.1 0.1 prepare.1
  8.2 0.7 %collective-permute-start = (bf16[2,176,128]{2,1,0:T(8,128)(2,1)S(1)}, bf16[2,176,128]{2,1,0:T(8,128)(2,1)S(1)}, u32[]{:S(2)}, u32[]{:S(2)}) collective-permute-start(bf16[2,176,128]{2,1,0:T(8,128)(2,1)S(1)} %get-tuple-element.17), channel_id=1, source_target_pairs={{0,4},{4,0},{8,12},{12,8},{16,20},{20,16},{24,28},{28,24},{1,5},{5... | collective-permute-start | bytes 270344 | tf_op jit(solution)/shard_map/ppermute | solution.py:347
  9.0 3.1 %collective-permute-start.1 = (bf16[2,176,128]{2,1,0:T(8,128)(2,1)S(1)}, bf16[2,176,128]{2,1,0:T(8,128)(2,1)S(1)}, u32[]{:S(2)}, u32[]{:S(2)}) collective-permute-start(bf16[2,176,128]{2,1,0:T(8,128)(2,1)S(1)} %get-tuple-element.18), channel_id=1, source_target_pairs={{4,8},{12,16},{20,24},{8,4},{16,12},{24,20},{5,9},{13,17},{21,25},... | collective-permute-start | bytes 270344 | tf_op jit(solution)/shard_map/ppermute | solution.py:348
  12.1 2.4 %collective-permute-start.4 = (bf16[32,8,128]{2,1,0:T(8,128)(2,1)S(1)}, bf16[32,8,128]{2,1,0:T(8,128)(2,1)S(1)}, u32[]{:S(2)}, u32[]{:S(2)}) collective-permute-start(bf16[32,8,128]{2,1,0:T(8,128)(2,1)S(1)} %pack_surface.1.anchor.refs_2_), channel_id=1, source_target_pairs={{0,2},{1,3},{2,0},{3,1},{4,6},{5,7},{6,4},{7,5},{8,10},{9,11},{10,... | collective-permute-start | bytes 196616 | tf_op jit(solution)/shard_map/ppermute | solution.py:322
  14.5 1.1 %collective-permute-start.3 = (bf16[32,8,128]{2,1,0:T(8,128)(2,1)S(1)}, bf16[32,8,128]{2,1,0:T(8,128)(2,1)S(1)}, u32[]{:S(2)}, u32[]{:S(2)}) collective-permute-start(bf16[32,8,128]{2,1,0:T(8,128)(2,1)S(1)} %pack_surface.1.anchor.refs_2_), channel_id=1, source_target_pairs={{0,3},{1,2},{2,1},{3,0},{4,7},{5,6},{6,5},{7,4},{8,11},{9,10},{10,... | collective-permute-start | bytes 196616 | tf_op jit(solution)/shard_map/ppermute | solution.py:322
  15.6 0.2 collective-permute-start.2
  15.8 0.0 collective-permute-done.even_in
  15.8 0.4 %collective-permute-done.1.odd_in = bf16[2,176,128]{2,1,0:T(8,128)(2,1)S(1)} collective-permute-done((bf16[2,176,128]{2,1,0:T(8,128)(2,1)S(1)}, bf16[2,176,128]{2,1,0:T(8,128)(2,1)S(1)}, u32[]{:S(2)}, u32[]{:S(2)}) %collective-permute-start.1) | collective-permute-done | bytes 90144 | tf_op jit(solution)/shard_map/ppermute | solution.py:348
  16.3 1.2 %pack_columns.1 = (bf16[48,128]{1,0:T(8,128)(2,1)S(1)}, bf16[48,128]{1,0:T(8,128)(2,1)S(1)}) custom-call(f32[2048,128]{1,0:T(8,128)S(1)} %bitcast.10, f32[768,128]{1,0:T(8,128)S(1)} %bitcast.14, f32[176,128]{1,0:T(8,128)S(1)} %get-tuple-element.16.rate, bf16[2,176,128]{2,1,0:T(8,128)(2,1)S(1)} %collective-permute-done.even_in, ...), custom_call_target="tpu_custom_call" | custom-call | tf_op jit(solution)/shard_map/pack_columns/pallas_call | solution.py:350
  17.4 0.0 collective-permute-done.4.refs_7_
  17.4 2.9 %collective-permute-done.3.refs_6_ = bf16[32,8,128]{2,1,0:T(8,128)(2,1)S(1)} collective-permute-done((bf16[32,8,128]{2,1,0:T(8,128)(2,1)S(1)}, bf16[32,8,128]{2,1,0:T(8,128)(2,1)S(1)}, u32[]{:S(2)}, u32[]{:S(2)}) %collective-permute-start.3) | collective-permute-done | bytes 65568 | tf_op jit(solution)/shard_map/ppermute | solution.py:322
  20.3 0.4 %collective-permute-done.2.refs_5_ = bf16[32,8,128]{2,1,0:T(8,128)(2,1)S(1)} collective-permute-done((bf16[32,8,128]{2,1,0:T(8,128)(2,1)S(1)}, bf16[32,8,128]{2,1,0:T(8,128)(2,1)S(1)}, u32[]{:S(2)}, u32[]{:S(2)}) %collective-permute-start.2) | collective-permute-done | bytes 65568 | tf_op jit(solution)/shard_map/ppermute | solution.py:322
  20.7 0.0 copy-done.4
  20.7 0.0 copy-start.6
  20.7 2.1 %remap.1 = (f32[32,8,128]{2,1,0:T(8,128)S(1)}, bf16[304,128]{1,0:T(8,128)(2,1)S(1)}, bf16[304,128]{1,0:T(8,128)(2,1)S(1)}, bf16[256,128]{1,0:T(8,128)(2,1)S(1)}) custom-call(s32[8,128]{1,0:T(8,128)S(1)} %get-tuple-element.21.refs_0_, bf16[48,128,128]{2,1,0:T(8,128)(2,1)S(1)} %bitcast.16, bf16[32,8,128]{2,1,0:T(8,128)(2,1)S(1)} %pack_surface.1.anchor.refs_2_, ...), custom_call_target="tpu_custom_call" | custom-call | tf_op jit(solution)/shard_map/remap/pallas_call | solution.py:365
  22.8 1.1 %collective-permute-start.5 = (bf16[304,128]{1,0:T(8,128)(2,1)S(1)}, bf16[304,128]{1,0:T(8,128)(2,1)S(1)}, u32[]{:S(2)}, u32[]{:S(2)}) collective-permute-start(bf16[304,128]{1,0:T(8,128)(2,1)S(1)} %get-tuple-element.25), channel_id=1, source_target_pairs={{0,1},{1,0},{2,3},{3,2},{4,5},{5,4},{6,7},{7,6},{8,9},{9,8},{10,11... | collective-permute-start | bytes 233480 | tf_op jit(solution)/shard_map/ppermute | solution.py:377
  23.9 3.1 %collective-permute-start.6 = (bf16[304,128]{1,0:T(8,128)(2,1)S(1)}, bf16[304,128]{1,0:T(8,128)(2,1)S(1)}, u32[]{:S(2)}, u32[]{:S(2)}) collective-permute-start(bf16[304,128]{1,0:T(8,128)(2,1)S(1)} %get-tuple-element.26), channel_id=1, source_target_pairs={{0,3},{1,2},{2,1},{3,0},{4,7},{5,6},{6,5},{7,4},{8,11},{9,10},{10,... | collective-permute-start | bytes 233480 | tf_op jit(solution)/shard_map/ppermute | solution.py:377
  27.0 0.0 collective-permute-start.7
  27.0 2.4 %stencil.1 = (f32[2048,128]{1,0:T(8,128)S(1)}, f32[768,128]{1,0:T(8,128)S(1)}) custom-call(f32[2048,128]{1,0:T(8,128)S(1)} %bitcast.11, f32[768,128]{1,0:T(8,128)S(1)} %bitcast.15, f32[176,128]{1,0:T(8,128)S(1)} %get-tuple-element.16.rate, bf16[2,176,128]{2,1,0:T(8,128)(2,1)S(1)} %collective-permute-done.even_in, ...), custom_call_target="tpu_custom_call" | custom-call | tf_op jit(solution)/shard_map/stencil/pallas_call | solution.py:379
  29.4 4.9 %collective-permute-done.7.refs_6_ = bf16[256,128]{1,0:T(8,128)(2,1)S(1)} collective-permute-done((bf16[256,128]{1,0:T(8,128)(2,1)S(1)}, bf16[256,128]{1,0:T(8,128)(2,1)S(1)}, u32[]{:S(2)}, u32[]{:S(2)}) %collective-permute-start.7) | collective-permute-done | bytes 65568 | tf_op jit(solution)/shard_map/ppermute | solution.py:377
  34.3 0.0 collective-permute-done.5.refs_4_
  34.3 0.0 collective-permute-done.6.refs_5_
  34.3 0.0 copy-done.6
  34.3 2.1 %final.1 = (f32[2048,128]{1,0:T(8,128)}, f32[768,128]{1,0:T(8,128)}) custom-call(s32[1,16]{1,0:T(1,128)S(1)} %bitcast.18, f32[2048,128]{1,0:T(8,128)S(1)} %get-tuple-element.19.refs_1_, f32[768,128]{1,0:T(8,128)S(1)} %get-tuple-element.20.refs_2_, f32[32,8,128]{2,1,0:T(8,128)S(1)} %get-tuple-element.24.refs_3_, ...), custom_call_target="tpu_custom_call" | custom-call | tf_op jit(solution)/shard_map/final/pallas_call | solution.py:391
Async XLA Ops:
  1.3 1.2 %copy-start = (f32[128,16,128]{2,1,0:T(8,128)S(1)}, f32[128,16,128]{2,1,0:T(8,128)}, u32[]{:S(2)}) copy-start(f32[128,16,128]{2,1,0:T(8,128)} %param.9) | copy-start | bytes 3145732
  2.5 1.0 %copy-start.2 = (f32[48,16,128]{2,1,0:T(8,128)S(1)}, f32[48,16,128]{2,1,0:T(8,128)}, u32[]{:S(2)}) copy-start(f32[48,16,128]{2,1,0:T(8,128)} %param.10) | copy-start | bytes 1179652
  3.5 0.7 %copy-start.5 = (s32[16,1]{0,1:T(1,128)S(1)}, s32[16,1]{0,1:T(1,128)}, u32[]{:S(2)}) copy-start(s32[16,1]{0,1:T(1,128)} %param.13) | copy-start | bytes 196
  4.2 1.2 %copy-start.1 = (f32[128,16,128]{2,1,0:T(8,128)S(1)}, f32[128,16,128]{2,1,0:T(8,128)}, u32[]{:S(2)}) copy-start(f32[128,16,128]{2,1,0:T(8,128)} %param.9) | copy-start | bytes 3145732
  4.2 1.3 %copy-start.3 = (f32[48,16,128]{2,1,0:T(8,128)S(1)}, f32[48,16,128]{2,1,0:T(8,128)}, u32[]{:S(2)}) copy-start(f32[48,16,128]{2,1,0:T(8,128)} %param.10) | copy-start | bytes 1179652
  5.5 0.7 %copy-start.7 = (f32[128]{0:T(128)S(1)}, f32[128]{0:T(128)}, u32[]{:S(2)}) copy-start(f32[128]{0:T(128)} %param.11) | copy-start | bytes 1540
  6.1 0.7 %copy-start.8 = (f32[48]{0:T(128)S(1)}, f32[48]{0:T(128)}, u32[]{:S(2)}) copy-start(f32[48]{0:T(128)} %param.12) | copy-start | bytes 580
  6.8 0.7 %copy-start.9 = (s32[1,48]{1,0:T(1,128)S(1)}, s32[1,48]{1,0:T(1,128)}, u32[]{:S(2)}) copy-start(s32[1,48]{1,0:T(1,128)} %src.1) | copy-start | bytes 580
  7.4 0.7 %copy-start.10 = (s32[1,48]{1,0:T(1,128)S(1)}, s32[1,48]{1,0:T(1,128)}, u32[]{:S(2)}) copy-start(s32[1,48]{1,0:T(1,128)} %tgt.1) | copy-start | bytes 580
  8.1 12.6 %copy-start.4 = (bf16[1,48,128,128]{3,2,1,0:T(8,128)(2,1)S(1)}, bf16[1,48,128,128]{3,2,1,0:T(8,128)(2,1)}, u32[]{:S(2)}) copy-start(bf16[1,48,128,128]{3,2,1,0:T(8,128)(2,1)} %param.14) | copy-start | bytes 4718596
  8.2 7.6 %collective-permute-start = (bf16[2,176,128]{2,1,0:T(8,128)(2,1)S(1)}, bf16[2,176,128]{2,1,0:T(8,128)(2,1)S(1)}, u32[]{:S(2)}, u32[]{:S(2)}) collective-permute-start(bf16[2,176,128]{2,1,0:T(8,128)(2,1)S(1)} %get-tuple-element.17), channel_id=1, source_target_pairs={{0,4},{4,0},{8,12},{12,8},{16,20},{20,16},{24,28},{28,24},{1,5},{5... | collective-permute-start | bytes 270344 | tf_op jit(solution)/shard_map/ppermute | solution.py:347
  9.0 7.3 %collective-permute-start.1 = (bf16[2,176,128]{2,1,0:T(8,128)(2,1)S(1)}, bf16[2,176,128]{2,1,0:T(8,128)(2,1)S(1)}, u32[]{:S(2)}, u32[]{:S(2)}) collective-permute-start(bf16[2,176,128]{2,1,0:T(8,128)(2,1)S(1)} %get-tuple-element.18), channel_id=1, source_target_pairs={{4,8},{12,16},{20,24},{8,4},{16,12},{24,20},{5,9},{13,17},{21,25},... | collective-permute-start | bytes 270344 | tf_op jit(solution)/shard_map/ppermute | solution.py:348
  12.1 5.3 %collective-permute-start.4 = (bf16[32,8,128]{2,1,0:T(8,128)(2,1)S(1)}, bf16[32,8,128]{2,1,0:T(8,128)(2,1)S(1)}, u32[]{:S(2)}, u32[]{:S(2)}) collective-permute-start(bf16[32,8,128]{2,1,0:T(8,128)(2,1)S(1)} %pack_surface.1.anchor.refs_2_), channel_id=1, source_target_pairs={{0,2},{1,3},{2,0},{3,1},{4,6},{5,7},{6,4},{7,5},{8,10},{9,11},{10,... | collective-permute-start | bytes 196616 | tf_op jit(solution)/shard_map/ppermute | solution.py:322
  14.5 5.8 %collective-permute-start.3 = (bf16[32,8,128]{2,1,0:T(8,128)(2,1)S(1)}, bf16[32,8,128]{2,1,0:T(8,128)(2,1)S(1)}, u32[]{:S(2)}, u32[]{:S(2)}) collective-permute-start(bf16[32,8,128]{2,1,0:T(8,128)(2,1)S(1)} %pack_surface.1.anchor.refs_2_), channel_id=1, source_target_pairs={{0,3},{1,2},{2,1},{3,0},{4,7},{5,6},{6,5},{7,4},{8,11},{9,10},{10,... | collective-permute-start | bytes 196616 | tf_op jit(solution)/shard_map/ppermute | solution.py:322
  15.6 5.1 %collective-permute-start.2 = (bf16[32,8,128]{2,1,0:T(8,128)(2,1)S(1)}, bf16[32,8,128]{2,1,0:T(8,128)(2,1)S(1)}, u32[]{:S(2)}, u32[]{:S(2)}) collective-permute-start(bf16[32,8,128]{2,1,0:T(8,128)(2,1)S(1)} %pack_surface.1.anchor.refs_2_), channel_id=1, source_target_pairs={{0,1},{1,0},{2,3},{3,2},{4,5},{5,4},{6,7},{7,6},{8,9},{9,8},{10,11... | collective-permute-start | bytes 196616 | tf_op jit(solution)/shard_map/ppermute | solution.py:322
  20.7 13.6 %copy-start.6 = (s32[16,1]{0,1:T(1,128)S(1)}, s32[16,1]{0,1:T(1,128)}, u32[]{:S(2)}) copy-start(s32[16,1]{0,1:T(1,128)} %param.13) | copy-start | bytes 196
  22.8 11.5 %collective-permute-start.5 = (bf16[304,128]{1,0:T(8,128)(2,1)S(1)}, bf16[304,128]{1,0:T(8,128)(2,1)S(1)}, u32[]{:S(2)}, u32[]{:S(2)}) collective-permute-start(bf16[304,128]{1,0:T(8,128)(2,1)S(1)} %get-tuple-element.25), channel_id=1, source_target_pairs={{0,1},{1,0},{2,3},{3,2},{4,5},{5,4},{6,7},{7,6},{8,9},{9,8},{10,11... | collective-permute-start | bytes 233480 | tf_op jit(solution)/shard_map/ppermute | solution.py:377
  23.9 10.4 %collective-permute-start.6 = (bf16[304,128]{1,0:T(8,128)(2,1)S(1)}, bf16[304,128]{1,0:T(8,128)(2,1)S(1)}, u32[]{:S(2)}, u32[]{:S(2)}) collective-permute-start(bf16[304,128]{1,0:T(8,128)(2,1)S(1)} %get-tuple-element.26), channel_id=1, source_target_pairs={{0,3},{1,2},{2,1},{3,0},{4,7},{5,6},{6,5},{7,4},{8,11},{9,10},{10,... | collective-permute-start | bytes 233480 | tf_op jit(solution)/shard_map/ppermute | solution.py:377
  27.0 7.3 %collective-permute-start.7 = (bf16[256,128]{1,0:T(8,128)(2,1)S(1)}, bf16[256,128]{1,0:T(8,128)(2,1)S(1)}, u32[]{:S(2)}, u32[]{:S(2)}) collective-permute-start(bf16[256,128]{1,0:T(8,128)(2,1)S(1)} %get-tuple-element.27), channel_id=1, source_target_pairs={{0,2},{1,3},{2,0},{3,1},{4,6},{5,7},{6,4},{7,5},{8,10},{9,11},{10,... | collective-permute-start | bytes 196616 | tf_op jit(solution)/shard_map/ppermute | solution.py:377

commit v3 on v2

--- a/solution.py
+++ b/solution.py
@@ -6,6 +6,7 @@
 from jax.experimental import pallas as pl
 from jax.experimental.pallas import tpu as pltpu
 from jax.sharding import PartitionSpec as P
+
 
 SURF = 8
 F32 = jnp.float32
@@ -48,28 +49,40 @@
     return even, odd
 
 
-def pack_surface(rows_a, rows_o, mask, atm, ocean, out, wet, atm_part, ocean_part, done):
+def prepare(rows_a, rows_o, *refs):
+    ins, outs = refs[:7], refs[7:15]
+    rate_a, rate_o, done = refs[15:]
+    atm_in, ocean_in, mask_in, src_in, tgt_in, rate_a_in, rate_o_in = ins
+    atm, ocean, surface, even_out, odd_out, rate, table, mask = outs
     copies = [
-        pltpu.make_async_copy(mask, wet, done.at[0]),
-        pltpu.make_async_copy(atm.at[0 : SURF * rows_a], atm_part, done.at[1]),
-        pltpu.make_async_copy(ocean.at[0 : SURF * rows_o], ocean_part, done.at[2]),
+        (mask_in, mask),
+        (atm_in.at[0 : SURF * rows_a], atm.at[0 : SURF * rows_a]),
+        (ocean_in.at[0 : SURF * rows_o], ocean.at[0 : SURF * rows_o]),
+        (src_in, table.at[0:1]),
+        (tgt_in, table.at[1:2]),
+        (rate_a_in, rate_a),
+        (rate_o_in, rate_o),
+        (atm_in.at[SURF * rows_a :], atm.at[SURF * rows_a :]),
+        (ocean_in.at[SURF * rows_o :], ocean.at[SURF * rows_o :]),
     ]
+    copies = [pltpu.make_async_copy(a, b, done.at[i]) for i, (a, b) in enumerate(copies)]
     for copy in copies:
         copy.start()
     copies[1].wait()
     for y in range(rows_a):
-        out[y] = atm_part[pl.ds(y, SURF, stride=rows_a), :].astype(BF16)
+        surface[y] = atm[pl.ds(y, SURF, stride=rows_a), :].astype(BF16)
     copies[0].wait()
     copies[2].wait()
     for y in range(rows_o):
-        tile = ocean_part[pl.ds(y, SURF, stride=rows_o), :]
-        out[rows_a + y] = (tile * wet[0, y].astype(F32)).astype(BF16)
-
-
-def prepare(rows_a, rows_o, anchor, atm, ocean, rate_a, rate_o, src, tgt, number, even_out, odd_out, table, rate):
-    del anchor
+        tile = ocean[pl.ds(y, SURF, stride=rows_o), :]
+        surface[rows_a + y] = (tile * mask[0, y].astype(F32)).astype(BF16)
+    for copy in copies[3:]:
+        copy.wait()
+    lanes = atm.shape[1]
+    split = rate_a.shape[1]
+    rate[0:split, :] = jnp.broadcast_to(rate_a[...], (lanes, split)).T
+    rate[split:, :] = jnp.broadcast_to(rate_o[...], (lanes, rate_o.shape[1])).T
     parity = lax.rem(lax.axis_index("comp"), 2)
-    lanes = atm.shape[1]
     at = 0
     for ref, rows in ((atm, rows_a), (ocean, rows_o)):
         channels = ref.shape[0] // rows
@@ -80,14 +93,6 @@
                 even_out[r, at + c : at + c + 8, :] = jnp.where(parity == 0, high, low).astype(BF16)
                 odd_out[r, at + c : at + c + 8, :] = jnp.where(parity == 0, low, high).astype(BF16)
         at += channels
-    split = rate_a.shape[1]
-    rate[0:split, :] = jnp.broadcast_to(rate_a[...], (lanes, split)).T
-    rate[split:, :] = jnp.broadcast_to(rate_o[...], (lanes, rate_o.shape[1])).T
-    block = rows_a + rows_o
-    pairs = src.shape[1]
-    table[0:1, 0:pairs] = lax.div(src[...], rows_a) * block + lax.rem(src[...], rows_a)
-    table[1:2, 0:pairs] = lax.div(tgt[...], rows_o) * block + rows_a + lax.rem(tgt[...], rows_o)
-    table[2:3, 0:1] = number[...]
 
 
 def halo_rows(parity, even_in, odd_in, at):
@@ -139,12 +144,13 @@
     out_b[...] = stage[1].astype(BF16)
 
 
-def remap(tile_count, block, *refs):
-    table, weights, own, col_a, col_b = refs[:5]
-    got = refs[5 : 4 + tile_count]
-    own_out = refs[4 + tile_count]
-    outs = refs[5 + tile_count : 4 + 2 * tile_count]
-    band, total = refs[4 + 2 * tile_count :]
+def remap(tile_count, rows_a, rows_o, *refs):
+    table, number, weights, own, col_a, col_b = refs[:6]
+    got = refs[6 : 5 + tile_count]
+    own_out = refs[5 + tile_count]
+    outs = refs[6 + tile_count : 5 + 2 * tile_count]
+    band, total = refs[5 + 2 * tile_count :]
+    block = rows_a + rows_o
     me = lax.axis_index("tile")
     sources, targets = peers(me, tile_count)
     band[pl.ds(me * block, block)] = own[...]
@@ -152,15 +158,17 @@
         band[pl.ds(e * block, block)] = ref[...]
     total[...] = jnp.zeros_like(total)
     pairs = weights.shape[0]
-    live_count = table[2, 0]
+    live_count = number[0, 0]
     trans = (((1,), (1,)), ((), ()))
     plain = (((1,), (0,)), ((), ()))
     group = 8
     for start in range(0, pairs, group):
         made = []
         for k in range(start, min(start + group, pairs)):
-            at_a = table[0, k]
-            at_o = table[1, k]
+            a = table[0, k]
+            o = table[1, k]
+            at_a = lax.div(a, rows_a) * block + lax.rem(a, rows_a)
+            at_o = lax.div(o, rows_o) * block + rows_a + lax.rem(o, rows_o)
             live = k < live_count
             w = weights[k]
             ta = band[at_a]
@@ -277,11 +285,25 @@
         copy.wait()
 
 
-def params(limit=None):
-    return pltpu.CompilerParams(vmem_limit_bytes=limit)
-
-
-def shards(
+def call(body, micros, limit, **rest):
+    return pl.pallas_call(
+        body,
+        compiler_params=pltpu.CompilerParams(vmem_limit_bytes=limit),
+        cost_estimate=pl.CostEstimate(
+            flops=0, transcendentals=0, bytes_accessed=int(micros * 3.0e6)
+        ),
+        **rest,
+    )
+
+
+def exchange(blocks, routes):
+    out = []
+    for block, route in zip(blocks, routes):
+        out.append(lax.ppermute(block, "tile", route))
+    return out
+
+
+def interval(
     atm_state,
     ocean_state,
     atm_rate,
@@ -305,50 +327,52 @@
     routes = tile_pairs(tile_count)
     even_pairs, odd_pairs = comp_pairs(lax.axis_size("comp"))
 
-    surface = pl.pallas_call(
-        functools.partial(pack_surface, rows_a, rows_o),
-        in_specs=[HBM] * 3,
-        out_specs=VMEM,
-        out_shape=jax.ShapeDtypeStruct((block, SURF, lanes), BF16),
-        scratch_shapes=[
-            pltpu.SMEM((1, rows_o), jnp.int32),
-            pltpu.VMEM((SURF * rows_a, lanes), F32),
-            pltpu.VMEM((SURF * rows_o, lanes), F32),
-            pltpu.SemaphoreType.DMA((3,)),
-        ],
-        compiler_params=params(4 << 20),
-        name="pack_surface",
-    )(mask, atm, ocean)
-    received = [lax.ppermute(surface, "tile", route) for route in routes]
-
-    halo = jax.ShapeDtypeStruct((2, channels, lanes), BF16)
-    even_rows, odd_rows, table, rate = pl.pallas_call(
+    halo = pltpu.VMEM((2, channels, lanes), BF16)
+    atm, ocean, surface, even_rows, odd_rows, rate, table, mask = call(
         functools.partial(prepare, rows_a, rows_o),
-        in_specs=[ANY] + [VMEM] * 7,
-        out_specs=[VMEM] * 4,
+        1.5,
+        8 << 20,
+        in_specs=[HBM] * 7,
+        out_specs=[VMEM] * 6 + [SMEM] * 2,
         out_shape=[
+            pltpu.VMEM(atm.shape, F32),
+            pltpu.VMEM(ocean.shape, F32),
+            pltpu.VMEM((block, SURF, lanes), BF16),
             halo,
             halo,
-            jax.ShapeDtypeStruct((8, lanes), jnp.int32),
-            jax.ShapeDtypeStruct((channels, lanes), F32),
-        ],
-        compiler_params=params(8 << 20),
+            pltpu.VMEM((channels, lanes), F32),
+            pltpu.SMEM((2, pair_src.shape[1]), jnp.int32),
+            pltpu.SMEM((1, rows_o), jnp.int32),
+        ],
+        scratch_shapes=[
+            pltpu.VMEM((1, channels_a), F32),
+            pltpu.VMEM((1, channels_o), F32),
+            pltpu.SemaphoreType.DMA((9,)),
+        ],
         name="prepare",
     )(
-        surface,
-        atm,
-        ocean,
-        atm_rate.reshape(1, channels_a),
-        ocean_rate.reshape(1, channels_o),
-        pair_src,
-        pair_tgt,
-        pair_count,
+        *[
+            pltpu.with_memory_space_constraint(x, pltpu.HBM)
+            for x in (
+                atm,
+                ocean,
+                mask,
+                pair_src,
+                pair_tgt,
+                atm_rate.reshape(1, channels_a),
+                ocean_rate.reshape(1, channels_o),
+            )
+        ]
     )
+    received = exchange([surface] * len(routes), routes)
+
     even_in = lax.ppermute(even_rows, "comp", even_pairs)
     odd_in = lax.ppermute(odd_rows, "comp", odd_pairs)
 
-    col_a, col_b = pl.pallas_call(
+    col_a, col_b = call(
         functools.partial(pack_columns, rows_a, rows_o),
+        1.2,
+        8 << 20,
         in_specs=[VMEM] * 5,
         out_specs=[VMEM, VMEM],
         out_shape=[jax.ShapeDtypeStruct((extra, lanes), BF16)] * 2,
@@ -356,40 +380,43 @@
             pltpu.VMEM((channels_a * rows_a + channels_o * rows_o, lanes), F32),
             pltpu.VMEM((2, extra, lanes), F32),
         ],
-        compiler_params=params(8 << 20),
         name="pack_columns",
     )(atm, ocean, rate, even_in, odd_in)
 
     sends = [jax.ShapeDtypeStruct((message + extra, lanes), BF16)] * 2
     sends += [jax.ShapeDtypeStruct((message, lanes), BF16)] * (tile_count - 3)
-    own_part, *parts = pl.pallas_call(
-        functools.partial(remap, tile_count, block),
-        in_specs=[SMEM] + [VMEM] * (3 + tile_count),
+    own_part, *parts = call(
+        functools.partial(remap, tile_count, rows_a, rows_o),
+        2.0,
+        12 << 20,
+        in_specs=[SMEM, SMEM] + [VMEM] * (3 + tile_count),
         out_specs=[VMEM] * tile_count,
         out_shape=[jax.ShapeDtypeStruct((block, SURF, lanes), F32)] + sends,
         scratch_shapes=[
             pltpu.VMEM((tile_count * block, SURF, lanes), BF16),
             pltpu.VMEM((tile_count * block, SURF, lanes), F32),
         ],
-        compiler_params=params(12 << 20),
         name="remap",
-    )(table, remap_weight[0], surface, col_a, col_b, *received)
-    returned = [lax.ppermute(part, "tile", route) for part, route in zip(parts, routes)]
-
-    atm_base, ocean_base = pl.pallas_call(
+    )(table, pair_count, remap_weight[0], surface, col_a, col_b, *received)
+    returned = exchange(parts, routes)
+
+    atm_base, ocean_base = call(
         functools.partial(stencil, rows_a, rows_o),
+        2.5,
+        8 << 20,
         in_specs=[VMEM] * 5,
         out_specs=[VMEM, VMEM],
         out_shape=[
             jax.ShapeDtypeStruct(atm.shape, F32),
             jax.ShapeDtypeStruct(ocean.shape, F32),
         ],
-        compiler_params=params(8 << 20),
         name="stencil",
     )(atm, ocean, rate, even_in, odd_in)
 
-    atm_next, ocean_next = pl.pallas_call(
+    atm_next, ocean_next = call(
         functools.partial(final, tile_count, rows_a, rows_o),
+        2.0,
+        12 << 20,
         in_specs=[SMEM] + [VMEM] * (2 + tile_count),
         out_specs=[HBM, HBM],
         out_shape=[
@@ -402,7 +429,6 @@
             pltpu.VMEM(ocean.shape, F32),
             pltpu.SemaphoreType.DMA((channels // 8,)),
         ],
-        compiler_params=params(12 << 20),
         name="final",
     )(mask, atm_base, ocean_base, own_part, *returned)
     return (
@@ -413,7 +439,7 @@
 
 def solution(mesh):
     return jax.shard_map(
-        shards,
+        interval,
         mesh=mesh,
         in_specs=(
             P(None, "comp", "tile"),

time: 36.6 us -> 30 us (0.82)
  the two profiles are of different devices: /device:TPU:3 before, /device:TPU:0 now
where the time goes in v3:
time: 30 us; the launch traced here: 29.9 us
  waiting for transfers between devices  10.2 us (34%)
  starting transfers between devices  10 us (33%)
  Pallas kernels  8.26 us (28%)
  between operations  1.35 us (4%)
    ppermute x6, waiting for transfers between devices, exchange(): out.append(lax.ppermute(block, 'tile', route))  10.2 us
    ppermute x6, starting transfers between devices, exchange(): out.append(lax.ppermute(block, 'tile', route))  8.79 us
    pallas_call x1, Pallas kernels, interval(): call(functools.partial(stencil, rows_a, rows_o), 2.5, 8 << 20, in_specs=[...  2.43 us
    pallas_call x1, Pallas kernels, interval(): call(functools.partial(prepare, rows_a, rows_o), 1.5, 8 << 20, in_specs=[...  1.75 us
    pallas_call x1, Pallas kernels, interval(): call(functools.partial(final, tile_count, rows_a, rows_o), 2.0, 12 << 20,...  1.52 us
    pallas_call x1, Pallas kernels, interval(): call(functools.partial(remap, tile_count, rows_a, rows_o), 2.0, 12 << 20,...  1.47 us
    pallas_call x1, Pallas kernels, interval(): call(functools.partial(pack_columns, rows_a, rows_o), 1.2, 8 << 20, in_sp...  1.09 us
    ppermute x1, starting transfers between devices, interval(): odd_in = lax.ppermute(odd_rows, 'comp', odd_pairs)  0.65 us
  transfers between devices with their start and end apart: 8, of which 3 were waited for; matrix products, arithmetic and copies ran while one was open for 0% of the time, Pallas kernels for 12%

profile of v3, /device:TPU:0, one launch (start us, length us, event | category | flops | bytes accessed | tf_op | source)
XLA Modules:
  0.0 29.9 jit_solution(8674966263497690207)
XLA Ops:
  0.6 0.0 copy-start
  0.6 1.8 %prepare.1 = (f32[2048,128]{1,0:T(8,128)S(1)}, f32[768,128]{1,0:T(8,128)S(1)}, bf16[32,8,128]{2,1,0:T(8,128)(2,1)S(1)}, bf16[2,176,128]{2,1,0:T(8,128)(2,1)S(1)}...) custom-call(f32[2048,128]{1,0:T(8,128)} %bitcast.9, ...), custom_call_target="tpu_custom_call" | custom-call | bytes 4500000 | tf_op jit(solution)/shard_map/prepare/pallas_call | solution.py:331
  2.4 0.6 %collective-permute-start = (bf16[2,176,128]{2,1,0:T(8,128)(2,1)S(1)}, bf16[2,176,128]{2,1,0:T(8,128)(2,1)S(1)}, u32[]{:S(2)}, u32[]{:S(2)}) collective-permute-start(bf16[2,176,128]{2,1,0:T(8,128)(2,1)S(1)} %get-tuple-element.24), channel_id=1, source_target_pairs={{0,4},{4,0},{8,12},{12,8},{16,20},{20,16},{24,28},{28,24},{1,5},{5... | collective-permute-start | bytes 270344 | tf_op jit(solution)/shard_map/ppermute | solution.py:369
  3.0 0.7 %collective-permute-start.1 = (bf16[2,176,128]{2,1,0:T(8,128)(2,1)S(1)}, bf16[2,176,128]{2,1,0:T(8,128)(2,1)S(1)}, u32[]{:S(2)}, u32[]{:S(2)}) collective-permute-start(bf16[2,176,128]{2,1,0:T(8,128)(2,1)S(1)} %get-tuple-element.25), channel_id=1, source_target_pairs={{4,8},{12,16},{20,24},{8,4},{16,12},{24,20},{5,9},{13,17},{21,25},... | collective-permute-start | bytes 270344 | tf_op jit(solution)/shard_map/ppermute | solution.py:370
  3.6 2.6 %collective-permute-start.2 = (bf16[32,8,128]{2,1,0:T(8,128)(2,1)S(1)}, bf16[32,8,128]{2,1,0:T(8,128)(2,1)S(1)}, u32[]{:S(2)}, u32[]{:S(2)}) collective-permute-start(bf16[32,8,128]{2,1,0:T(8,128)(2,1)S(1)} %get-tuple-element.29.refs_3_), channel_id=1, source_target_pairs={{0,1},{1,0},{2,3},{3,2},{4,5},{5,4},{6,7},{7,6},{8,9},{9,8},{10,11... | collective-permute-start | bytes 196616 | tf_op jit(solution)/shard_map/ppermute | solution.py:302
  6.3 2.5 %collective-permute-start.3 = (bf16[32,8,128]{2,1,0:T(8,128)(2,1)S(1)}, bf16[32,8,128]{2,1,0:T(8,128)(2,1)S(1)}, u32[]{:S(2)}, u32[]{:S(2)}) collective-permute-start(bf16[32,8,128]{2,1,0:T(8,128)(2,1)S(1)} %get-tuple-element.29.refs_3_), channel_id=1, source_target_pairs={{0,3},{1,2},{2,1},{3,0},{4,7},{5,6},{6,5},{7,4},{8,11},{9,10},{10,... | collective-permute-start | bytes 196616 | tf_op jit(solution)/shard_map/ppermute | solution.py:302
  8.7 0.1 collective-permute-start.4
  9.5 0.0 collective-permute-done.even_in
  9.5 0.0 collective-permute-done.1.odd_in
  9.5 1.1 %pack_columns.1 = (bf16[48,128]{1,0:T(8,128)(2,1)S(1)}, bf16[48,128]{1,0:T(8,128)(2,1)S(1)}) custom-call(f32[2048,128]{1,0:T(8,128)S(1)} %get-tuple-element.21.atm, f32[768,128]{1,0:T(8,128)S(1)} %get-tuple-element.22.ocean, f32[176,128]{1,0:T(8,128)S(1)} %get-tuple-element.23.rate, bf16[2,176,128]{2,1,0:T(8,128)(2,1)S(1)} %collective-permute-done.even_in, ...), custom_call_target="tpu_custom_call" | custom-call | bytes 3600000 | tf_op jit(solution)/shard_map/pack_columns/pallas_call | solution.py:372
  10.6 0.0 collective-permute-done.2.refs_6_
  10.6 1.9 %collective-permute-done.3.refs_7_ = bf16[32,8,128]{2,1,0:T(8,128)(2,1)S(1)} collective-permute-done((bf16[32,8,128]{2,1,0:T(8,128)(2,1)S(1)}, bf16[32,8,128]{2,1,0:T(8,128)(2,1)S(1)}, u32[]{:S(2)}, u32[]{:S(2)}) %collective-permute-start.3) | collective-permute-done | bytes 65568 | tf_op jit(solution)/shard_map/ppermute | solution.py:302
  12.5 4.1 %collective-permute-done.4.refs_8_ = bf16[32,8,128]{2,1,0:T(8,128)(2,1)S(1)} collective-permute-done((bf16[32,8,128]{2,1,0:T(8,128)(2,1)S(1)}, bf16[32,8,128]{2,1,0:T(8,128)(2,1)S(1)}, u32[]{:S(2)}, u32[]{:S(2)}) %collective-permute-start.4) | collective-permute-done | bytes 65568 | tf_op jit(solution)/shard_map/ppermute | solution.py:302
  16.6 0.0 copy-done
  16.6 1.5 %remap.1 = (f32[32,8,128]{2,1,0:T(8,128)S(1)}, bf16[304,128]{1,0:T(8,128)(2,1)S(1)}, bf16[304,128]{1,0:T(8,128)(2,1)S(1)}, bf16[256,128]{1,0:T(8,128)(2,1)S(1)}) custom-call(s32[2,48]{1,0:T(2,128)S(4)} %get-tuple-element.28.refs_0_, s32[1,1]{1,0:T(1,128)S(6)} %copy.11.refs_1_, bf16[48,128,128]{2,1,0:T(8,128)(2,1)S(1)} %bitcast.8, ...), custom_call_target="tpu_custom_call" | custom-call | bytes 6000000 | tf_op jit(solution)/shard_map/remap/pallas_call | solution.py:388
  18.1 0.1 collective-permute-start.5
  18.2 1.9 %collective-permute-start.6 = (bf16[304,128]{1,0:T(8,128)(2,1)S(1)}, bf16[304,128]{1,0:T(8,128)(2,1)S(1)}, u32[]{:S(2)}, u32[]{:S(2)}) collective-permute-start(bf16[304,128]{1,0:T(8,128)(2,1)S(1)} %get-tuple-element.34), channel_id=1, source_target_pairs={{0,3},{1,2},{2,1},{3,0},{4,7},{5,6},{6,5},{7,4},{8,11},{9,10},{10,... | collective-permute-start | bytes 233480 | tf_op jit(solution)/shard_map/ppermute | solution.py:302
  20.0 1.6 %collective-permute-start.7 = (bf16[256,128]{1,0:T(8,128)(2,1)S(1)}, bf16[256,128]{1,0:T(8,128)(2,1)S(1)}, u32[]{:S(2)}, u32[]{:S(2)}) collective-permute-start(bf16[256,128]{1,0:T(8,128)(2,1)S(1)} %get-tuple-element.35), channel_id=1, source_target_pairs={{0,2},{1,3},{2,0},{3,1},{4,6},{5,7},{6,4},{7,5},{8,10},{9,11},{10,... | collective-permute-start | bytes 196616 | tf_op jit(solution)/shard_map/ppermute | solution.py:302
  21.6 2.4 %stencil.1 = (f32[2048,128]{1,0:T(8,128)S(1)}, f32[768,128]{1,0:T(8,128)S(1)}) custom-call(f32[2048,128]{1,0:T(8,128)S(1)} %get-tuple-element.21.atm, f32[768,128]{1,0:T(8,128)S(1)} %get-tuple-element.22.ocean, f32[176,128]{1,0:T(8,128)S(1)} %get-tuple-element.23.rate, bf16[2,176,128]{2,1,0:T(8,128)(2,1)S(1)} %collective-permute-done.even_in, ...), custom_call_target="tpu_custom_call" | custom-call | bytes 7500000 | tf_op jit(solution)/shard_map/stencil/pallas_call | solution.py:403
  24.1 4.3 %collective-permute-done.7.refs_6_ = bf16[256,128]{1,0:T(8,128)(2,1)S(1)} collective-permute-done((bf16[256,128]{1,0:T(8,128)(2,1)S(1)}, bf16[256,128]{1,0:T(8,128)(2,1)S(1)}, u32[]{:S(2)}, u32[]{:S(2)}) %collective-permute-start.7) | collective-permute-done | bytes 65568 | tf_op jit(solution)/shard_map/ppermute | solution.py:302
  28.3 0.0 collective-permute-done.5.refs_4_
  28.3 0.0 collective-permute-done.6.refs_5_
  28.3 1.5 %final.1 = (f32[2048,128]{1,0:T(8,128)}, f32[768,128]{1,0:T(8,128)}) custom-call(s32[1,16]{1,0:T(1,128)S(4)} %get-tuple-element.20.refs_0_, f32[2048,128]{1,0:T(8,128)S(1)} %get-tuple-element.26.refs_1_, f32[768,128]{1,0:T(8,128)S(1)} %get-tuple-element.27.refs_2_, f32[32,8,128]{2,1,0:T(8,128)S(1)} %get-tuple-element.32.refs_3_, ...), custom_call_target="tpu_custom_call" | custom-call | bytes 6000000 | tf_op jit(solution)/shard_map/final/pallas_call | solution.py:416
Async XLA Ops:
  0.6 16.0 %copy-start = (bf16[1,48,128,128]{3,2,1,0:T(8,128)(2,1)S(1)}, bf16[1,48,128,128]{3,2,1,0:T(8,128)(2,1)}, u32[]{:S(2)}) copy-start(bf16[1,48,128,128]{3,2,1,0:T(8,128)(2,1)} %param.14) | copy-start | bytes 4718596
  2.4 7.1 %collective-permute-start = (bf16[2,176,128]{2,1,0:T(8,128)(2,1)S(1)}, bf16[2,176,128]{2,1,0:T(8,128)(2,1)S(1)}, u32[]{:S(2)}, u32[]{:S(2)}) collective-permute-start(bf16[2,176,128]{2,1,0:T(8,128)(2,1)S(1)} %get-tuple-element.24), channel_id=1, source_target_pairs={{0,4},{4,0},{8,12},{12,8},{16,20},{20,16},{24,28},{28,24},{1,5},{5... | collective-permute-start | bytes 270344 | tf_op jit(solution)/shard_map/ppermute | solution.py:369
  3.0 6.6 %collective-permute-start.1 = (bf16[2,176,128]{2,1,0:T(8,128)(2,1)S(1)}, bf16[2,176,128]{2,1,0:T(8,128)(2,1)S(1)}, u32[]{:S(2)}, u32[]{:S(2)}) collective-permute-start(bf16[2,176,128]{2,1,0:T(8,128)(2,1)S(1)} %get-tuple-element.25), channel_id=1, source_target_pairs={{4,8},{12,16},{20,24},{8,4},{16,12},{24,20},{5,9},{13,17},{21,25},... | collective-permute-start | bytes 270344 | tf_op jit(solution)/shard_map/ppermute | solution.py:370
  3.6 7.0 %collective-permute-start.2 = (bf16[32,8,128]{2,1,0:T(8,128)(2,1)S(1)}, bf16[32,8,128]{2,1,0:T(8,128)(2,1)S(1)}, u32[]{:S(2)}, u32[]{:S(2)}) collective-permute-start(bf16[32,8,128]{2,1,0:T(8,128)(2,1)S(1)} %get-tuple-element.29.refs_3_), channel_id=1, source_target_pairs={{0,1},{1,0},{2,3},{3,2},{4,5},{5,4},{6,7},{7,6},{8,9},{9,8},{10,11... | collective-permute-start | bytes 196616 | tf_op jit(solution)/shard_map/ppermute | solution.py:302
  6.3 6.2 %collective-permute-start.3 = (bf16[32,8,128]{2,1,0:T(8,128)(2,1)S(1)}, bf16[32,8,128]{2,1,0:T(8,128)(2,1)S(1)}, u32[]{:S(2)}, u32[]{:S(2)}) collective-permute-start(bf16[32,8,128]{2,1,0:T(8,128)(2,1)S(1)} %get-tuple-element.29.refs_3_), channel_id=1, source_target_pairs={{0,3},{1,2},{2,1},{3,0},{4,7},{5,6},{6,5},{7,4},{8,11},{9,10},{10,... | collective-permute-start | bytes 196616 | tf_op jit(solution)/shard_map/ppermute | solution.py:302
  8.7 7.8 %collective-permute-start.4 = (bf16[32,8,128]{2,1,0:T(8,128)(2,1)S(1)}, bf16[32,8,128]{2,1,0:T(8,128)(2,1)S(1)}, u32[]{:S(2)}, u32[]{:S(2)}) collective-permute-start(bf16[32,8,128]{2,1,0:T(8,128)(2,1)S(1)} %get-tuple-element.29.refs_3_), channel_id=1, source_target_pairs={{0,2},{1,3},{2,0},{3,1},{4,6},{5,7},{6,4},{7,5},{8,10},{9,11},{10,... | collective-permute-start | bytes 196616 | tf_op jit(solution)/shard_map/ppermute | solution.py:302
  18.1 10.3 %collective-permute-start.5 = (bf16[304,128]{1,0:T(8,128)(2,1)S(1)}, bf16[304,128]{1,0:T(8,128)(2,1)S(1)}, u32[]{:S(2)}, u32[]{:S(2)}) collective-permute-start(bf16[304,128]{1,0:T(8,128)(2,1)S(1)} %get-tuple-element.33), channel_id=1, source_target_pairs={{0,1},{1,0},{2,3},{3,2},{4,5},{5,4},{6,7},{7,6},{8,9},{9,8},{10,11... | collective-permute-start | bytes 233480 | tf_op jit(solution)/shard_map/ppermute | solution.py:302
  18.2 10.2 %collective-permute-start.6 = (bf16[304,128]{1,0:T(8,128)(2,1)S(1)}, bf16[304,128]{1,0:T(8,128)(2,1)S(1)}, u32[]{:S(2)}, u32[]{:S(2)}) collective-permute-start(bf16[304,128]{1,0:T(8,128)(2,1)S(1)} %get-tuple-element.34), channel_id=1, source_target_pairs={{0,3},{1,2},{2,1},{3,0},{4,7},{5,6},{6,5},{7,4},{8,11},{9,10},{10,... | collective-permute-start | bytes 233480 | tf_op jit(solution)/shard_map/ppermute | solution.py:302
  20.0 8.3 %collective-permute-start.7 = (bf16[256,128]{1,0:T(8,128)(2,1)S(1)}, bf16[256,128]{1,0:T(8,128)(2,1)S(1)}, u32[]{:S(2)}, u32[]{:S(2)}) collective-permute-start(bf16[256,128]{1,0:T(8,128)(2,1)S(1)} %get-tuple-element.35), channel_id=1, source_target_pairs={{0,2},{1,3},{2,0},{3,1},{4,6},{5,7},{6,4},{7,5},{8,10},{9,11},{10,... | collective-permute-start | bytes 196616 | tf_op jit(solution)/shard_map/ppermute | solution.py:302

commit v4 on v3

--- a/solution.py
+++ b/solution.py
@@ -49,21 +49,11 @@
     return even, odd
 
 
-def prepare(rows_a, rows_o, *refs):
-    ins, outs = refs[:7], refs[7:15]
-    rate_a, rate_o, done = refs[15:]
-    atm_in, ocean_in, mask_in, src_in, tgt_in, rate_a_in, rate_o_in = ins
-    atm, ocean, surface, even_out, odd_out, rate, table, mask = outs
+def pack_surface(rows_a, rows_o, atm_in, ocean_in, mask_in, surface, mask, atm, ocean, done):
     copies = [
         (mask_in, mask),
-        (atm_in.at[0 : SURF * rows_a], atm.at[0 : SURF * rows_a]),
-        (ocean_in.at[0 : SURF * rows_o], ocean.at[0 : SURF * rows_o]),
-        (src_in, table.at[0:1]),
-        (tgt_in, table.at[1:2]),
-        (rate_a_in, rate_a),
-        (rate_o_in, rate_o),
-        (atm_in.at[SURF * rows_a :], atm.at[SURF * rows_a :]),
-        (ocean_in.at[SURF * rows_o :], ocean.at[SURF * rows_o :]),
+        (atm_in.at[0 : SURF * rows_a], atm),
+        (ocean_in.at[0 : SURF * rows_o], ocean),
     ]
     copies = [pltpu.make_async_copy(a, b, done.at[i]) for i, (a, b) in enumerate(copies)]
     for copy in copies:
@@ -76,7 +66,24 @@
     for y in range(rows_o):
         tile = ocean[pl.ds(y, SURF, stride=rows_o), :]
         surface[rows_a + y] = (tile * mask[0, y].astype(F32)).astype(BF16)
-    for copy in copies[3:]:
+
+
+def prepare(rows_a, rows_o, *refs):
+    atm_in, ocean_in, number, src_in, tgt_in, rate_a_in, rate_o_in = refs[:7]
+    atm, ocean, even_out, odd_out, rate, table, live, rate_a, rate_o, done = refs[7:]
+    live[0, 0] = number[0, 0]
+    copies = [
+        (atm_in, atm),
+        (ocean_in, ocean),
+        (rate_a_in, rate_a),
+        (rate_o_in, rate_o),
+        (src_in, table.at[0:1]),
+        (tgt_in, table.at[1:2]),
+    ]
+    copies = [pltpu.make_async_copy(a, b, done.at[i]) for i, (a, b) in enumerate(copies)]
+    for copy in copies:
+        copy.start()
+    for copy in copies[2:]:
         copy.wait()
     lanes = atm.shape[1]
     split = rate_a.shape[1]
@@ -84,7 +91,8 @@
     rate[split:, :] = jnp.broadcast_to(rate_o[...], (lanes, rate_o.shape[1])).T
     parity = lax.rem(lax.axis_index("comp"), 2)
     at = 0
-    for ref, rows in ((atm, rows_a), (ocean, rows_o)):
+    for copy, ref, rows in ((copies[0], atm, rows_a), (copies[1], ocean, rows_o)):
+        copy.wait()
         channels = ref.shape[0] // rows
         for c in range(0, channels, 8):
             for r in range(2):
@@ -103,7 +111,8 @@
     return north, south
 
 
-def pack_columns(rows_a, rows_o, atm, ocean, rate, even_in, odd_in, out_a, out_b, spread, stage):
+def pack_columns(rows_a, rows_o, atm, ocean, rate, even_in, odd_in, part_a, part_b, out_a, out_b, spread, stage):
+    del part_a, part_b
     parity = lax.rem(lax.axis_index("comp"), 2)
     tile_parity = lax.rem(lax.axis_index("tile"), 2)
     lanes = atm.shape[1]
@@ -140,16 +149,17 @@
         found = lax.dot_general(pick, part, dims, preferred_element_type=F32)
         stage[0, 2 * j : 2 * j + 2, :] = found[0:2, :]
         stage[1, 2 * j : 2 * j + 2, :] = found[2:4, :]
-    out_a[...] = stage[0].astype(BF16)
-    out_b[...] = stage[1].astype(BF16)
+    behind = out_a.shape[0] - stage.shape[1]
+    out_a[behind:, :] = stage[0].astype(BF16)
+    out_b[behind:, :] = stage[1].astype(BF16)
 
 
 def remap(tile_count, rows_a, rows_o, *refs):
-    table, number, weights, own, col_a, col_b = refs[:6]
-    got = refs[6 : 5 + tile_count]
-    own_out = refs[5 + tile_count]
-    outs = refs[6 + tile_count : 5 + 2 * tile_count]
-    band, total = refs[5 + 2 * tile_count :]
+    table, number, weights, own = refs[:4]
+    got = refs[4 : 3 + tile_count]
+    own_out = refs[3 + tile_count]
+    outs = refs[4 + tile_count : 3 + 2 * tile_count]
+    band, total = refs[3 + 2 * tile_count :]
     block = rows_a + rows_o
     me = lax.axis_index("tile")
     sources, targets = peers(me, tile_count)
@@ -186,8 +196,6 @@
     for e, ref in zip(targets, outs):
         part = total[pl.ds(e * block, block)].astype(BF16)
         ref[0 : block * SURF, :] = part.reshape(block * SURF, lanes)
-    for ref, col in zip(outs, (col_a, col_b)):
-        ref[block * SURF :, :] = col[...]
 
 
 def stencil(rows_a, rows_o, atm, ocean, rate, even_in, odd_in, atm_out, ocean_out):
@@ -327,61 +335,59 @@
     routes = tile_pairs(tile_count)
     even_pairs, odd_pairs = comp_pairs(lax.axis_size("comp"))
 
+    hbm = lambda x: pltpu.with_memory_space_constraint(x, pltpu.HBM)
+    surface, wet = call(
+        functools.partial(pack_surface, rows_a, rows_o),
+        0.8,
+        4 << 20,
+        in_specs=[HBM] * 3,
+        out_specs=[VMEM, SMEM],
+        out_shape=[
+            pltpu.VMEM((block, SURF, lanes), BF16),
+            pltpu.SMEM((1, rows_o), jnp.int32),
+        ],
+        scratch_shapes=[
+            pltpu.VMEM((SURF * rows_a, lanes), F32),
+            pltpu.VMEM((SURF * rows_o, lanes), F32),
+            pltpu.SemaphoreType.DMA((3,)),
+        ],
+        name="pack_surface",
+    )(hbm(atm), hbm(ocean), hbm(mask))
+    received = exchange([surface] * len(routes), routes)
+
     halo = pltpu.VMEM((2, channels, lanes), BF16)
-    atm, ocean, surface, even_rows, odd_rows, rate, table, mask = call(
+    atm, ocean, even_rows, odd_rows, rate, table, live = call(
         functools.partial(prepare, rows_a, rows_o),
         1.5,
         8 << 20,
-        in_specs=[HBM] * 7,
-        out_specs=[VMEM] * 6 + [SMEM] * 2,
+        in_specs=[HBM, HBM, SMEM] + [HBM] * 4,
+        out_specs=[VMEM] * 5 + [SMEM] * 2,
         out_shape=[
             pltpu.VMEM(atm.shape, F32),
             pltpu.VMEM(ocean.shape, F32),
-            pltpu.VMEM((block, SURF, lanes), BF16),
             halo,
             halo,
             pltpu.VMEM((channels, lanes), F32),
             pltpu.SMEM((2, pair_src.shape[1]), jnp.int32),
-            pltpu.SMEM((1, rows_o), jnp.int32),
+            pltpu.SMEM((1, pair_src.shape[1]), jnp.int32),
         ],
         scratch_shapes=[
             pltpu.VMEM((1, channels_a), F32),
             pltpu.VMEM((1, channels_o), F32),
-            pltpu.SemaphoreType.DMA((9,)),
+            pltpu.SemaphoreType.DMA((6,)),
         ],
         name="prepare",
     )(
-        *[
-            pltpu.with_memory_space_constraint(x, pltpu.HBM)
-            for x in (
-                atm,
-                ocean,
-                mask,
-                pair_src,
-                pair_tgt,
-                atm_rate.reshape(1, channels_a),
-                ocean_rate.reshape(1, channels_o),
-            )
-        ]
+        hbm(atm),
+        hbm(ocean),
+        pair_count,
+        hbm(pair_src),
+        hbm(pair_tgt),
+        hbm(atm_rate.reshape(1, channels_a)),
+        hbm(ocean_rate.reshape(1, channels_o)),
     )
-    received = exchange([surface] * len(routes), routes)
-
     even_in = lax.ppermute(even_rows, "comp", even_pairs)
     odd_in = lax.ppermute(odd_rows, "comp", odd_pairs)
-
-    col_a, col_b = call(
-        functools.partial(pack_columns, rows_a, rows_o),
-        1.2,
-        8 << 20,
-        in_specs=[VMEM] * 5,
-        out_specs=[VMEM, VMEM],
-        out_shape=[jax.ShapeDtypeStruct((extra, lanes), BF16)] * 2,
-        scratch_shapes=[
-            pltpu.VMEM((channels_a * rows_a + channels_o * rows_o, lanes), F32),
-            pltpu.VMEM((2, extra, lanes), F32),
-        ],
-        name="pack_columns",
-    )(atm, ocean, rate, even_in, odd_in)
 
     sends = [jax.ShapeDtypeStruct((message + extra, lanes), BF16)] * 2
     sends += [jax.ShapeDtypeStruct((message, lanes), BF16)] * (tile_count - 3)
@@ -389,7 +395,7 @@
         functools.partial(remap, tile_count, rows_a, rows_o),
         2.0,
         12 << 20,
-        in_specs=[SMEM, SMEM] + [VMEM] * (3 + tile_count),
+        in_specs=[SMEM, SMEM] + [VMEM] * (1 + tile_count),
         out_specs=[VMEM] * tile_count,
         out_shape=[jax.ShapeDtypeStruct((block, SURF, lanes), F32)] + sends,
         scratch_shapes=[
@@ -397,7 +403,21 @@
             pltpu.VMEM((tile_count * block, SURF, lanes), F32),
         ],
         name="remap",
-    )(table, pair_count, remap_weight[0], surface, col_a, col_b, *received)
+    )(table, live, remap_weight[0], surface, *received)
+    parts[:2] = call(
+        functools.partial(pack_columns, rows_a, rows_o),
+        1.2,
+        8 << 20,
+        in_specs=[VMEM] * 7,
+        out_specs=[VMEM, VMEM],
+        out_shape=sends[:2],
+        input_output_aliases={5: 0, 6: 1},
+        scratch_shapes=[
+            pltpu.VMEM((channels_a * rows_a + channels_o * rows_o, lanes), F32),
+            pltpu.VMEM((2, extra, lanes), F32),
+        ],
+        name="pack_columns",
+    )(atm, ocean, rate, even_in, odd_in, *parts[:2])
     returned = exchange(parts, routes)
 
     atm_base, ocean_base = call(
@@ -430,7 +450,7 @@
             pltpu.SemaphoreType.DMA((channels // 8,)),
         ],
         name="final",
-    )(mask, atm_base, ocean_base, own_part, *returned)
+    )(wet, atm_base, ocean_base, own_part, *returned)
     return (
         atm_next.reshape(channels_a, rows_a, lanes),
         ocean_next.reshape(channels_o, rows_o, lanes),

time: 30 us -> 32 us (1.067)
  the two profiles are of different devices: /device:TPU:0 before, /device:TPU:3 now
where the time goes in v4:
time: 32 us; the launch traced here: 31.8 us
  starting transfers between devices  12 us (38%)
  waiting for transfers between devices  9.48 us (30%)
  Pallas kernels  8.87 us (28%)
  between operations  1.47 us (5%)
    ppermute x6, waiting for transfers between devices, exchange(): out.append(lax.ppermute(block, 'tile', route))  9.48 us
    ppermute x6, starting transfers between devices, exchange(): out.append(lax.ppermute(block, 'tile', route))  8.21 us
    ppermute x1, starting transfers between devices, interval(): odd_in = lax.ppermute(odd_rows, 'comp', odd_pairs)  3.02 us
    pallas_call x1, Pallas kernels, interval(): call(functools.partial(stencil, rows_a, rows_o), 2.5, 8 << 20, in_specs=[...  2.44 us
    pallas_call x1, Pallas kernels, interval(): call(functools.partial(final, tile_count, rows_a, rows_o), 2.0, 12 << 20,...  1.52 us
    pallas_call x1, Pallas kernels, interval(): call(functools.partial(remap, tile_count, rows_a, rows_o), 2.0, 12 << 20,...  1.47 us
    pallas_call x1, Pallas kernels, interval(): call(functools.partial(prepare, rows_a, rows_o), 1.5, 8 << 20, in_specs=[...  1.41 us
    pallas_call x1, Pallas kernels, interval(): call(functools.partial(pack_columns, rows_a, rows_o), 1.2, 8 << 20, in_sp...  1.1 us
  transfers between devices with their start and end apart: 8, of which 4 were waited for; matrix products, arithmetic and copies ran while one was open for 0% of the time, Pallas kernels for 15%

profile of v4, /device:TPU:3, one launch (start us, length us, event | category | flops | bytes accessed | tf_op | source)
XLA Modules:
  0.0 31.8 jit_solution(13961493603190262116)
XLA Ops:
  0.6 0.0 copy-start
  1.4 1.4 %prepare.1 = (f32[2048,128]{1,0:T(8,128)S(1)}, f32[768,128]{1,0:T(8,128)S(1)}, bf16[2,176,128]{2,1,0:T(8,128)(2,1)S(1)}, bf16[2,176,128]{2,1,0:T(8,128)(2,1)S(1)...) custom-call(f32[2048,128]{1,0:T(8,128)} %bitcast.9, f32[768,128]{1,0:T(8,128)} %bitcast.11, ...), custom_call_target="tpu_custom_call" | custom-call | bytes 4500000 | tf_op jit(solution)/shard_map/prepare/pallas_call | solution.py:359
  2.8 0.7 %collective-permute-start = (bf16[2,176,128]{2,1,0:T(8,128)(2,1)S(1)}, bf16[2,176,128]{2,1,0:T(8,128)(2,1)S(1)}, u32[]{:S(2)}, u32[]{:S(2)}) collective-permute-start(bf16[2,176,128]{2,1,0:T(8,128)(2,1)S(1)} %get-tuple-element.25), channel_id=1, source_target_pairs={{0,4},{4,0},{8,12},{12,8},{16,20},{20,16},{24,28},{28,24},{1,5},{5... | collective-permute-start | bytes 270344 | tf_op jit(solution)/shard_map/ppermute | solution.py:389
  3.6 3.0 %collective-permute-start.1 = (bf16[2,176,128]{2,1,0:T(8,128)(2,1)S(1)}, bf16[2,176,128]{2,1,0:T(8,128)(2,1)S(1)}, u32[]{:S(2)}, u32[]{:S(2)}) collective-permute-start(bf16[2,176,128]{2,1,0:T(8,128)(2,1)S(1)} %get-tuple-element.26), channel_id=1, source_target_pairs={{4,8},{12,16},{20,24},{8,4},{16,12},{24,20},{5,9},{13,17},{21,25},... | collective-permute-start | bytes 270344 | tf_op jit(solution)/shard_map/ppermute | solution.py:390
  6.6 0.9 %pack_surface.1 = (bf16[32,8,128]{2,1,0:T(8,128)(2,1)S(1)}, s32[1,16]{1,0:T(1,128)S(4)}) custom-call(f32[2048,128]{1,0:T(8,128)} %bitcast.10, f32[768,128]{1,0:T(8,128)} %bitcast.12, s32[1,16]{1,0:T(1,128)} %bitcast.15), custom_call_target="tpu_custom_call" | custom-call | bytes 2400000 | tf_op jit(solution)/shard_map/pack_surface/pallas_call | solution.py:339
  7.5 2.4 %collective-permute-start.4 = (bf16[32,8,128]{2,1,0:T(8,128)(2,1)S(1)}, bf16[32,8,128]{2,1,0:T(8,128)(2,1)S(1)}, u32[]{:S(2)}, u32[]{:S(2)}) collective-permute-start(bf16[32,8,128]{2,1,0:T(8,128)(2,1)S(1)} %get-tuple-element.31.refs_3_), channel_id=1, source_target_pairs={{0,2},{1,3},{2,0},{3,1},{4,6},{5,7},{6,4},{7,5},{8,10},{9,11},{10,... | collective-permute-start | bytes 196616 | tf_op jit(solution)/shard_map/ppermute | solution.py:310
  9.9 1.1 %collective-permute-start.3 = (bf16[32,8,128]{2,1,0:T(8,128)(2,1)S(1)}, bf16[32,8,128]{2,1,0:T(8,128)(2,1)S(1)}, u32[]{:S(2)}, u32[]{:S(2)}) collective-permute-start(bf16[32,8,128]{2,1,0:T(8,128)(2,1)S(1)} %get-tuple-element.31.refs_3_), channel_id=1, source_target_pairs={{0,3},{1,2},{2,1},{3,0},{4,7},{5,6},{6,5},{7,4},{8,11},{9,10},{10,... | collective-permute-start | bytes 196616 | tf_op jit(solution)/shard_map/ppermute | solution.py:310
  11.0 0.2 collective-permute-start.2
  11.2 0.8 %collective-permute-done.4.refs_6_ = bf16[32,8,128]{2,1,0:T(8,128)(2,1)S(1)} collective-permute-done((bf16[32,8,128]{2,1,0:T(8,128)(2,1)S(1)}, bf16[32,8,128]{2,1,0:T(8,128)(2,1)S(1)}, u32[]{:S(2)}, u32[]{:S(2)}) %collective-permute-start.4) | collective-permute-done | bytes 65568 | tf_op jit(solution)/shard_map/ppermute | solution.py:310
  12.0 3.6 %collective-permute-done.3.refs_5_ = bf16[32,8,128]{2,1,0:T(8,128)(2,1)S(1)} collective-permute-done((bf16[32,8,128]{2,1,0:T(8,128)(2,1)S(1)}, bf16[32,8,128]{2,1,0:T(8,128)(2,1)S(1)}, u32[]{:S(2)}, u32[]{:S(2)}) %collective-permute-start.3) | collective-permute-done | bytes 65568 | tf_op jit(solution)/shard_map/ppermute | solution.py:310
  15.6 0.2 collective-permute-done.2.refs_4_
  15.8 0.0 copy-done
  15.8 1.5 %remap.1 = (f32[32,8,128]{2,1,0:T(8,128)S(1)}, bf16[304,128]{1,0:T(8,128)(2,1)S(1)}, bf16[304,128]{1,0:T(8,128)(2,1)S(1)}, bf16[256,128]{1,0:T(8,128)(2,1)S(1)}) custom-call(s32[2,48]{1,0:T(2,128)S(4)} %get-tuple-element.29.refs_0_, s32[1,48]{1,0:T(1,128)S(4)} %get-tuple-element.30.refs_1_, bf16[48,128,128]{2,1,0:T(8,128)(2,1)S(1)} %bitcast.8, ...), custom_call_target="tpu_custom_call" | custom-call | bytes 6000000 | tf_op jit(solution)/shard_map/remap/pallas_call | solution.py:394
  17.3 0.0 collective-permute-done.even_in
  17.3 0.0 collective-permute-done.1.odd_in
  17.3 1.1 %pack_columns.1 = (bf16[304,128]{1,0:T(8,128)(2,1)S(1)}, bf16[304,128]{1,0:T(8,128)(2,1)S(1)}) custom-call(f32[2048,128]{1,0:T(8,128)S(1)} %get-tuple-element.22.atm, f32[768,128]{1,0:T(8,128)S(1)} %get-tuple-element.23.ocean, f32[176,128]{1,0:T(8,128)S(1)} %get-tuple-element.24.rate, ...), custom_call_target="tpu_custom_call", output_to_operand_aliasing={{0}: (5, {}), {1}: (6, {})} | custom-call | bytes 3600000 | tf_op jit(solution)/shard_map/pack_columns/pallas_call | solution.py:407
  18.4 1.4 %collective-permute-start.5 = (bf16[304,128]{1,0:T(8,128)(2,1)S(1)}, bf16[304,128]{1,0:T(8,128)(2,1)S(1)}, u32[]{:S(2)}, u32[]{:S(2)}) collective-permute-start(bf16[304,128]{1,0:T(8,128)(2,1)S(1)} %get-tuple-element.35), channel_id=1, source_target_pairs={{0,1},{1,0},{2,3},{3,2},{4,5},{5,4},{6,7},{7,6},{8,9},{9,8},{10,11... | collective-permute-start | bytes 233480 | tf_op jit(solution)/shard_map/ppermute | solution.py:310
  19.9 3.1 %collective-permute-start.6 = (bf16[304,128]{1,0:T(8,128)(2,1)S(1)}, bf16[304,128]{1,0:T(8,128)(2,1)S(1)}, u32[]{:S(2)}, u32[]{:S(2)}) collective-permute-start(bf16[304,128]{1,0:T(8,128)(2,1)S(1)} %get-tuple-element.36), channel_id=1, source_target_pairs={{0,3},{1,2},{2,1},{3,0},{4,7},{5,6},{6,5},{7,4},{8,11},{9,10},{10,... | collective-permute-start | bytes 233480 | tf_op jit(solution)/shard_map/ppermute | solution.py:310
  23.0 0.0 collective-permute-start.7
  23.0 2.4 %stencil.1 = (f32[2048,128]{1,0:T(8,128)S(1)}, f32[768,128]{1,0:T(8,128)S(1)}) custom-call(f32[2048,128]{1,0:T(8,128)S(1)} %get-tuple-element.22.atm, f32[768,128]{1,0:T(8,128)S(1)} %get-tuple-element.23.ocean, f32[176,128]{1,0:T(8,128)S(1)} %get-tuple-element.24.rate, bf16[2,176,128]{2,1,0:T(8,128)(2,1)S(1)} %collective-permute-done.even_in, ...), custom_call_target="tpu_custom_call" | custom-call | bytes 7500000 | tf_op jit(solution)/shard_map/stencil/pallas_call | solution.py:423
  25.4 4.8 %collective-permute-done.7.refs_6_ = bf16[256,128]{1,0:T(8,128)(2,1)S(1)} collective-permute-done((bf16[256,128]{1,0:T(8,128)(2,1)S(1)}, bf16[256,128]{1,0:T(8,128)(2,1)S(1)}, u32[]{:S(2)}, u32[]{:S(2)}) %collective-permute-start.7) | collective-permute-done | bytes 65568 | tf_op jit(solution)/shard_map/ppermute | solution.py:310
  30.3 0.0 collective-permute-done.5.refs_4_
  30.3 0.0 collective-permute-done.6.refs_5_
  30.3 1.5 %final.1 = (f32[2048,128]{1,0:T(8,128)}, f32[768,128]{1,0:T(8,128)}) custom-call(s32[1,16]{1,0:T(1,128)S(4)} %get-tuple-element.21.refs_0_, f32[2048,128]{1,0:T(8,128)S(1)} %get-tuple-element.27.refs_1_, f32[768,128]{1,0:T(8,128)S(1)} %get-tuple-element.28.refs_2_, f32[32,8,128]{2,1,0:T(8,128)S(1)} %get-tuple-element.32.refs_3_, ...), custom_call_target="tpu_custom_call" | custom-call | bytes 6000000 | tf_op jit(solution)/shard_map/final/pallas_call | solution.py:436
Async XLA Ops:
  0.6 15.2 %copy-start = (bf16[1,48,128,128]{3,2,1,0:T(8,128)(2,1)S(1)}, bf16[1,48,128,128]{3,2,1,0:T(8,128)(2,1)}, u32[]{:S(2)}) copy-start(bf16[1,48,128,128]{3,2,1,0:T(8,128)(2,1)} %param.14) | copy-start | bytes 4718596
  2.8 14.5 %collective-permute-start = (bf16[2,176,128]{2,1,0:T(8,128)(2,1)S(1)}, bf16[2,176,128]{2,1,0:T(8,128)(2,1)S(1)}, u32[]{:S(2)}, u32[]{:S(2)}) collective-permute-start(bf16[2,176,128]{2,1,0:T(8,128)(2,1)S(1)} %get-tuple-element.25), channel_id=1, source_target_pairs={{0,4},{4,0},{8,12},{12,8},{16,20},{20,16},{24,28},{28,24},{1,5},{5... | collective-permute-start | bytes 270344 | tf_op jit(solution)/shard_map/ppermute | solution.py:389
  3.6 13.8 %collective-permute-start.1 = (bf16[2,176,128]{2,1,0:T(8,128)(2,1)S(1)}, bf16[2,176,128]{2,1,0:T(8,128)(2,1)S(1)}, u32[]{:S(2)}, u32[]{:S(2)}) collective-permute-start(bf16[2,176,128]{2,1,0:T(8,128)(2,1)S(1)} %get-tuple-element.26), channel_id=1, source_target_pairs={{4,8},{12,16},{20,24},{8,4},{16,12},{24,20},{5,9},{13,17},{21,25},... | collective-permute-start | bytes 270344 | tf_op jit(solution)/shard_map/ppermute | solution.py:390
  7.5 4.5 %collective-permute-start.4 = (bf16[32,8,128]{2,1,0:T(8,128)(2,1)S(1)}, bf16[32,8,128]{2,1,0:T(8,128)(2,1)S(1)}, u32[]{:S(2)}, u32[]{:S(2)}) collective-permute-start(bf16[32,8,128]{2,1,0:T(8,128)(2,1)S(1)} %get-tuple-element.31.refs_3_), channel_id=1, source_target_pairs={{0,2},{1,3},{2,0},{3,1},{4,6},{5,7},{6,4},{7,5},{8,10},{9,11},{10,... | collective-permute-start | bytes 196616 | tf_op jit(solution)/shard_map/ppermute | solution.py:310
  9.9 5.7 %collective-permute-start.3 = (bf16[32,8,128]{2,1,0:T(8,128)(2,1)S(1)}, bf16[32,8,128]{2,1,0:T(8,128)(2,1)S(1)}, u32[]{:S(2)}, u32[]{:S(2)}) collective-permute-start(bf16[32,8,128]{2,1,0:T(8,128)(2,1)S(1)} %get-tuple-element.31.refs_3_), channel_id=1, source_target_pairs={{0,3},{1,2},{2,1},{3,0},{4,7},{5,6},{6,5},{7,4},{8,11},{9,10},{10,... | collective-permute-start | bytes 196616 | tf_op jit(solution)/shard_map/ppermute | solution.py:310
  11.0 4.8 %collective-permute-start.2 = (bf16[32,8,128]{2,1,0:T(8,128)(2,1)S(1)}, bf16[32,8,128]{2,1,0:T(8,128)(2,1)S(1)}, u32[]{:S(2)}, u32[]{:S(2)}) collective-permute-start(bf16[32,8,128]{2,1,0:T(8,128)(2,1)S(1)} %get-tuple-element.31.refs_3_), channel_id=1, source_target_pairs={{0,1},{1,0},{2,3},{3,2},{4,5},{5,4},{6,7},{7,6},{8,9},{9,8},{10,11... | collective-permute-start | bytes 196616 | tf_op jit(solution)/shard_map/ppermute | solution.py:310
  18.4 11.8 %collective-permute-start.5 = (bf16[304,128]{1,0:T(8,128)(2,1)S(1)}, bf16[304,128]{1,0:T(8,128)(2,1)S(1)}, u32[]{:S(2)}, u32[]{:S(2)}) collective-permute-start(bf16[304,128]{1,0:T(8,128)(2,1)S(1)} %get-tuple-element.35), channel_id=1, source_target_pairs={{0,1},{1,0},{2,3},{3,2},{4,5},{5,4},{6,7},{7,6},{8,9},{9,8},{10,11... | collective-permute-start | bytes 233480 | tf_op jit(solution)/shard_map/ppermute | solution.py:310
  19.9 10.4 %collective-permute-start.6 = (bf16[304,128]{1,0:T(8,128)(2,1)S(1)}, bf16[304,128]{1,0:T(8,128)(2,1)S(1)}, u32[]{:S(2)}, u32[]{:S(2)}) collective-permute-start(bf16[304,128]{1,0:T(8,128)(2,1)S(1)} %get-tuple-element.36), channel_id=1, source_target_pairs={{0,3},{1,2},{2,1},{3,0},{4,7},{5,6},{6,5},{7,4},{8,11},{9,10},{10,... | collective-permute-start | bytes 233480 | tf_op jit(solution)/shard_map/ppermute | solution.py:310
  23.0 7.3 %collective-permute-start.7 = (bf16[256,128]{1,0:T(8,128)(2,1)S(1)}, bf16[256,128]{1,0:T(8,128)(2,1)S(1)}, u32[]{:S(2)}, u32[]{:S(2)}) collective-permute-start(bf16[256,128]{1,0:T(8,128)(2,1)S(1)} %get-tuple-element.37), channel_id=1, source_target_pairs={{0,2},{1,3},{2,0},{3,1},{4,6},{5,7},{6,4},{7,5},{8,10},{9,11},{10,... | collective-permute-start | bytes 196616 | tf_op jit(solution)/shard_map/ppermute | solution.py:310

commit v5 on v4

--- a/solution.py
+++ b/solution.py
@@ -49,11 +49,17 @@
     return even, odd
 
 
-def pack_surface(rows_a, rows_o, atm_in, ocean_in, mask_in, surface, mask, atm, ocean, done):
+def pack_surface(rows_a, rows_o, *refs):
+    atm_in, ocean_in, mask_in, src_in, tgt_in, rate_a_in, rate_o_in = refs[:7]
+    surface, rate_a, rate_o, table, mask, atm, ocean, done = refs[7:]
     copies = [
         (mask_in, mask),
         (atm_in.at[0 : SURF * rows_a], atm),
         (ocean_in.at[0 : SURF * rows_o], ocean),
+        (src_in, table.at[0:1]),
+        (tgt_in, table.at[1:2]),
+        (rate_a_in, rate_a),
+        (rate_o_in, rate_o),
     ]
     copies = [pltpu.make_async_copy(a, b, done.at[i]) for i, (a, b) in enumerate(copies)]
     for copy in copies:
@@ -66,33 +72,17 @@
     for y in range(rows_o):
         tile = ocean[pl.ds(y, SURF, stride=rows_o), :]
         surface[rows_a + y] = (tile * mask[0, y].astype(F32)).astype(BF16)
+    for copy in copies[3:]:
+        copy.wait()
 
 
 def prepare(rows_a, rows_o, *refs):
-    atm_in, ocean_in, number, src_in, tgt_in, rate_a_in, rate_o_in = refs[:7]
-    atm, ocean, even_out, odd_out, rate, table, live, rate_a, rate_o, done = refs[7:]
+    atm, ocean, number, _, rate_a, rate_o = refs[:6]
+    even_out, odd_out, rate, live = refs[6:]
     live[0, 0] = number[0, 0]
-    copies = [
-        (atm_in, atm),
-        (ocean_in, ocean),
-        (rate_a_in, rate_a),
-        (rate_o_in, rate_o),
-        (src_in, table.at[0:1]),
-        (tgt_in, table.at[1:2]),
-    ]
-    copies = [pltpu.make_async_copy(a, b, done.at[i]) for i, (a, b) in enumerate(copies)]
-    for copy in copies:
-        copy.start()
-    for copy in copies[2:]:
-        copy.wait()
-    lanes = atm.shape[1]
-    split = rate_a.shape[1]
-    rate[0:split, :] = jnp.broadcast_to(rate_a[...], (lanes, split)).T
-    rate[split:, :] = jnp.broadcast_to(rate_o[...], (lanes, rate_o.shape[1])).T
     parity = lax.rem(lax.axis_index("comp"), 2)
     at = 0
-    for copy, ref, rows in ((copies[0], atm, rows_a), (copies[1], ocean, rows_o)):
-        copy.wait()
+    for ref, rows in ((atm, rows_a), (ocean, rows_o)):
         channels = ref.shape[0] // rows
         for c in range(0, channels, 8):
             for r in range(2):
@@ -101,6 +91,10 @@
                 even_out[r, at + c : at + c + 8, :] = jnp.where(parity == 0, high, low).astype(BF16)
                 odd_out[r, at + c : at + c + 8, :] = jnp.where(parity == 0, low, high).astype(BF16)
         at += channels
+    lanes = atm.shape[1]
+    split = rate_a.shape[1]
+    rate[0:split, :] = jnp.broadcast_to(rate_a[...], (lanes, split)).T
+    rate[split:, :] = jnp.broadcast_to(rate_o[...], (lanes, rate_o.shape[1])).T
 
 
 def halo_rows(parity, even_in, odd_in, at):
@@ -336,56 +330,51 @@
     even_pairs, odd_pairs = comp_pairs(lax.axis_size("comp"))
 
     hbm = lambda x: pltpu.with_memory_space_constraint(x, pltpu.HBM)
-    surface, wet = call(
+    surface, rate_a, rate_o, table, wet = call(
         functools.partial(pack_surface, rows_a, rows_o),
         0.8,
         4 << 20,
-        in_specs=[HBM] * 3,
-        out_specs=[VMEM, SMEM],
+        in_specs=[HBM] * 7,
+        out_specs=[VMEM] * 3 + [SMEM] * 2,
         out_shape=[
             pltpu.VMEM((block, SURF, lanes), BF16),
+            pltpu.VMEM((1, channels_a), F32),
+            pltpu.VMEM((1, channels_o), F32),
+            pltpu.SMEM((2, pair_src.shape[1]), jnp.int32),
             pltpu.SMEM((1, rows_o), jnp.int32),
         ],
         scratch_shapes=[
             pltpu.VMEM((SURF * rows_a, lanes), F32),
             pltpu.VMEM((SURF * rows_o, lanes), F32),
-            pltpu.SemaphoreType.DMA((3,)),
+            pltpu.SemaphoreType.DMA((7,)),
         ],
         name="pack_surface",
-    )(hbm(atm), hbm(ocean), hbm(mask))
-    received = exchange([surface] * len(routes), routes)
-
-    halo = pltpu.VMEM((2, channels, lanes), BF16)
-    atm, ocean, even_rows, odd_rows, rate, table, live = call(
-        functools.partial(prepare, rows_a, rows_o),
-        1.5,
-        8 << 20,
-        in_specs=[HBM, HBM, SMEM] + [HBM] * 4,
-        out_specs=[VMEM] * 5 + [SMEM] * 2,
-        out_shape=[
-            pltpu.VMEM(atm.shape, F32),
-            pltpu.VMEM(ocean.shape, F32),
-            halo,
-            halo,
-            pltpu.VMEM((channels, lanes), F32),
-            pltpu.SMEM((2, pair_src.shape[1]), jnp.int32),
-            pltpu.SMEM((1, pair_src.shape[1]), jnp.int32),
-        ],
-        scratch_shapes=[
-            pltpu.VMEM((1, channels_a), F32),
-            pltpu.VMEM((1, channels_o), F32),
-            pltpu.SemaphoreType.DMA((6,)),
-        ],
-        name="prepare",
     )(
         hbm(atm),
         hbm(ocean),
-        pair_count,
+        hbm(mask),
         hbm(pair_src),
         hbm(pair_tgt),
         hbm(atm_rate.reshape(1, channels_a)),
         hbm(ocean_rate.reshape(1, channels_o)),
     )
+    received = exchange([surface] * len(routes), routes)
+
+    halo = pltpu.VMEM((2, channels, lanes), BF16)
+    even_rows, odd_rows, rate, live = call(
+        functools.partial(prepare, rows_a, rows_o),
+        0.5,
+        4 << 20,
+        in_specs=[VMEM, VMEM, SMEM, HBM, VMEM, VMEM],
+        out_specs=[VMEM] * 3 + [SMEM],
+        out_shape=[
+            halo,
+            halo,
+            pltpu.VMEM((channels, lanes), F32),
+            pltpu.SMEM((1, pair_src.shape[1]), jnp.int32),
+        ],
+        name="prepare",
+    )(atm, ocean, pair_count, hbm(remap_weight[0]), rate_a, rate_o)
     even_in = lax.ppermute(even_rows, "comp", even_pairs)
     odd_in = lax.ppermute(odd_rows, "comp", odd_pairs)
 

time: 32 us -> 30.8 us (0.963)
  Pallas kernels: 8.87 us -> 7.65 us
    pallas_call x1, Pallas kernels: 1.41 us -> 0.13 us  [interval(): call(functools.partial(prepare, rows_a, rows_o), 0.5, 4 << 20, in_specs=[...]
    ppermute x6, starting transfers between devices: 8.21 us -> 7.79 us  [exchange(): out.append(lax.ppermute(block, 'tile', route))]
  transfers between devices with their start and end apart: 8 -> 8, of which waited for: 4 -> 4; matrix products, arithmetic and copies ran while one was open for 0% -> 0% of each run, Pallas kernels for 15% -> 13%
where the time goes in v5:
time: 30.8 us; the launch traced here: 30.6 us
  starting transfers between devices  11.7 us (38%)
  waiting for transfers between devices  9.78 us (32%)
  Pallas kernels  7.65 us (25%)
  between operations  1.49 us (5%)
    ppermute x6, waiting for transfers between devices, exchange(): out.append(lax.ppermute(block, 'tile', route))  9.77 us
    ppermute x6, starting transfers between devices, exchange(): out.append(lax.ppermute(block, 'tile', route))  7.79 us
    ppermute x1, starting transfers between devices, interval(): odd_in = lax.ppermute(odd_rows, 'comp', odd_pairs)  3.15 us
    pallas_call x1, Pallas kernels, interval(): call(functools.partial(stencil, rows_a, rows_o), 2.5, 8 << 20, in_specs=[...  2.44 us
    pallas_call x1, Pallas kernels, interval(): call(functools.partial(final, tile_count, rows_a, rows_o), 2.0, 12 << 20,...  1.52 us
    pallas_call x1, Pallas kernels, interval(): call(functools.partial(remap, tile_count, rows_a, rows_o), 2.0, 12 << 20,...  1.47 us
    pallas_call x1, Pallas kernels, interval(): call(functools.partial(pack_columns, rows_a, rows_o), 1.2, 8 << 20, in_sp...  1.1 us
    pallas_call x1, Pallas kernels, interval(): call(functools.partial(pack_surface, rows_a, rows_o), 0.8, 4 << 20, in_sp...  0.98 us
  transfers between devices with their start and end apart: 8, of which 4 were waited for; matrix products, arithmetic and copies ran while one was open for 0% of the time, Pallas kernels for 13%

profile of v5, /device:TPU:3, one launch (start us, length us, event | category | flops | bytes accessed | tf_op | source)
XLA Modules:
  0.0 30.6 jit_solution(6768512370616480251)
XLA Ops:
  0.6 0.0 copy-start.2
  0.6 0.0 copy-start
  1.4 1.0 %pack_surface.1 = (bf16[32,8,128]{2,1,0:T(8,128)(2,1)S(1)}, f32[1,128]{1,0:T(1,128)S(1)}, f32[1,48]{1,0:T(1,128)S(1)}, s32[2,48]{1,0:T(2,128)S(4)}, s32[1,16]{1,0:T(1,128)S(4)}) custom-call(f32[2048,128]{1,0:T(8,128)} %bitcast.8, f32[768,128]{1,0:T(8,128)} %bitcast.14, s32[1,16]{1,0:T(1,128)} %bitcast.18, s32[1,48]{1,0:T(1,128)} %refs_3_.1, ...), custom_call_target="tpu_custom_call" | custom-call | bytes 2400000 | tf_op jit(solution)/shard_map/pack_surface/pallas_call | solution.py:333
  2.4 0.0 copy-start.1
  2.4 0.0 copy-done.2
  2.4 0.0 copy-done
  2.4 0.1 prepare.1
  2.6 0.7 %collective-permute-start = (bf16[2,176,128]{2,1,0:T(8,128)(2,1)S(1)}, bf16[2,176,128]{2,1,0:T(8,128)(2,1)S(1)}, u32[]{:S(2)}, u32[]{:S(2)}) collective-permute-start(bf16[2,176,128]{2,1,0:T(8,128)(2,1)S(1)} %get-tuple-element.25), channel_id=1, source_target_pairs={{0,4},{4,0},{8,12},{12,8},{16,20},{20,16},{24,28},{28,24},{1,5},{5... | collective-permute-start | bytes 270344 | tf_op jit(solution)/shard_map/ppermute | solution.py:378
  3.3 3.1 %collective-permute-start.1 = (bf16[2,176,128]{2,1,0:T(8,128)(2,1)S(1)}, bf16[2,176,128]{2,1,0:T(8,128)(2,1)S(1)}, u32[]{:S(2)}, u32[]{:S(2)}) collective-permute-start(bf16[2,176,128]{2,1,0:T(8,128)(2,1)S(1)} %get-tuple-element.26), channel_id=1, source_target_pairs={{4,8},{12,16},{20,24},{8,4},{16,12},{24,20},{5,9},{13,17},{21,25},... | collective-permute-start | bytes 270344 | tf_op jit(solution)/shard_map/ppermute | solution.py:379
  6.5 2.4 %collective-permute-start.4 = (bf16[32,8,128]{2,1,0:T(8,128)(2,1)S(1)}, bf16[32,8,128]{2,1,0:T(8,128)(2,1)S(1)}, u32[]{:S(2)}, u32[]{:S(2)}) collective-permute-start(bf16[32,8,128]{2,1,0:T(8,128)(2,1)S(1)} %get-tuple-element.31.refs_3_), channel_id=1, source_target_pairs={{0,2},{1,3},{2,0},{3,1},{4,6},{5,7},{6,4},{7,5},{8,10},{9,11},{10,... | collective-permute-start | bytes 196616 | tf_op jit(solution)/shard_map/ppermute | solution.py:304
  8.8 1.1 %collective-permute-start.3 = (bf16[32,8,128]{2,1,0:T(8,128)(2,1)S(1)}, bf16[32,8,128]{2,1,0:T(8,128)(2,1)S(1)}, u32[]{:S(2)}, u32[]{:S(2)}) collective-permute-start(bf16[32,8,128]{2,1,0:T(8,128)(2,1)S(1)} %get-tuple-element.31.refs_3_), channel_id=1, source_target_pairs={{0,3},{1,2},{2,1},{3,0},{4,7},{5,6},{6,5},{7,4},{8,11},{9,10},{10,... | collective-permute-start | bytes 196616 | tf_op jit(solution)/shard_map/ppermute | solution.py:304
  9.9 0.2 collective-permute-start.2
  10.1 0.6 %collective-permute-done.4.refs_6_ = bf16[32,8,128]{2,1,0:T(8,128)(2,1)S(1)} collective-permute-done((bf16[32,8,128]{2,1,0:T(8,128)(2,1)S(1)}, bf16[32,8,128]{2,1,0:T(8,128)(2,1)S(1)}, u32[]{:S(2)}, u32[]{:S(2)}) %collective-permute-start.4) | collective-permute-done | bytes 65568 | tf_op jit(solution)/shard_map/ppermute | solution.py:304
  10.8 3.9 %collective-permute-done.3.refs_5_ = bf16[32,8,128]{2,1,0:T(8,128)(2,1)S(1)} collective-permute-done((bf16[32,8,128]{2,1,0:T(8,128)(2,1)S(1)}, bf16[32,8,128]{2,1,0:T(8,128)(2,1)S(1)}, u32[]{:S(2)}, u32[]{:S(2)}) %collective-permute-start.3) | collective-permute-done | bytes 65568 | tf_op jit(solution)/shard_map/ppermute | solution.py:304
  14.7 0.4 %collective-permute-done.2.refs_4_ = bf16[32,8,128]{2,1,0:T(8,128)(2,1)S(1)} collective-permute-done((bf16[32,8,128]{2,1,0:T(8,128)(2,1)S(1)}, bf16[32,8,128]{2,1,0:T(8,128)(2,1)S(1)}, u32[]{:S(2)}, u32[]{:S(2)}) %collective-permute-start.2) | collective-permute-done | bytes 65568 | tf_op jit(solution)/shard_map/ppermute | solution.py:304
  15.1 0.0 copy-done.1
  15.1 1.5 %remap.1 = (f32[32,8,128]{2,1,0:T(8,128)S(1)}, bf16[304,128]{1,0:T(8,128)(2,1)S(1)}, bf16[304,128]{1,0:T(8,128)(2,1)S(1)}, bf16[256,128]{1,0:T(8,128)(2,1)S(1)}) custom-call(s32[2,48]{1,0:T(2,128)S(4)} %get-tuple-element.29.refs_0_, s32[1,48]{1,0:T(1,128)S(4)} %get-tuple-element.30.refs_1_, bf16[48,128,128]{2,1,0:T(8,128)(2,1)S(1)} %bitcast.13, ...), custom_call_target="tpu_custom_call" | custom-call | bytes 6000000 | tf_op jit(solution)/shard_map/remap/pallas_call | solution.py:383
  16.5 0.0 collective-permute-done.even_in
  16.6 0.0 collective-permute-done.1.odd_in
  16.6 1.1 %pack_columns.1 = (bf16[304,128]{1,0:T(8,128)(2,1)S(1)}, bf16[304,128]{1,0:T(8,128)(2,1)S(1)}) custom-call(f32[2048,128]{1,0:T(8,128)S(1)} %bitcast.10, f32[768,128]{1,0:T(8,128)S(1)} %bitcast.16, f32[176,128]{1,0:T(8,128)S(1)} %get-tuple-element.24.rate, ...), custom_call_target="tpu_custom_call", output_to_operand_aliasing={{0}: (5, {}), {1}: (6, {})} | custom-call | bytes 3600000 | tf_op jit(solution)/shard_map/pack_columns/pallas_call | solution.py:396
  17.7 1.0 %collective-permute-start.5 = (bf16[304,128]{1,0:T(8,128)(2,1)S(1)}, bf16[304,128]{1,0:T(8,128)(2,1)S(1)}, u32[]{:S(2)}, u32[]{:S(2)}) collective-permute-start(bf16[304,128]{1,0:T(8,128)(2,1)S(1)} %get-tuple-element.35), channel_id=1, source_target_pairs={{0,1},{1,0},{2,3},{3,2},{4,5},{5,4},{6,7},{7,6},{8,9},{9,8},{10,11... | collective-permute-start | bytes 233480 | tf_op jit(solution)/shard_map/ppermute | solution.py:304
  18.7 3.1 %collective-permute-start.6 = (bf16[304,128]{1,0:T(8,128)(2,1)S(1)}, bf16[304,128]{1,0:T(8,128)(2,1)S(1)}, u32[]{:S(2)}, u32[]{:S(2)}) collective-permute-start(bf16[304,128]{1,0:T(8,128)(2,1)S(1)} %get-tuple-element.36), channel_id=1, source_target_pairs={{0,3},{1,2},{2,1},{3,0},{4,7},{5,6},{6,5},{7,4},{8,11},{9,10},{10,... | collective-permute-start | bytes 233480 | tf_op jit(solution)/shard_map/ppermute | solution.py:304
  21.8 0.0 collective-permute-start.7
  21.8 2.4 %stencil.1 = (f32[2048,128]{1,0:T(8,128)S(1)}, f32[768,128]{1,0:T(8,128)S(1)}) custom-call(f32[2048,128]{1,0:T(8,128)S(1)} %bitcast.11, f32[768,128]{1,0:T(8,128)S(1)} %bitcast.17, f32[176,128]{1,0:T(8,128)S(1)} %get-tuple-element.24.rate, bf16[2,176,128]{2,1,0:T(8,128)(2,1)S(1)} %collective-permute-done.even_in, ...), custom_call_target="tpu_custom_call" | custom-call | bytes 7500000 | tf_op jit(solution)/shard_map/stencil/pallas_call | solution.py:412
  24.2 4.9 %collective-permute-done.7.refs_6_ = bf16[256,128]{1,0:T(8,128)(2,1)S(1)} collective-permute-done((bf16[256,128]{1,0:T(8,128)(2,1)S(1)}, bf16[256,128]{1,0:T(8,128)(2,1)S(1)}, u32[]{:S(2)}, u32[]{:S(2)}) %collective-permute-start.7) | collective-permute-done | bytes 65568 | tf_op jit(solution)/shard_map/ppermute | solution.py:304
  29.1 0.0 collective-permute-done.5.refs_4_
  29.1 0.0 collective-permute-done.6.refs_5_
  29.1 1.5 %final.1 = (f32[2048,128]{1,0:T(8,128)}, f32[768,128]{1,0:T(8,128)}) custom-call(s32[1,16]{1,0:T(1,128)S(4)} %get-tuple-element.21.refs_0_, f32[2048,128]{1,0:T(8,128)S(1)} %get-tuple-element.27.refs_1_, f32[768,128]{1,0:T(8,128)S(1)} %get-tuple-element.28.refs_2_, f32[32,8,128]{2,1,0:T(8,128)S(1)} %get-tuple-element.32.refs_3_, ...), custom_call_target="tpu_custom_call" | custom-call | bytes 6000000 | tf_op jit(solution)/shard_map/final/pallas_call | solution.py:425
Async XLA Ops:
  0.6 1.8 %copy-start.2 = (f32[48,16,128]{2,1,0:T(8,128)S(1)}, f32[48,16,128]{2,1,0:T(8,128)}, u32[]{:S(2)}) copy-start(f32[48,16,128]{2,1,0:T(8,128)} %param.10) | copy-start | bytes 1179652
  0.6 1.8 %copy-start = (f32[128,16,128]{2,1,0:T(8,128)S(1)}, f32[128,16,128]{2,1,0:T(8,128)}, u32[]{:S(2)}) copy-start(f32[128,16,128]{2,1,0:T(8,128)} %param.9) | copy-start | bytes 3145732
  2.4 12.7 %copy-start.1 = (bf16[1,48,128,128]{3,2,1,0:T(8,128)(2,1)S(1)}, bf16[1,48,128,128]{3,2,1,0:T(8,128)(2,1)}, u32[]{:S(2)}) copy-start(bf16[1,48,128,128]{3,2,1,0:T(8,128)(2,1)} %param.14) | copy-start | bytes 4718596
  2.6 14.0 %collective-permute-start = (bf16[2,176,128]{2,1,0:T(8,128)(2,1)S(1)}, bf16[2,176,128]{2,1,0:T(8,128)(2,1)S(1)}, u32[]{:S(2)}, u32[]{:S(2)}) collective-permute-start(bf16[2,176,128]{2,1,0:T(8,128)(2,1)S(1)} %get-tuple-element.25), channel_id=1, source_target_pairs={{0,4},{4,0},{8,12},{12,8},{16,20},{20,16},{24,28},{28,24},{1,5},{5... | collective-permute-start | bytes 270344 | tf_op jit(solution)/shard_map/ppermute | solution.py:378
  3.3 13.2 %collective-permute-start.1 = (bf16[2,176,128]{2,1,0:T(8,128)(2,1)S(1)}, bf16[2,176,128]{2,1,0:T(8,128)(2,1)S(1)}, u32[]{:S(2)}, u32[]{:S(2)}) collective-permute-start(bf16[2,176,128]{2,1,0:T(8,128)(2,1)S(1)} %get-tuple-element.26), channel_id=1, source_target_pairs={{4,8},{12,16},{20,24},{8,4},{16,12},{24,20},{5,9},{13,17},{21,25},... | collective-permute-start | bytes 270344 | tf_op jit(solution)/shard_map/ppermute | solution.py:379
  6.5 4.3 %collective-permute-start.4 = (bf16[32,8,128]{2,1,0:T(8,128)(2,1)S(1)}, bf16[32,8,128]{2,1,0:T(8,128)(2,1)S(1)}, u32[]{:S(2)}, u32[]{:S(2)}) collective-permute-start(bf16[32,8,128]{2,1,0:T(8,128)(2,1)S(1)} %get-tuple-element.31.refs_3_), channel_id=1, source_target_pairs={{0,2},{1,3},{2,0},{3,1},{4,6},{5,7},{6,4},{7,5},{8,10},{9,11},{10,... | collective-permute-start | bytes 196616 | tf_op jit(solution)/shard_map/ppermute | solution.py:304
  8.8 5.8 %collective-permute-start.3 = (bf16[32,8,128]{2,1,0:T(8,128)(2,1)S(1)}, bf16[32,8,128]{2,1,0:T(8,128)(2,1)S(1)}, u32[]{:S(2)}, u32[]{:S(2)}) collective-permute-start(bf16[32,8,128]{2,1,0:T(8,128)(2,1)S(1)} %get-tuple-element.31.refs_3_), channel_id=1, source_target_pairs={{0,3},{1,2},{2,1},{3,0},{4,7},{5,6},{6,5},{7,4},{8,11},{9,10},{10,... | collective-permute-start | bytes 196616 | tf_op jit(solution)/shard_map/ppermute | solution.py:304
  9.9 5.1 %collective-permute-start.2 = (bf16[32,8,128]{2,1,0:T(8,128)(2,1)S(1)}, bf16[32,8,128]{2,1,0:T(8,128)(2,1)S(1)}, u32[]{:S(2)}, u32[]{:S(2)}) collective-permute-start(bf16[32,8,128]{2,1,0:T(8,128)(2,1)S(1)} %get-tuple-element.31.refs_3_), channel_id=1, source_target_pairs={{0,1},{1,0},{2,3},{3,2},{4,5},{5,4},{6,7},{7,6},{8,9},{9,8},{10,11... | collective-permute-start | bytes 196616 | tf_op jit(solution)/shard_map/ppermute | solution.py:304
  17.7 11.4 %collective-permute-start.5 = (bf16[304,128]{1,0:T(8,128)(2,1)S(1)}, bf16[304,128]{1,0:T(8,128)(2,1)S(1)}, u32[]{:S(2)}, u32[]{:S(2)}) collective-permute-start(bf16[304,128]{1,0:T(8,128)(2,1)S(1)} %get-tuple-element.35), channel_id=1, source_target_pairs={{0,1},{1,0},{2,3},{3,2},{4,5},{5,4},{6,7},{7,6},{8,9},{9,8},{10,11... | collective-permute-start | bytes 233480 | tf_op jit(solution)/shard_map/ppermute | solution.py:304
  18.7 10.4 %collective-permute-start.6 = (bf16[304,128]{1,0:T(8,128)(2,1)S(1)}, bf16[304,128]{1,0:T(8,128)(2,1)S(1)}, u32[]{:S(2)}, u32[]{:S(2)}) collective-permute-start(bf16[304,128]{1,0:T(8,128)(2,1)S(1)} %get-tuple-element.36), channel_id=1, source_target_pairs={{0,3},{1,2},{2,1},{3,0},{4,7},{5,6},{6,5},{7,4},{8,11},{9,10},{10,... | collective-permute-start | bytes 233480 | tf_op jit(solution)/shard_map/ppermute | solution.py:304
  21.8 7.3 %collective-permute-start.7 = (bf16[256,128]{1,0:T(8,128)(2,1)S(1)}, bf16[256,128]{1,0:T(8,128)(2,1)S(1)}, u32[]{:S(2)}, u32[]{:S(2)}) collective-permute-start(bf16[256,128]{1,0:T(8,128)(2,1)S(1)} %get-tuple-element.37), channel_id=1, source_target_pairs={{0,2},{1,3},{2,0},{3,1},{4,6},{5,7},{6,4},{7,5},{8,10},{9,11},{10,... | collective-permute-start | bytes 196616 | tf_op jit(solution)/shard_map/ppermute | solution.py:304

commit v6 on v5

--- a/solution.py
+++ b/solution.py
@@ -45,7 +45,7 @@
 
 def comp_pairs(count):
     even = [(i, beside_even(i)) for i in range(count)]
-    odd = [(i, i + 1) for i in range(1, count - 1, 2)] + [(i + 1, i) for i in range(1, count - 1, 2)]
+    odd = [(i, beside_odd(i, count)) for i in range(count)]
     return even, odd
 
 
@@ -97,9 +97,12 @@
     rate[split:, :] = jnp.broadcast_to(rate_o[...], (lanes, rate_o.shape[1])).T
 
 
-def halo_rows(parity, even_in, odd_in, at):
+def halo_rows(comp, even_in, odd_in, at):
+    parity = lax.rem(comp, 2)
+    outside = (comp == 0) | (comp == lax.axis_size("comp") - 1)
     e = [even_in[r, at : at + 8, :].astype(F32) for r in range(2)]
     o = [odd_in[r, at : at + 8, :].astype(F32) for r in range(2)]
+    o = [jnp.where(outside, jnp.zeros_like(x), x) for x in o]
     north = [jnp.where(parity == 0, o[r], e[r]) for r in range(2)]
     south = [jnp.where(parity == 0, e[r], o[r]) for r in range(2)]
     return north, south
@@ -107,7 +110,7 @@
 
 def pack_columns(rows_a, rows_o, atm, ocean, rate, even_in, odd_in, part_a, part_b, out_a, out_b, spread, stage):
     del part_a, part_b
-    parity = lax.rem(lax.axis_index("comp"), 2)
+    comp = lax.axis_index("comp")
     tile_parity = lax.rem(lax.axis_index("tile"), 2)
     lanes = atm.shape[1]
     row = lax.broadcasted_iota(jnp.int32, (8, lanes), 0)
@@ -127,7 +130,7 @@
             rho = rate[at + c : at + c + 8, :]
             own = 2.0 * rho * (1.0 - 4.0 * rho)
             square = rho * rho
-            north, south = halo_rows(parity, even_in, odd_in, at + c)
+            north, south = halo_rows(comp, even_in, odd_in, at + c)
             q = [north[1]]
             q += [ref[pl.ds(c * rows + r, 8, stride=rows), :] for r in range(rows)]
             q += [south[0]]
@@ -194,7 +197,6 @@
 
 def stencil(rows_a, rows_o, atm, ocean, rate, even_in, odd_in, atm_out, ocean_out):
     comp = lax.axis_index("comp")
-    parity = lax.rem(comp, 2)
     lanes = atm.shape[1]
     lane = lax.broadcasted_iota(jnp.int32, (8, lanes), 1)
     at_west = lane == 0
@@ -207,7 +209,7 @@
         for c in range(0, channels, 8):
             rho = rate[at + c : at + c + 8, :]
             own = 1.0 - 4.0 * rho
-            north, south = halo_rows(parity, even_in, odd_in, at + c)
+            north, south = halo_rows(comp, even_in, odd_in, at + c)
             q = north + [ref[pl.ds(c * rows + r, 8, stride=rows), :] for r in range(rows)] + south
             p = []
             for i in range(1, rows + 3):

time: 30.8 us -> 29.7 us (0.964)
  the two profiles are of different devices: /device:TPU:3 before, /device:TPU:0 now
where the time goes in v6:
time: 29.7 us; the launch traced here: 29.5 us
  starting transfers between devices  11.8 us (40%)
  waiting for transfers between devices  8.58 us (29%)
  Pallas kernels  7.66 us (26%)
  between operations  1.48 us (5%)
    ppermute x6, waiting for transfers between devices, exchange(): out.append(lax.ppermute(block, 'tile', route))  8.57 us
    ppermute x6, starting transfers between devices, exchange(): out.append(lax.ppermute(block, 'tile', route))  7.69 us
    ppermute x1, starting transfers between devices, interval(): odd_in = lax.ppermute(odd_rows, 'comp', odd_pairs)  3.54 us
    pallas_call x1, Pallas kernels, interval(): call(functools.partial(stencil, rows_a, rows_o), 2.5, 8 << 20, in_specs=[...  2.44 us
    pallas_call x1, Pallas kernels, interval(): call(functools.partial(final, tile_count, rows_a, rows_o), 2.0, 12 << 20,...  1.52 us
    pallas_call x1, Pallas kernels, interval(): call(functools.partial(remap, tile_count, rows_a, rows_o), 2.0, 12 << 20,...  1.47 us
    pallas_call x1, Pallas kernels, interval(): call(functools.partial(pack_columns, rows_a, rows_o), 1.2, 8 << 20, in_sp...  1.11 us
    pallas_call x1, Pallas kernels, interval(): call(functools.partial(pack_surface, rows_a, rows_o), 0.8, 4 << 20, in_sp...  0.98 us
  transfers between devices with their start and end apart: 8, of which 4 were waited for; matrix products, arithmetic and copies ran while one was open for 0% of the time, Pallas kernels for 13%

profile of v6, /device:TPU:0, one launch (start us, length us, event | category | flops | bytes accessed | tf_op | source)
XLA Modules:
  0.0 29.5 jit_solution(17781972014789093331)
XLA Ops:
  0.6 0.0 copy-start.2
  0.6 0.0 copy-start
  1.4 1.0 %pack_surface.1 = (bf16[32,8,128]{2,1,0:T(8,128)(2,1)S(1)}, f32[1,128]{1,0:T(1,128)S(1)}, f32[1,48]{1,0:T(1,128)S(1)}, s32[2,48]{1,0:T(2,128)S(4)}, s32[1,16]{1,0:T(1,128)S(4)}) custom-call(f32[2048,128]{1,0:T(8,128)} %bitcast.8, f32[768,128]{1,0:T(8,128)} %bitcast.14, s32[1,16]{1,0:T(1,128)} %bitcast.18, s32[1,48]{1,0:T(1,128)} %refs_3_.1, ...), custom_call_target="tpu_custom_call" | custom-call | bytes 2400000 | tf_op jit(solution)/shard_map/pack_surface/pallas_call | solution.py:335
  2.4 0.0 copy-start.1
  2.4 0.0 copy-done.2
  2.4 0.0 copy-done
  2.4 0.1 prepare.1
  2.6 0.6 %collective-permute-start = (bf16[2,176,128]{2,1,0:T(8,128)(2,1)S(1)}, bf16[2,176,128]{2,1,0:T(8,128)(2,1)S(1)}, u32[]{:S(2)}, u32[]{:S(2)}) collective-permute-start(bf16[2,176,128]{2,1,0:T(8,128)(2,1)S(1)} %get-tuple-element.25), channel_id=1, source_target_pairs={{0,4},{4,0},{8,12},{12,8},{16,20},{20,16},{24,28},{28,24},{1,5},{5... | collective-permute-start | bytes 270344 | tf_op jit(solution)/shard_map/ppermute | solution.py:380
  3.1 3.5 %collective-permute-start.1 = (bf16[2,176,128]{2,1,0:T(8,128)(2,1)S(1)}, bf16[2,176,128]{2,1,0:T(8,128)(2,1)S(1)}, u32[]{:S(2)}, u32[]{:S(2)}) collective-permute-start(bf16[2,176,128]{2,1,0:T(8,128)(2,1)S(1)} %get-tuple-element.26), channel_id=1, source_target_pairs={{0,28},{4,8},{8,4},{12,16},{16,12},{20,24},{24,20},{28,0},{1,29},{... | collective-permute-start | bytes 270344 | tf_op jit(solution)/shard_map/ppermute | solution.py:381
  6.7 2.6 %collective-permute-start.4 = (bf16[32,8,128]{2,1,0:T(8,128)(2,1)S(1)}, bf16[32,8,128]{2,1,0:T(8,128)(2,1)S(1)}, u32[]{:S(2)}, u32[]{:S(2)}) collective-permute-start(bf16[32,8,128]{2,1,0:T(8,128)(2,1)S(1)} %get-tuple-element.31.refs_3_), channel_id=1, source_target_pairs={{0,2},{1,3},{2,0},{3,1},{4,6},{5,7},{6,4},{7,5},{8,10},{9,11},{10,... | collective-permute-start | bytes 196616 | tf_op jit(solution)/shard_map/ppermute | solution.py:306
  9.3 1.3 %collective-permute-start.3 = (bf16[32,8,128]{2,1,0:T(8,128)(2,1)S(1)}, bf16[32,8,128]{2,1,0:T(8,128)(2,1)S(1)}, u32[]{:S(2)}, u32[]{:S(2)}) collective-permute-start(bf16[32,8,128]{2,1,0:T(8,128)(2,1)S(1)} %get-tuple-element.31.refs_3_), channel_id=1, source_target_pairs={{0,3},{1,2},{2,1},{3,0},{4,7},{5,6},{6,5},{7,4},{8,11},{9,10},{10,... | collective-permute-start | bytes 196616 | tf_op jit(solution)/shard_map/ppermute | solution.py:306
  10.6 0.2 collective-permute-start.2
  10.8 1.1 %collective-permute-done.4.refs_6_ = bf16[32,8,128]{2,1,0:T(8,128)(2,1)S(1)} collective-permute-done((bf16[32,8,128]{2,1,0:T(8,128)(2,1)S(1)}, bf16[32,8,128]{2,1,0:T(8,128)(2,1)S(1)}, u32[]{:S(2)}, u32[]{:S(2)}) %collective-permute-start.4) | collective-permute-done | bytes 65568 | tf_op jit(solution)/shard_map/ppermute | solution.py:306
  12.0 3.5 %collective-permute-done.3.refs_5_ = bf16[32,8,128]{2,1,0:T(8,128)(2,1)S(1)} collective-permute-done((bf16[32,8,128]{2,1,0:T(8,128)(2,1)S(1)}, bf16[32,8,128]{2,1,0:T(8,128)(2,1)S(1)}, u32[]{:S(2)}, u32[]{:S(2)}) %collective-permute-start.3) | collective-permute-done | bytes 65568 | tf_op jit(solution)/shard_map/ppermute | solution.py:306
  15.4 0.2 collective-permute-done.2.refs_4_
  15.6 0.0 copy-done.1
  15.6 1.5 %remap.1 = (f32[32,8,128]{2,1,0:T(8,128)S(1)}, bf16[304,128]{1,0:T(8,128)(2,1)S(1)}, bf16[304,128]{1,0:T(8,128)(2,1)S(1)}, bf16[256,128]{1,0:T(8,128)(2,1)S(1)}) custom-call(s32[2,48]{1,0:T(2,128)S(4)} %get-tuple-element.29.refs_0_, s32[1,48]{1,0:T(1,128)S(4)} %get-tuple-element.30.refs_1_, bf16[48,128,128]{2,1,0:T(8,128)(2,1)S(1)} %bitcast.13, ...), custom_call_target="tpu_custom_call" | custom-call | bytes 6000000 | tf_op jit(solution)/shard_map/remap/pallas_call | solution.py:385
  17.1 0.0 collective-permute-done.even_in
  17.1 0.0 collective-permute-done.1.odd_in
  17.1 1.1 %pack_columns.1 = (bf16[304,128]{1,0:T(8,128)(2,1)S(1)}, bf16[304,128]{1,0:T(8,128)(2,1)S(1)}) custom-call(f32[2048,128]{1,0:T(8,128)S(1)} %bitcast.10, f32[768,128]{1,0:T(8,128)S(1)} %bitcast.16, f32[176,128]{1,0:T(8,128)S(1)} %get-tuple-element.24.rate, ...), custom_call_target="tpu_custom_call", output_to_operand_aliasing={{0}: (5, {}), {1}: (6, {})} | custom-call | bytes 3600000 | tf_op jit(solution)/shard_map/pack_columns/pallas_call | solution.py:398
  18.2 0.0 collective-permute-start.5
  18.2 3.4 %collective-permute-start.6 = (bf16[304,128]{1,0:T(8,128)(2,1)S(1)}, bf16[304,128]{1,0:T(8,128)(2,1)S(1)}, u32[]{:S(2)}, u32[]{:S(2)}) collective-permute-start(bf16[304,128]{1,0:T(8,128)(2,1)S(1)} %get-tuple-element.36), channel_id=1, source_target_pairs={{0,3},{1,2},{2,1},{3,0},{4,7},{5,6},{6,5},{7,4},{8,11},{9,10},{10,... | collective-permute-start | bytes 233480 | tf_op jit(solution)/shard_map/ppermute | solution.py:306
  21.6 0.1 collective-permute-start.7
  21.7 2.4 %stencil.1 = (f32[2048,128]{1,0:T(8,128)S(1)}, f32[768,128]{1,0:T(8,128)S(1)}) custom-call(f32[2048,128]{1,0:T(8,128)S(1)} %bitcast.11, f32[768,128]{1,0:T(8,128)S(1)} %bitcast.17, f32[176,128]{1,0:T(8,128)S(1)} %get-tuple-element.24.rate, bf16[2,176,128]{2,1,0:T(8,128)(2,1)S(1)} %collective-permute-done.even_in, ...), custom_call_target="tpu_custom_call" | custom-call | bytes 7500000 | tf_op jit(solution)/shard_map/stencil/pallas_call | solution.py:414
  24.2 3.8 %collective-permute-done.7.refs_6_ = bf16[256,128]{1,0:T(8,128)(2,1)S(1)} collective-permute-done((bf16[256,128]{1,0:T(8,128)(2,1)S(1)}, bf16[256,128]{1,0:T(8,128)(2,1)S(1)}, u32[]{:S(2)}, u32[]{:S(2)}) %collective-permute-start.7) | collective-permute-done | bytes 65568 | tf_op jit(solution)/shard_map/ppermute | solution.py:306
  28.0 0.0 collective-permute-done.5.refs_4_
  28.0 0.0 collective-permute-done.6.refs_5_
  28.0 1.5 %final.1 = (f32[2048,128]{1,0:T(8,128)}, f32[768,128]{1,0:T(8,128)}) custom-call(s32[1,16]{1,0:T(1,128)S(4)} %get-tuple-element.21.refs_0_, f32[2048,128]{1,0:T(8,128)S(1)} %get-tuple-element.27.refs_1_, f32[768,128]{1,0:T(8,128)S(1)} %get-tuple-element.28.refs_2_, f32[32,8,128]{2,1,0:T(8,128)S(1)} %get-tuple-element.32.refs_3_, ...), custom_call_target="tpu_custom_call" | custom-call | bytes 6000000 | tf_op jit(solution)/shard_map/final/pallas_call | solution.py:427
Async XLA Ops:
  0.6 1.8 %copy-start.2 = (f32[48,16,128]{2,1,0:T(8,128)S(1)}, f32[48,16,128]{2,1,0:T(8,128)}, u32[]{:S(2)}) copy-start(f32[48,16,128]{2,1,0:T(8,128)} %param.10) | copy-start | bytes 1179652
  0.6 1.8 %copy-start = (f32[128,16,128]{2,1,0:T(8,128)S(1)}, f32[128,16,128]{2,1,0:T(8,128)}, u32[]{:S(2)}) copy-start(f32[128,16,128]{2,1,0:T(8,128)} %param.9) | copy-start | bytes 3145732
  2.4 13.2 %copy-start.1 = (bf16[1,48,128,128]{3,2,1,0:T(8,128)(2,1)S(1)}, bf16[1,48,128,128]{3,2,1,0:T(8,128)(2,1)}, u32[]{:S(2)}) copy-start(bf16[1,48,128,128]{3,2,1,0:T(8,128)(2,1)} %param.14) | copy-start | bytes 4718596
  2.6 14.5 %collective-permute-start = (bf16[2,176,128]{2,1,0:T(8,128)(2,1)S(1)}, bf16[2,176,128]{2,1,0:T(8,128)(2,1)S(1)}, u32[]{:S(2)}, u32[]{:S(2)}) collective-permute-start(bf16[2,176,128]{2,1,0:T(8,128)(2,1)S(1)} %get-tuple-element.25), channel_id=1, source_target_pairs={{0,4},{4,0},{8,12},{12,8},{16,20},{20,16},{24,28},{28,24},{1,5},{5... | collective-permute-start | bytes 270344 | tf_op jit(solution)/shard_map/ppermute | solution.py:380
  3.1 13.9 %collective-permute-start.1 = (bf16[2,176,128]{2,1,0:T(8,128)(2,1)S(1)}, bf16[2,176,128]{2,1,0:T(8,128)(2,1)S(1)}, u32[]{:S(2)}, u32[]{:S(2)}) collective-permute-start(bf16[2,176,128]{2,1,0:T(8,128)(2,1)S(1)} %get-tuple-element.26), channel_id=1, source_target_pairs={{0,28},{4,8},{8,4},{12,16},{16,12},{20,24},{24,20},{28,0},{1,29},{... | collective-permute-start | bytes 270344 | tf_op jit(solution)/shard_map/ppermute | solution.py:381
  6.7 5.3 %collective-permute-start.4 = (bf16[32,8,128]{2,1,0:T(8,128)(2,1)S(1)}, bf16[32,8,128]{2,1,0:T(8,128)(2,1)S(1)}, u32[]{:S(2)}, u32[]{:S(2)}) collective-permute-start(bf16[32,8,128]{2,1,0:T(8,128)(2,1)S(1)} %get-tuple-element.31.refs_3_), channel_id=1, source_target_pairs={{0,2},{1,3},{2,0},{3,1},{4,6},{5,7},{6,4},{7,5},{8,10},{9,11},{10,... | collective-permute-start | bytes 196616 | tf_op jit(solution)/shard_map/ppermute | solution.py:306
  9.3 6.2 %collective-permute-start.3 = (bf16[32,8,128]{2,1,0:T(8,128)(2,1)S(1)}, bf16[32,8,128]{2,1,0:T(8,128)(2,1)S(1)}, u32[]{:S(2)}, u32[]{:S(2)}) collective-permute-start(bf16[32,8,128]{2,1,0:T(8,128)(2,1)S(1)} %get-tuple-element.31.refs_3_), channel_id=1, source_target_pairs={{0,3},{1,2},{2,1},{3,0},{4,7},{5,6},{6,5},{7,4},{8,11},{9,10},{10,... | collective-permute-start | bytes 196616 | tf_op jit(solution)/shard_map/ppermute | solution.py:306
  10.6 5.0 %collective-permute-start.2 = (bf16[32,8,128]{2,1,0:T(8,128)(2,1)S(1)}, bf16[32,8,128]{2,1,0:T(8,128)(2,1)S(1)}, u32[]{:S(2)}, u32[]{:S(2)}) collective-permute-start(bf16[32,8,128]{2,1,0:T(8,128)(2,1)S(1)} %get-tuple-element.31.refs_3_), channel_id=1, source_target_pairs={{0,1},{1,0},{2,3},{3,2},{4,5},{5,4},{6,7},{7,6},{8,9},{9,8},{10,11... | collective-permute-start | bytes 196616 | tf_op jit(solution)/shard_map/ppermute | solution.py:306
  18.2 9.8 %collective-permute-start.5 = (bf16[304,128]{1,0:T(8,128)(2,1)S(1)}, bf16[304,128]{1,0:T(8,128)(2,1)S(1)}, u32[]{:S(2)}, u32[]{:S(2)}) collective-permute-start(bf16[304,128]{1,0:T(8,128)(2,1)S(1)} %get-tuple-element.35), channel_id=1, source_target_pairs={{0,1},{1,0},{2,3},{3,2},{4,5},{5,4},{6,7},{7,6},{8,9},{9,8},{10,11... | collective-permute-start | bytes 233480 | tf_op jit(solution)/shard_map/ppermute | solution.py:306
  18.2 9.8 %collective-permute-start.6 = (bf16[304,128]{1,0:T(8,128)(2,1)S(1)}, bf16[304,128]{1,0:T(8,128)(2,1)S(1)}, u32[]{:S(2)}, u32[]{:S(2)}) collective-permute-start(bf16[304,128]{1,0:T(8,128)(2,1)S(1)} %get-tuple-element.36), channel_id=1, source_target_pairs={{0,3},{1,2},{2,1},{3,0},{4,7},{5,6},{6,5},{7,4},{8,11},{9,10},{10,... | collective-permute-start | bytes 233480 | tf_op jit(solution)/shard_map/ppermute | solution.py:306
  21.6 6.4 %collective-permute-start.7 = (bf16[256,128]{1,0:T(8,128)(2,1)S(1)}, bf16[256,128]{1,0:T(8,128)(2,1)S(1)}, u32[]{:S(2)}, u32[]{:S(2)}) collective-permute-start(bf16[256,128]{1,0:T(8,128)(2,1)S(1)} %get-tuple-element.37), channel_id=1, source_target_pairs={{0,2},{1,3},{2,0},{3,1},{4,6},{5,7},{6,4},{7,5},{8,10},{9,11},{10,... | collective-permute-start | bytes 196616 | tf_op jit(solution)/shard_map/ppermute | solution.py:306

commit v7 on v6

--- a/solution.py
+++ b/solution.py
@@ -108,9 +108,7 @@
     return north, south
 
 
-def pack_columns(rows_a, rows_o, atm, ocean, rate, even_in, odd_in, part_a, part_b, out_a, out_b, spread, stage):
-    del part_a, part_b
-    comp = lax.axis_index("comp")
+def pack_columns(rows_a, rows_o, atm, ocean, rate, out, spread):
     tile_parity = lax.rem(lax.axis_index("tile"), 2)
     lanes = atm.shape[1]
     row = lax.broadcasted_iota(jnp.int32, (8, lanes), 0)
@@ -122,7 +120,7 @@
     outer = (lane == 0) | (lane == lanes - 1)
     turn = (lane == 1) | (lane == lanes - 1)
     dims = (((1,), (1,)), ((), ()))
-    stage[...] = jnp.zeros_like(stage)
+    out[...] = jnp.zeros_like(out)
     at = 0
     for ref, rows in ((atm, rows_a), (ocean, rows_o)):
         channels = ref.shape[0] // rows
@@ -130,13 +128,13 @@
             rho = rate[at + c : at + c + 8, :]
             own = 2.0 * rho * (1.0 - 4.0 * rho)
             square = rho * rho
-            north, south = halo_rows(comp, even_in, odd_in, at + c)
-            q = [north[1]]
-            q += [ref[pl.ds(c * rows + r, 8, stride=rows), :] for r in range(rows)]
-            q += [south[0]]
+            q = [ref[pl.ds(c * rows + r, 8, stride=rows), :] for r in range(rows)]
             for r in range(rows):
-                far = square * q[r + 1]
-                near = own * q[r + 1] + 2.0 * square * (q[r] + q[r + 2])
+                far = square * q[r]
+                beside = q[1] if r == 0 else q[r - 1]
+                if 0 < r < rows - 1:
+                    beside = beside + q[r + 1]
+                near = own * q[r] + 2.0 * square * beside
                 moved = jnp.where(turn, pltpu.roll(far, 1, 1), pltpu.roll(far, lanes - 1, 1))
                 value = moved + jnp.where(outer, near, 0.0)
                 spread[pl.ds((at + c) * rows + r, 8, stride=rows), :] = value
@@ -144,11 +142,39 @@
     for j in range(at // 8):
         part = spread[j * 8 * rows_a : (j + 1) * 8 * rows_a, :].astype(BF16)
         found = lax.dot_general(pick, part, dims, preferred_element_type=F32)
-        stage[0, 2 * j : 2 * j + 2, :] = found[0:2, :]
-        stage[1, 2 * j : 2 * j + 2, :] = found[2:4, :]
-    behind = out_a.shape[0] - stage.shape[1]
-    out_a[behind:, :] = stage[0].astype(BF16)
-    out_b[behind:, :] = stage[1].astype(BF16)
+        out[0, 2 * j : 2 * j + 2, :] = found[0:2, :]
+        out[1, 2 * j : 2 * j + 2, :] = found[2:4, :]
+
+
+def corners(stage, even_in, odd_in, part_a, part_b, out_a, out_b, joined):
+    del part_a, part_b
+    comp = lax.axis_index("comp")
+    parity = lax.rem(comp, 2)
+    outside = (comp == 0) | (comp == lax.axis_size("comp") - 1)
+    tile_parity = lax.rem(lax.axis_index("tile"), 2)
+    channels, lanes = even_in.shape[1:]
+    row = lax.broadcasted_iota(jnp.int32, (8, lanes), 0)
+    lane = lax.broadcasted_iota(jnp.int32, (8, lanes), 1)
+    spot = jnp.where(row == tile_parity, lanes - 1, 0)
+    pick = jnp.where((row < 2) & (lane == spot), 1.0, 0.0).astype(BF16)
+    dims = (((1,), (1,)), ((), ()))
+    joined[...] = stage[...]
+    pieces = -(-channels // lanes)
+    first = 2 * channels // 8
+    for side in range(2):
+        even = even_in[1 - side]
+        odd = odd_in[1 - side]
+        odd = jnp.where(outside, jnp.zeros_like(odd), odd)
+        beyond = jnp.where(parity == side, odd, even)
+        for i in range(pieces):
+            part = beyond[i * lanes : min((i + 1) * lanes, channels), :]
+            found = lax.dot_general(pick, part, dims, preferred_element_type=F32)
+            at = first + side * pieces + i
+            for k in range(2):
+                joined[k, at : at + 1, 0 : part.shape[0]] = found[k : k + 1, :]
+    behind = out_a.shape[0] - joined.shape[1]
+    out_a[behind:, :] = joined[0].astype(BF16)
+    out_b[behind:, :] = joined[1].astype(BF16)
 
 
 def remap(tile_count, rows_a, rows_o, *refs):
@@ -228,11 +254,9 @@
         at += channels
 
 
-def final(tile_count, rows_a, rows_o, *refs):
-    mask, atm, ocean, own = refs[:4]
-    got = refs[4 : 3 + tile_count]
-    atm_out, ocean_out, force, value_a, value_o, done = refs[3 + tile_count :]
-    lanes = atm.shape[1]
+def edges(rows_a, rows_o, mask, rate, atm, ocean, own, got_a, got_b, *refs):
+    atm_out, ocean_out, surface, force, north, south, value_a, value_o, done = refs
+    channels, lanes = rate.shape
     block = rows_a + rows_o
     message = block * SURF
     tile_parity = lax.rem(lax.axis_index("tile"), 2)
@@ -242,41 +266,45 @@
     second = lax.rem(row, 2)
     spot = jnp.where(east, lanes - 1 - second, second)
     place = jnp.where((row < 4) & (lane == spot), 1.0, 0.0).astype(BF16)
-    for y in range(block):
-        total = own[y]
-        for ref in got:
-            total = total + ref[SURF * y : SURF * y + SURF, :].astype(F32)
-        if y >= rows_a:
-            total = total * mask[0, y - rows_a].astype(F32)
-        start = y if y < rows_a else SURF * rows_a + y - rows_a
-        force[pl.ds(start, SURF, stride=rows_a if y < rows_a else rows_o), :] = total
+    outer = jnp.where(row == tile_parity, lanes - 1, 0)
+    place_outer = jnp.where((row < 2) & (lane == outer), 1.0, 0.0).astype(BF16)
     dims = (((0,), (0,)), ((), ()))
+
+    def sides(at, count):
+        rows = [got_a[at : at + count, :].astype(F32), got_b[at : at + count, :].astype(F32)]
+        rows.append(jnp.zeros((8 - 2 * count, lanes), F32))
+        return jnp.concatenate(rows, axis=0).astype(BF16)
+
+    pieces = -(-channels // lanes)
+    first = message + 2 * channels // 8
+    for side, ref in ((0, north), (1, south)):
+        for i in range(pieces):
+            size = min(lanes, channels - i * lanes)
+            cells = lax.dot_general(
+                sides(first + side * pieces + i, 1), place_outer, dims, preferred_element_type=F32
+            )
+            rho = rate[i * lanes : i * lanes + size, :]
+            ref[i * lanes : i * lanes + size, :] = 2.0 * rho * rho * cells[0:size, :]
     group = 32
     at = 0
     copies = []
-    for ref, keep, out, rows, add in (
-        (atm, value_a, atm_out, rows_a, 0),
-        (ocean, value_o, ocean_out, rows_o, SURF * rows_a),
+    for ref, keep, out, rows in (
+        (atm, value_a, atm_out, rows_a),
+        (ocean, value_o, ocean_out, rows_o),
     ):
-        channels = ref.shape[0] // rows
-        for c in range(0, channels, 8):
-            j = message + 2 * ((at + c) // 8)
-            sides = jnp.concatenate(
-                [
-                    got[0][j : j + 2, :].astype(F32),
-                    got[1][j : j + 2, :].astype(F32),
-                    jnp.zeros((4, lanes), F32),
-                ],
-                axis=0,
-            ).astype(BF16)
-            value = ref[c * rows : (c + 8) * rows, :] + lax.dot_general(
-                sides, place, dims, preferred_element_type=F32
+        count = ref.shape[0] // rows
+        for c in range(0, count, 8):
+            keep[c * rows : (c + 8) * rows, :] = ref[
+                c * rows : (c + 8) * rows, :
+            ] + lax.dot_general(
+                sides(message + 2 * ((at + c) // 8), 2), place, dims, preferred_element_type=F32
             )
-            if c == 0:
-                value = value + force[add : add + SURF * rows, :]
-            keep[c * rows : (c + 8) * rows, :] = value
-            if (c + 8) % group == 0 or c + 8 == channels:
-                begin = c // group * group * rows
+            top = pl.ds(c * rows, 8, stride=rows)
+            bottom = pl.ds(c * rows + rows - 1, 8, stride=rows)
+            keep[top, :] = keep[top, :] + north[at + c : at + c + 8, :]
+            keep[bottom, :] = keep[bottom, :] + south[at + c : at + c + 8, :]
+            if (c + 8) % group == 0 or c + 8 == count:
+                begin = max(c // group * group, SURF) * rows
                 end = (c + 8) * rows
                 copies.append(
                     pltpu.make_async_copy(
@@ -284,7 +312,44 @@
                     )
                 )
                 copies[-1].start()
-        at += channels
+        at += count
+    for y in range(block):
+        total = own[y]
+        for ref in (got_a, got_b):
+            total = total + ref[SURF * y : SURF * y + SURF, :].astype(F32)
+        if y >= rows_a:
+            total = total * mask[0, y - rows_a].astype(F32)
+        start = y if y < rows_a else SURF * rows_a + y - rows_a
+        force[pl.ds(start, SURF, stride=rows_a if y < rows_a else rows_o), :] = total
+    split = SURF * rows_a
+    surface[0:split, :] = value_a[0:split, :] + force[0:split, :]
+    surface[split:, :] = value_o[0 : SURF * rows_o, :] + force[split:, :]
+    for copy in copies:
+        copy.wait()
+
+
+def final(rows_a, rows_o, mask, surface, *refs):
+    got = refs[:-7]
+    _, _, atm_out, ocean_out, force, value, done = refs[-7:]
+    block = rows_a + rows_o
+    for y in range(block):
+        total = got[0][SURF * y : SURF * y + SURF, :].astype(F32)
+        for ref in got[1:]:
+            total = total + ref[SURF * y : SURF * y + SURF, :].astype(F32)
+        if y >= rows_a:
+            total = total * mask[0, y - rows_a].astype(F32)
+        start = y if y < rows_a else SURF * rows_a + y - rows_a
+        force[pl.ds(start, SURF, stride=rows_a if y < rows_a else rows_o), :] = total
+    split = SURF * rows_a
+    copies = []
+    for i, (begin, end, out) in enumerate(
+        ((0, split, atm_out), (split, SURF * block, ocean_out))
+    ):
+        value[begin:end, :] = surface[begin:end, :] + force[begin:end, :]
+        copies.append(
+            pltpu.make_async_copy(value.at[begin:end], out.at[0 : end - begin], done.at[i])
+        )
+        copies[-1].start()
     for copy in copies:
         copy.wait()
 
@@ -324,7 +389,7 @@
     tile_count = lax.axis_size("tile")
     block = rows_a + rows_o
     message = block * SURF
-    extra = -(-2 * channels // 8 // 16) * 16
+    extra = -(-(2 * channels // 8 + 2 * -(-channels // lanes)) // 16) * 16
     atm = atm_state.reshape(channels_a * rows_a, lanes)
     ocean = ocean_state.reshape(channels_o * rows_o, lanes)
     mask = ocean_mask.reshape(1, rows_o)
@@ -380,6 +445,17 @@
     even_in = lax.ppermute(even_rows, "comp", even_pairs)
     odd_in = lax.ppermute(odd_rows, "comp", odd_pairs)
 
+    stage = call(
+        functools.partial(pack_columns, rows_a, rows_o),
+        1.1,
+        8 << 20,
+        in_specs=[VMEM] * 3,
+        out_specs=VMEM,
+        out_shape=pltpu.VMEM((2, extra, lanes), F32),
+        scratch_shapes=[pltpu.VMEM((channels_a * rows_a + channels_o * rows_o, lanes), F32)],
+        name="pack_columns",
+    )(atm, ocean, rate)
+
     sends = [jax.ShapeDtypeStruct((message + extra, lanes), BF16)] * 2
     sends += [jax.ShapeDtypeStruct((message, lanes), BF16)] * (tile_count - 3)
     own_part, *parts = call(
@@ -396,19 +472,16 @@
         name="remap",
     )(table, live, remap_weight[0], surface, *received)
     parts[:2] = call(
-        functools.partial(pack_columns, rows_a, rows_o),
-        1.2,
+        corners,
+        0.3,
         8 << 20,
-        in_specs=[VMEM] * 7,
+        in_specs=[VMEM] * 5,
         out_specs=[VMEM, VMEM],
         out_shape=sends[:2],
-        input_output_aliases={5: 0, 6: 1},
-        scratch_shapes=[
-            pltpu.VMEM((channels_a * rows_a + channels_o * rows_o, lanes), F32),
-            pltpu.VMEM((2, extra, lanes), F32),
-        ],
-        name="pack_columns",
-    )(atm, ocean, rate, even_in, odd_in, *parts[:2])
+        input_output_aliases={3: 0, 4: 1},
+        scratch_shapes=[pltpu.VMEM((2, extra, lanes), F32)],
+        name="corners",
+    )(stage, even_in, odd_in, *parts[:2])
     returned = exchange(parts, routes)
 
     atm_base, ocean_base = call(
@@ -424,24 +497,40 @@
         name="stencil",
     )(atm, ocean, rate, even_in, odd_in)
 
-    atm_next, ocean_next = call(
-        functools.partial(final, tile_count, rows_a, rows_o),
-        2.0,
+    result = [pltpu.HBM(atm.shape, F32), pltpu.HBM(ocean.shape, F32)]
+    atm_next, ocean_next, base = call(
+        functools.partial(edges, rows_a, rows_o),
+        1.5,
         12 << 20,
-        in_specs=[SMEM] + [VMEM] * (2 + tile_count),
-        out_specs=[HBM, HBM],
-        out_shape=[
-            jax.ShapeDtypeStruct(atm.shape, F32),
-            jax.ShapeDtypeStruct(ocean.shape, F32),
-        ],
+        in_specs=[SMEM] + [VMEM] * 6,
+        out_specs=[HBM, HBM, VMEM],
+        out_shape=result + [pltpu.VMEM((message, lanes), F32)],
         scratch_shapes=[
-            pltpu.VMEM((SURF * block, lanes), F32),
+            pltpu.VMEM((message, lanes), F32),
+            pltpu.VMEM((channels, lanes), F32),
+            pltpu.VMEM((channels, lanes), F32),
             pltpu.VMEM(atm.shape, F32),
             pltpu.VMEM(ocean.shape, F32),
             pltpu.SemaphoreType.DMA((channels // 8,)),
         ],
+        name="edges",
+    )(wet, rate, atm_base, ocean_base, own_part, *returned[:2])
+    far = returned[2:]
+    atm_next, ocean_next = call(
+        functools.partial(final, rows_a, rows_o),
+        0.7,
+        4 << 20,
+        in_specs=[SMEM] + [VMEM] * (1 + len(far)) + [HBM, HBM],
+        out_specs=[HBM, HBM],
+        out_shape=result,
+        input_output_aliases={2 + len(far): 0, 3 + len(far): 1},
+        scratch_shapes=[
+            pltpu.VMEM((message, lanes), F32),
+            pltpu.VMEM((message, lanes), F32),
+            pltpu.SemaphoreType.DMA((2,)),
+        ],
         name="final",
-    )(wet, atm_base, ocean_base, own_part, *returned)
+    )(wet, base, *far, hbm(atm_next), hbm(ocean_next))
     return (
         atm_next.reshape(channels_a, rows_a, lanes),
         ocean_next.reshape(channels_o, rows_o, lanes),

time: 29.7 us -> 27.9 us (0.939)
  waiting for transfers between devices: 8.58 us -> 5.95 us
  Pallas kernels: 7.66 us -> 8.51 us
    ppermute x6, waiting for transfers between devices: 8.57 us -> 5.94 us  [exchange(): out.append(lax.ppermute(block, 'tile', route))]
    pallas_call x2 -> x4, Pallas kernels: 2.63 us -> 3.48 us  [the longest x1 1.54 us: interval(): call(functools.partial(edges, rows_a, rows_o), 1.5, 12 << 20, in_specs=[S...]
  transfers between devices with their start and end apart: 8 -> 8, of which waited for: 4 -> 4; matrix products, arithmetic and copies ran while one was open for 0% -> 0% of each run, Pallas kernels for 13% -> 23%
where the time goes in v7:
time: 27.9 us; the launch traced here: 27.8 us
  starting transfers between devices  11.8 us (42%)
  Pallas kernels  8.51 us (31%)
  waiting for transfers between devices  5.95 us (21%)
  between operations  1.5 us (5%)
    ppermute x6, starting transfers between devices, exchange(): out.append(lax.ppermute(block, 'tile', route))  7.69 us
    ppermute x6, waiting for transfers between devices, exchange(): out.append(lax.ppermute(block, 'tile', route))  5.94 us
    ppermute x1, starting transfers between devices, interval(): odd_in = lax.ppermute(odd_rows, 'comp', odd_pairs)  3.54 us
    pallas_call x1, Pallas kernels, interval(): call(functools.partial(stencil, rows_a, rows_o), 2.5, 8 << 20, in_specs=[...  2.44 us
    pallas_call x1, Pallas kernels, interval(): call(functools.partial(edges, rows_a, rows_o), 1.5, 12 << 20, in_specs=[S...  1.54 us
    pallas_call x1, Pallas kernels, interval(): call(functools.partial(remap, tile_count, rows_a, rows_o), 2.0, 12 << 20,...  1.47 us
    pallas_call x1, Pallas kernels, interval(): call(functools.partial(pack_columns, rows_a, rows_o), 1.1, 8 << 20, in_sp...  1.07 us
    pallas_call x1, Pallas kernels, interval(): call(functools.partial(pack_surface, rows_a, rows_o), 0.8, 4 << 20, in_sp...  0.98 us
  transfers between devices with their start and end apart: 8, of which 4 were waited for; matrix products, arithmetic and copies ran while one was open for 0% of the time, Pallas kernels for 23%

profile of v7, /device:TPU:0, one launch (start us, length us, event | category | flops | bytes accessed | tf_op | source)
XLA Modules:
  0.0 27.8 jit_solution(17848994164203567748)
XLA Ops:
  0.6 0.0 copy-start.2
  0.6 0.0 copy-start
  1.4 1.0 %pack_surface.1 = (bf16[32,8,128]{2,1,0:T(8,128)(2,1)S(1)}, f32[1,128]{1,0:T(1,128)S(1)}, f32[1,48]{1,0:T(1,128)S(1)}, s32[2,48]{1,0:T(2,128)S(4)}, s32[1,16]{1,0:T(1,128)S(4)}) custom-call(f32[2048,128]{1,0:T(8,128)} %bitcast.8, f32[768,128]{1,0:T(8,128)} %bitcast.14, s32[1,16]{1,0:T(1,128)} %bitcast.20, s32[1,48]{1,0:T(1,128)} %refs_3_.1, ...), custom_call_target="tpu_custom_call" | custom-call | bytes 2400000 | tf_op jit(solution)/shard_map/pack_surface/pallas_call | solution.py:400
  2.4 0.0 copy-done.2
  2.4 0.0 copy-done
  2.4 0.0 copy-start.1
  2.4 0.1 prepare.1
  2.6 0.6 %collective-permute-start = (bf16[2,176,128]{2,1,0:T(8,128)(2,1)S(1)}, bf16[2,176,128]{2,1,0:T(8,128)(2,1)S(1)}, u32[]{:S(2)}, u32[]{:S(2)}) collective-permute-start(bf16[2,176,128]{2,1,0:T(8,128)(2,1)S(1)} %get-tuple-element.28), channel_id=1, source_target_pairs={{0,4},{4,0},{8,12},{12,8},{16,20},{20,16},{24,28},{28,24},{1,5},{5... | collective-permute-start | bytes 270344 | tf_op jit(solution)/shard_map/ppermute | solution.py:445
  3.1 3.5 %collective-permute-start.1 = (bf16[2,176,128]{2,1,0:T(8,128)(2,1)S(1)}, bf16[2,176,128]{2,1,0:T(8,128)(2,1)S(1)}, u32[]{:S(2)}, u32[]{:S(2)}) collective-permute-start(bf16[2,176,128]{2,1,0:T(8,128)(2,1)S(1)} %get-tuple-element.29), channel_id=1, source_target_pairs={{0,28},{4,8},{8,4},{12,16},{16,12},{20,24},{24,20},{28,0},{1,29},{... | collective-permute-start | bytes 270344 | tf_op jit(solution)/shard_map/ppermute | solution.py:446
  6.7 2.6 %collective-permute-start.4 = (bf16[32,8,128]{2,1,0:T(8,128)(2,1)S(1)}, bf16[32,8,128]{2,1,0:T(8,128)(2,1)S(1)}, u32[]{:S(2)}, u32[]{:S(2)}) collective-permute-start(bf16[32,8,128]{2,1,0:T(8,128)(2,1)S(1)} %get-tuple-element.34.refs_3_), channel_id=1, source_target_pairs={{0,2},{1,3},{2,0},{3,1},{4,6},{5,7},{6,4},{7,5},{8,10},{9,11},{10,... | collective-permute-start | bytes 196616 | tf_op jit(solution)/shard_map/ppermute | solution.py:371
  9.3 1.3 %collective-permute-start.3 = (bf16[32,8,128]{2,1,0:T(8,128)(2,1)S(1)}, bf16[32,8,128]{2,1,0:T(8,128)(2,1)S(1)}, u32[]{:S(2)}, u32[]{:S(2)}) collective-permute-start(bf16[32,8,128]{2,1,0:T(8,128)(2,1)S(1)} %get-tuple-element.34.refs_3_), channel_id=1, source_target_pairs={{0,3},{1,2},{2,1},{3,0},{4,7},{5,6},{6,5},{7,4},{8,11},{9,10},{10,... | collective-permute-start | bytes 196616 | tf_op jit(solution)/shard_map/ppermute | solution.py:371
  10.6 0.2 collective-permute-start.2
  10.8 1.1 %pack_columns.1.stage = f32[2,48,128]{2,1,0:T(8,128)S(1)} custom-call(f32[2048,128]{1,0:T(8,128)S(1)} %bitcast.10, f32[768,128]{1,0:T(8,128)S(1)} %bitcast.16, f32[176,128]{1,0:T(8,128)S(1)} %get-tuple-element.27.rate), custom_call_target="tpu_custom_call" | custom-call | bytes 3300000 | tf_op jit(solution)/shard_map/pack_columns/pallas_call | solution.py:448
  11.9 0.0 collective-permute-done.4.refs_6_
  12.0 3.5 %collective-permute-done.3.refs_5_ = bf16[32,8,128]{2,1,0:T(8,128)(2,1)S(1)} collective-permute-done((bf16[32,8,128]{2,1,0:T(8,128)(2,1)S(1)}, bf16[32,8,128]{2,1,0:T(8,128)(2,1)S(1)}, u32[]{:S(2)}, u32[]{:S(2)}) %collective-permute-start.3) | collective-permute-done | bytes 65568 | tf_op jit(solution)/shard_map/ppermute | solution.py:371
  15.4 0.2 collective-permute-done.2.refs_4_
  15.6 0.0 copy-done.1
  15.6 1.5 %remap.1 = (f32[32,8,128]{2,1,0:T(8,128)S(1)}, bf16[304,128]{1,0:T(8,128)(2,1)S(1)}, bf16[304,128]{1,0:T(8,128)(2,1)S(1)}, bf16[256,128]{1,0:T(8,128)(2,1)S(1)}) custom-call(s32[2,48]{1,0:T(2,128)S(4)} %get-tuple-element.32.refs_0_, s32[1,48]{1,0:T(1,128)S(4)} %get-tuple-element.33.refs_1_, bf16[48,128,128]{2,1,0:T(8,128)(2,1)S(1)} %bitcast.13, ...), custom_call_target="tpu_custom_call" | custom-call | bytes 6000000 | tf_op jit(solution)/shard_map/remap/pallas_call | solution.py:461
  17.1 0.0 collective-permute-done.even_in
  17.1 0.0 collective-permute-done.1.odd_in
  17.1 0.2 corners.1
  17.3 0.1 collective-permute-start.5
  17.3 3.4 %collective-permute-start.6 = (bf16[304,128]{1,0:T(8,128)(2,1)S(1)}, bf16[304,128]{1,0:T(8,128)(2,1)S(1)}, u32[]{:S(2)}, u32[]{:S(2)}) collective-permute-start(bf16[304,128]{1,0:T(8,128)(2,1)S(1)} %get-tuple-element.39), channel_id=1, source_target_pairs={{0,3},{1,2},{2,1},{3,0},{4,7},{5,6},{6,5},{7,4},{8,11},{9,10},{10,... | collective-permute-start | bytes 233480 | tf_op jit(solution)/shard_map/ppermute | solution.py:371
  20.7 0.1 collective-permute-start.7
  20.8 2.4 %stencil.1 = (f32[2048,128]{1,0:T(8,128)S(1)}, f32[768,128]{1,0:T(8,128)S(1)}) custom-call(f32[2048,128]{1,0:T(8,128)S(1)} %bitcast.11, f32[768,128]{1,0:T(8,128)S(1)} %bitcast.17, f32[176,128]{1,0:T(8,128)S(1)} %get-tuple-element.27.rate, bf16[2,176,128]{2,1,0:T(8,128)(2,1)S(1)} %collective-permute-done.even_in, ...), custom_call_target="tpu_custom_call" | custom-call | bytes 7500000 | tf_op jit(solution)/shard_map/stencil/pallas_call | solution.py:487
  23.2 0.0 collective-permute-done.5.got_a
  23.2 1.8 %collective-permute-done.6.got_b = bf16[304,128]{1,0:T(8,128)(2,1)S(1)} collective-permute-done((bf16[304,128]{1,0:T(8,128)(2,1)S(1)}, bf16[304,128]{1,0:T(8,128)(2,1)S(1)}, u32[]{:S(2)}, u32[]{:S(2)}) %collective-permute-start.6) | collective-permute-done | bytes 77856 | tf_op jit(solution)/shard_map/ppermute | solution.py:371
  25.0 1.5 %edges.1 = (f32[2048,128]{1,0:T(8,128)}, f32[768,128]{1,0:T(8,128)}, f32[256,128]{1,0:T(8,128)S(1)}) custom-call(s32[1,16]{1,0:T(1,128)S(4)} %get-tuple-element.24.mask, f32[176,128]{1,0:T(8,128)S(1)} %get-tuple-element.27.rate, f32[2048,128]{1,0:T(8,128)S(1)} %get-tuple-element.30.atm, f32[768,128]{1,0:T(8,128)S(1)} %get-tuple-element.31.ocean, ...), custom_call_target="tpu_custom_call" | custom-call | bytes 4500000 | tf_op jit(solution)/shard_map/edges/pallas_call | solution.py:501
  26.6 0.5 %collective-permute-done.7.refs_0_ = bf16[256,128]{1,0:T(8,128)(2,1)S(1)} collective-permute-done((bf16[256,128]{1,0:T(8,128)(2,1)S(1)}, bf16[256,128]{1,0:T(8,128)(2,1)S(1)}, u32[]{:S(2)}, u32[]{:S(2)}) %collective-permute-start.7) | collective-permute-done | bytes 65568 | tf_op jit(solution)/shard_map/ppermute | solution.py:371
  27.1 0.7 %final.1 = (f32[2048,128]{1,0:T(8,128)}, f32[768,128]{1,0:T(8,128)}) custom-call(s32[1,16]{1,0:T(1,128)S(4)} %get-tuple-element.24.mask, f32[256,128]{1,0:T(8,128)S(1)} %get-tuple-element.40.surface, bf16[256,128]{1,0:T(8,128)(2,1)S(1)} %collective-permute-done.7.refs_0_, ...), custom_call_target="tpu_custom_call", output_to_operand_aliasing={{0}: (3, {}), {1}: (4, {})} | custom-call | bytes 2100000 | tf_op jit(solution)/shard_map/final/pallas_call | solution.py:519
Async XLA Ops:
  0.6 1.8 %copy-start.2 = (f32[48,16,128]{2,1,0:T(8,128)S(1)}, f32[48,16,128]{2,1,0:T(8,128)}, u32[]{:S(2)}) copy-start(f32[48,16,128]{2,1,0:T(8,128)} %param.10) | copy-start | bytes 1179652
  0.6 1.8 %copy-start = (f32[128,16,128]{2,1,0:T(8,128)S(1)}, f32[128,16,128]{2,1,0:T(8,128)}, u32[]{:S(2)}) copy-start(f32[128,16,128]{2,1,0:T(8,128)} %param.9) | copy-start | bytes 3145732
  2.4 13.2 %copy-start.1 = (bf16[1,48,128,128]{3,2,1,0:T(8,128)(2,1)S(1)}, bf16[1,48,128,128]{3,2,1,0:T(8,128)(2,1)}, u32[]{:S(2)}) copy-start(bf16[1,48,128,128]{3,2,1,0:T(8,128)(2,1)} %param.14) | copy-start | bytes 4718596
  2.6 14.5 %collective-permute-start = (bf16[2,176,128]{2,1,0:T(8,128)(2,1)S(1)}, bf16[2,176,128]{2,1,0:T(8,128)(2,1)S(1)}, u32[]{:S(2)}, u32[]{:S(2)}) collective-permute-start(bf16[2,176,128]{2,1,0:T(8,128)(2,1)S(1)} %get-tuple-element.28), channel_id=1, source_target_pairs={{0,4},{4,0},{8,12},{12,8},{16,20},{20,16},{24,28},{28,24},{1,5},{5... | collective-permute-start | bytes 270344 | tf_op jit(solution)/shard_map/ppermute | solution.py:445
  3.1 13.9 %collective-permute-start.1 = (bf16[2,176,128]{2,1,0:T(8,128)(2,1)S(1)}, bf16[2,176,128]{2,1,0:T(8,128)(2,1)S(1)}, u32[]{:S(2)}, u32[]{:S(2)}) collective-permute-start(bf16[2,176,128]{2,1,0:T(8,128)(2,1)S(1)} %get-tuple-element.29), channel_id=1, source_target_pairs={{0,28},{4,8},{8,4},{12,16},{16,12},{20,24},{24,20},{28,0},{1,29},{... | collective-permute-start | bytes 270344 | tf_op jit(solution)/shard_map/ppermute | solution.py:446
  6.7 5.3 %collective-permute-start.4 = (bf16[32,8,128]{2,1,0:T(8,128)(2,1)S(1)}, bf16[32,8,128]{2,1,0:T(8,128)(2,1)S(1)}, u32[]{:S(2)}, u32[]{:S(2)}) collective-permute-start(bf16[32,8,128]{2,1,0:T(8,128)(2,1)S(1)} %get-tuple-element.34.refs_3_), channel_id=1, source_target_pairs={{0,2},{1,3},{2,0},{3,1},{4,6},{5,7},{6,4},{7,5},{8,10},{9,11},{10,... | collective-permute-start | bytes 196616 | tf_op jit(solution)/shard_map/ppermute | solution.py:371
  9.3 6.2 %collective-permute-start.3 = (bf16[32,8,128]{2,1,0:T(8,128)(2,1)S(1)}, bf16[32,8,128]{2,1,0:T(8,128)(2,1)S(1)}, u32[]{:S(2)}, u32[]{:S(2)}) collective-permute-start(bf16[32,8,128]{2,1,0:T(8,128)(2,1)S(1)} %get-tuple-element.34.refs_3_), channel_id=1, source_target_pairs={{0,3},{1,2},{2,1},{3,0},{4,7},{5,6},{6,5},{7,4},{8,11},{9,10},{10,... | collective-permute-start | bytes 196616 | tf_op jit(solution)/shard_map/ppermute | solution.py:371
  10.6 5.0 %collective-permute-start.2 = (bf16[32,8,128]{2,1,0:T(8,128)(2,1)S(1)}, bf16[32,8,128]{2,1,0:T(8,128)(2,1)S(1)}, u32[]{:S(2)}, u32[]{:S(2)}) collective-permute-start(bf16[32,8,128]{2,1,0:T(8,128)(2,1)S(1)} %get-tuple-element.34.refs_3_), channel_id=1, source_target_pairs={{0,1},{1,0},{2,3},{3,2},{4,5},{5,4},{6,7},{7,6},{8,9},{9,8},{10,11... | collective-permute-start | bytes 196616 | tf_op jit(solution)/shard_map/ppermute | solution.py:371
  17.3 6.0 %collective-permute-start.5 = (bf16[304,128]{1,0:T(8,128)(2,1)S(1)}, bf16[304,128]{1,0:T(8,128)(2,1)S(1)}, u32[]{:S(2)}, u32[]{:S(2)}) collective-permute-start(bf16[304,128]{1,0:T(8,128)(2,1)S(1)} %get-tuple-element.38), channel_id=1, source_target_pairs={{0,1},{1,0},{2,3},{3,2},{4,5},{5,4},{6,7},{7,6},{8,9},{9,8},{10,11... | collective-permute-start | bytes 233480 | tf_op jit(solution)/shard_map/ppermute | solution.py:371
  17.3 7.7 %collective-permute-start.6 = (bf16[304,128]{1,0:T(8,128)(2,1)S(1)}, bf16[304,128]{1,0:T(8,128)(2,1)S(1)}, u32[]{:S(2)}, u32[]{:S(2)}) collective-permute-start(bf16[304,128]{1,0:T(8,128)(2,1)S(1)} %get-tuple-element.39), channel_id=1, source_target_pairs={{0,3},{1,2},{2,1},{3,0},{4,7},{5,6},{6,5},{7,4},{8,11},{9,10},{10,... | collective-permute-start | bytes 233480 | tf_op jit(solution)/shard_map/ppermute | solution.py:371
  20.7 6.4 %collective-permute-start.7 = (bf16[256,128]{1,0:T(8,128)(2,1)S(1)}, bf16[256,128]{1,0:T(8,128)(2,1)S(1)}, u32[]{:S(2)}, u32[]{:S(2)}) collective-permute-start(bf16[256,128]{1,0:T(8,128)(2,1)S(1)} %get-tuple-element.41), channel_id=1, source_target_pairs={{0,2},{1,3},{2,0},{3,1},{4,6},{5,7},{6,4},{7,5},{8,10},{9,11},{10,... | collective-permute-start | bytes 196616 | tf_op jit(solution)/shard_map/ppermute | solution.py:371

commit v8 on v7

--- a/solution.py
+++ b/solution.py
@@ -194,26 +194,36 @@
     live_count = number[0, 0]
     trans = (((1,), (1,)), ((), ()))
     plain = (((1,), (0,)), ((), ()))
-    group = 8
-    for start in range(0, pairs, group):
-        made = []
-        for k in range(start, min(start + group, pairs)):
-            a = table[0, k]
-            o = table[1, k]
-            at_a = lax.div(a, rows_a) * block + lax.rem(a, rows_a)
-            at_o = lax.div(o, rows_o) * block + rows_a + lax.rem(o, rows_o)
-            live = k < live_count
-            w = weights[k]
-            ta = band[at_a]
-            to = band[at_o]
-            ta = jnp.where(live, ta, jnp.zeros_like(ta))
-            to = jnp.where(live, to, jnp.zeros_like(to))
-            ahead = lax.dot_general(ta, w, plain, preferred_element_type=F32)
-            back = lax.dot_general(to, w, trans, preferred_element_type=F32)
-            made.append((at_a, at_o, ahead, back))
-        for at_a, at_o, ahead, back in made:
-            total[at_o] += ahead
-            total[at_a] += back
+    depth, width = weights.shape[1:]
+
+    def picked(k):
+        a = table[0, k]
+        o = table[1, k]
+        at_a = lax.div(a, rows_a) * block + lax.rem(a, rows_a)
+        at_o = lax.div(o, rows_o) * block + rows_a + lax.rem(o, rows_o)
+        live = k < live_count
+        ta = band[at_a]
+        to = band[at_o]
+        ta = jnp.where(live, ta, jnp.zeros_like(ta))
+        to = jnp.where(live, to, jnp.zeros_like(to))
+        return at_a, at_o, ta, to
+
+    for k in range(0, pairs, 2):
+        first, second = picked(k), picked(k + 1)
+        both = weights[k : k + 2].reshape(2 * depth, width)
+        none = jnp.zeros_like(first[2])
+        left = jnp.concatenate([first[2], none], axis=0)
+        right = jnp.concatenate([none, second[2]], axis=0)
+        ahead = lax.dot_general(
+            jnp.concatenate([left, right], axis=1), both, plain, preferred_element_type=F32
+        )
+        back = lax.dot_general(
+            jnp.concatenate([first[3], second[3]], axis=0), both, trans, preferred_element_type=F32
+        )
+        total[first[1]] += ahead[0:SURF]
+        total[second[1]] += ahead[SURF:]
+        total[first[0]] += back[0:SURF, 0:depth]
+        total[second[0]] += back[SURF:, depth:]
     own_out[...] = total[pl.ds(me * block, block)]
     lanes = weights.shape[2]
     for e, ref in zip(targets, outs):

time: 27.9 us -> 27.3 us (0.978)
  Pallas kernels: 8.51 us -> 7.87 us
    pallas_call x1, Pallas kernels: 1.47 us -> 0.83 us  [interval(): call(functools.partial(remap, tile_count, rows_a, rows_o), 2.0, 12 << 20,...]
  transfers between devices with their start and end apart: 8 -> 8, of which waited for: 4 -> 4; matrix products, arithmetic and copies ran while one was open for 0% -> 0% of each run, Pallas kernels for 23% -> 22%
where the time goes in v8:
time: 27.3 us; the launch traced here: 27.1 us
  starting transfers between devices  11.8 us (43%)
  Pallas kernels  7.87 us (29%)
  waiting for transfers between devices  5.95 us (22%)
  between operations  1.5 us (5%)
    ppermute x6, starting transfers between devices, exchange(): out.append(lax.ppermute(block, 'tile', route))  7.69 us
    ppermute x6, waiting for transfers between devices, exchange(): out.append(lax.ppermute(block, 'tile', route))  5.94 us
    ppermute x1, starting transfers between devices, interval(): odd_in = lax.ppermute(odd_rows, 'comp', odd_pairs)  3.54 us
    pallas_call x1, Pallas kernels, interval(): call(functools.partial(stencil, rows_a, rows_o), 2.5, 8 << 20, in_specs=[...  2.44 us
    pallas_call x1, Pallas kernels, interval(): call(functools.partial(edges, rows_a, rows_o), 1.5, 12 << 20, in_specs=[S...  1.54 us
    pallas_call x1, Pallas kernels, interval(): call(functools.partial(pack_columns, rows_a, rows_o), 1.1, 8 << 20, in_sp...  1.07 us
    pallas_call x1, Pallas kernels, interval(): call(functools.partial(pack_surface, rows_a, rows_o), 0.8, 4 << 20, in_sp...  0.98 us
    pallas_call x1, Pallas kernels, interval(): call(functools.partial(remap, tile_count, rows_a, rows_o), 2.0, 12 << 20,...  0.83 us
  transfers between devices with their start and end apart: 8, of which 4 were waited for; matrix products, arithmetic and copies ran while one was open for 0% of the time, Pallas kernels for 22%

profile of v8, /device:TPU:0, one launch (start us, length us, event | category | flops | bytes accessed | tf_op | source)
XLA Modules:
  0.0 27.1 jit_solution(6924328298008123755)
XLA Ops:
  0.6 0.0 copy-start.2
  0.6 0.0 copy-start
  1.4 1.0 %pack_surface.1 = (bf16[32,8,128]{2,1,0:T(8,128)(2,1)S(1)}, f32[1,128]{1,0:T(1,128)S(1)}, f32[1,48]{1,0:T(1,128)S(1)}, s32[2,48]{1,0:T(2,128)S(4)}, s32[1,16]{1,0:T(1,128)S(4)}) custom-call(f32[2048,128]{1,0:T(8,128)} %bitcast.8, f32[768,128]{1,0:T(8,128)} %bitcast.14, s32[1,16]{1,0:T(1,128)} %bitcast.20, s32[1,48]{1,0:T(1,128)} %refs_3_.1, ...), custom_call_target="tpu_custom_call" | custom-call | bytes 2400000 | tf_op jit(solution)/shard_map/pack_surface/pallas_call | solution.py:410
  2.4 0.0 copy-done.2
  2.4 0.0 copy-done
  2.4 0.0 copy-start.1
  2.4 0.1 prepare.1
  2.6 0.6 %collective-permute-start = (bf16[2,176,128]{2,1,0:T(8,128)(2,1)S(1)}, bf16[2,176,128]{2,1,0:T(8,128)(2,1)S(1)}, u32[]{:S(2)}, u32[]{:S(2)}) collective-permute-start(bf16[2,176,128]{2,1,0:T(8,128)(2,1)S(1)} %get-tuple-element.28), channel_id=1, source_target_pairs={{0,4},{4,0},{8,12},{12,8},{16,20},{20,16},{24,28},{28,24},{1,5},{5... | collective-permute-start | bytes 270344 | tf_op jit(solution)/shard_map/ppermute | solution.py:455
  3.1 3.5 %collective-permute-start.1 = (bf16[2,176,128]{2,1,0:T(8,128)(2,1)S(1)}, bf16[2,176,128]{2,1,0:T(8,128)(2,1)S(1)}, u32[]{:S(2)}, u32[]{:S(2)}) collective-permute-start(bf16[2,176,128]{2,1,0:T(8,128)(2,1)S(1)} %get-tuple-element.29), channel_id=1, source_target_pairs={{0,28},{4,8},{8,4},{12,16},{16,12},{20,24},{24,20},{28,0},{1,29},{... | collective-permute-start | bytes 270344 | tf_op jit(solution)/shard_map/ppermute | solution.py:456
  6.7 2.6 %collective-permute-start.4 = (bf16[32,8,128]{2,1,0:T(8,128)(2,1)S(1)}, bf16[32,8,128]{2,1,0:T(8,128)(2,1)S(1)}, u32[]{:S(2)}, u32[]{:S(2)}) collective-permute-start(bf16[32,8,128]{2,1,0:T(8,128)(2,1)S(1)} %get-tuple-element.34.refs_3_), channel_id=1, source_target_pairs={{0,2},{1,3},{2,0},{3,1},{4,6},{5,7},{6,4},{7,5},{8,10},{9,11},{10,... | collective-permute-start | bytes 196616 | tf_op jit(solution)/shard_map/ppermute | solution.py:381
  9.3 1.3 %collective-permute-start.3 = (bf16[32,8,128]{2,1,0:T(8,128)(2,1)S(1)}, bf16[32,8,128]{2,1,0:T(8,128)(2,1)S(1)}, u32[]{:S(2)}, u32[]{:S(2)}) collective-permute-start(bf16[32,8,128]{2,1,0:T(8,128)(2,1)S(1)} %get-tuple-element.34.refs_3_), channel_id=1, source_target_pairs={{0,3},{1,2},{2,1},{3,0},{4,7},{5,6},{6,5},{7,4},{8,11},{9,10},{10,... | collective-permute-start | bytes 196616 | tf_op jit(solution)/shard_map/ppermute | solution.py:381
  10.6 0.2 collective-permute-start.2
  10.8 1.1 %pack_columns.1.stage = f32[2,48,128]{2,1,0:T(8,128)S(1)} custom-call(f32[2048,128]{1,0:T(8,128)S(1)} %bitcast.10, f32[768,128]{1,0:T(8,128)S(1)} %bitcast.16, f32[176,128]{1,0:T(8,128)S(1)} %get-tuple-element.27.rate), custom_call_target="tpu_custom_call" | custom-call | bytes 3300000 | tf_op jit(solution)/shard_map/pack_columns/pallas_call | solution.py:458
  11.9 0.0 collective-permute-done.4.refs_6_
  12.0 3.5 %collective-permute-done.3.refs_5_ = bf16[32,8,128]{2,1,0:T(8,128)(2,1)S(1)} collective-permute-done((bf16[32,8,128]{2,1,0:T(8,128)(2,1)S(1)}, bf16[32,8,128]{2,1,0:T(8,128)(2,1)S(1)}, u32[]{:S(2)}, u32[]{:S(2)}) %collective-permute-start.3) | collective-permute-done | bytes 65568 | tf_op jit(solution)/shard_map/ppermute | solution.py:381
  15.4 0.2 collective-permute-done.2.refs_4_
  15.6 0.0 copy-done.1
  15.6 0.8 %remap.1 = (f32[32,8,128]{2,1,0:T(8,128)S(1)}, bf16[304,128]{1,0:T(8,128)(2,1)S(1)}, bf16[304,128]{1,0:T(8,128)(2,1)S(1)}, bf16[256,128]{1,0:T(8,128)(2,1)S(1)}) custom-call(s32[2,48]{1,0:T(2,128)S(4)} %get-tuple-element.32.refs_0_, s32[1,48]{1,0:T(1,128)S(4)} %get-tuple-element.33.refs_1_, bf16[48,128,128]{2,1,0:T(8,128)(2,1)S(1)} %bitcast.13, ...), custom_call_target="tpu_custom_call" | custom-call | bytes 6000000 | tf_op jit(solution)/shard_map/remap/pallas_call | solution.py:471
  16.4 0.0 collective-permute-done.even_in
  16.4 0.0 collective-permute-done.1.odd_in
  16.4 0.2 corners.1
  16.6 0.1 collective-permute-start.5
  16.7 3.4 %collective-permute-start.6 = (bf16[304,128]{1,0:T(8,128)(2,1)S(1)}, bf16[304,128]{1,0:T(8,128)(2,1)S(1)}, u32[]{:S(2)}, u32[]{:S(2)}) collective-permute-start(bf16[304,128]{1,0:T(8,128)(2,1)S(1)} %get-tuple-element.39), channel_id=1, source_target_pairs={{0,3},{1,2},{2,1},{3,0},{4,7},{5,6},{6,5},{7,4},{8,11},{9,10},{10,... | collective-permute-start | bytes 233480 | tf_op jit(solution)/shard_map/ppermute | solution.py:381
  20.0 0.1 collective-permute-start.7
  20.1 2.4 %stencil.1 = (f32[2048,128]{1,0:T(8,128)S(1)}, f32[768,128]{1,0:T(8,128)S(1)}) custom-call(f32[2048,128]{1,0:T(8,128)S(1)} %bitcast.11, f32[768,128]{1,0:T(8,128)S(1)} %bitcast.17, f32[176,128]{1,0:T(8,128)S(1)} %get-tuple-element.27.rate, bf16[2,176,128]{2,1,0:T(8,128)(2,1)S(1)} %collective-permute-done.even_in, ...), custom_call_target="tpu_custom_call" | custom-call | bytes 7500000 | tf_op jit(solution)/shard_map/stencil/pallas_call | solution.py:497
  22.6 0.0 collective-permute-done.5.got_a
  22.6 1.8 %collective-permute-done.6.got_b = bf16[304,128]{1,0:T(8,128)(2,1)S(1)} collective-permute-done((bf16[304,128]{1,0:T(8,128)(2,1)S(1)}, bf16[304,128]{1,0:T(8,128)(2,1)S(1)}, u32[]{:S(2)}, u32[]{:S(2)}) %collective-permute-start.6) | collective-permute-done | bytes 77856 | tf_op jit(solution)/shard_map/ppermute | solution.py:381
  24.4 1.5 %edges.1 = (f32[2048,128]{1,0:T(8,128)}, f32[768,128]{1,0:T(8,128)}, f32[256,128]{1,0:T(8,128)S(1)}) custom-call(s32[1,16]{1,0:T(1,128)S(4)} %get-tuple-element.24.mask, f32[176,128]{1,0:T(8,128)S(1)} %get-tuple-element.27.rate, f32[2048,128]{1,0:T(8,128)S(1)} %get-tuple-element.30.atm, f32[768,128]{1,0:T(8,128)S(1)} %get-tuple-element.31.ocean, ...), custom_call_target="tpu_custom_call" | custom-call | bytes 4500000 | tf_op jit(solution)/shard_map/edges/pallas_call | solution.py:511
  25.9 0.5 %collective-permute-done.7.refs_0_ = bf16[256,128]{1,0:T(8,128)(2,1)S(1)} collective-permute-done((bf16[256,128]{1,0:T(8,128)(2,1)S(1)}, bf16[256,128]{1,0:T(8,128)(2,1)S(1)}, u32[]{:S(2)}, u32[]{:S(2)}) %collective-permute-start.7) | collective-permute-done | bytes 65568 | tf_op jit(solution)/shard_map/ppermute | solution.py:381
  26.4 0.7 %final.1 = (f32[2048,128]{1,0:T(8,128)}, f32[768,128]{1,0:T(8,128)}) custom-call(s32[1,16]{1,0:T(1,128)S(4)} %get-tuple-element.24.mask, f32[256,128]{1,0:T(8,128)S(1)} %get-tuple-element.40.surface, bf16[256,128]{1,0:T(8,128)(2,1)S(1)} %collective-permute-done.7.refs_0_, ...), custom_call_target="tpu_custom_call", output_to_operand_aliasing={{0}: (3, {}), {1}: (4, {})} | custom-call | bytes 2100000 | tf_op jit(solution)/shard_map/final/pallas_call | solution.py:529
Async XLA Ops:
  0.6 1.8 %copy-start.2 = (f32[48,16,128]{2,1,0:T(8,128)S(1)}, f32[48,16,128]{2,1,0:T(8,128)}, u32[]{:S(2)}) copy-start(f32[48,16,128]{2,1,0:T(8,128)} %param.10) | copy-start | bytes 1179652
  0.6 1.8 %copy-start = (f32[128,16,128]{2,1,0:T(8,128)S(1)}, f32[128,16,128]{2,1,0:T(8,128)}, u32[]{:S(2)}) copy-start(f32[128,16,128]{2,1,0:T(8,128)} %param.9) | copy-start | bytes 3145732
  2.4 13.2 %copy-start.1 = (bf16[1,48,128,128]{3,2,1,0:T(8,128)(2,1)S(1)}, bf16[1,48,128,128]{3,2,1,0:T(8,128)(2,1)}, u32[]{:S(2)}) copy-start(bf16[1,48,128,128]{3,2,1,0:T(8,128)(2,1)} %param.14) | copy-start | bytes 4718596
  2.6 13.8 %collective-permute-start = (bf16[2,176,128]{2,1,0:T(8,128)(2,1)S(1)}, bf16[2,176,128]{2,1,0:T(8,128)(2,1)S(1)}, u32[]{:S(2)}, u32[]{:S(2)}) collective-permute-start(bf16[2,176,128]{2,1,0:T(8,128)(2,1)S(1)} %get-tuple-element.28), channel_id=1, source_target_pairs={{0,4},{4,0},{8,12},{12,8},{16,20},{20,16},{24,28},{28,24},{1,5},{5... | collective-permute-start | bytes 270344 | tf_op jit(solution)/shard_map/ppermute | solution.py:455
  3.1 13.3 %collective-permute-start.1 = (bf16[2,176,128]{2,1,0:T(8,128)(2,1)S(1)}, bf16[2,176,128]{2,1,0:T(8,128)(2,1)S(1)}, u32[]{:S(2)}, u32[]{:S(2)}) collective-permute-start(bf16[2,176,128]{2,1,0:T(8,128)(2,1)S(1)} %get-tuple-element.29), channel_id=1, source_target_pairs={{0,28},{4,8},{8,4},{12,16},{16,12},{20,24},{24,20},{28,0},{1,29},{... | collective-permute-start | bytes 270344 | tf_op jit(solution)/shard_map/ppermute | solution.py:456
  6.7 5.3 %collective-permute-start.4 = (bf16[32,8,128]{2,1,0:T(8,128)(2,1)S(1)}, bf16[32,8,128]{2,1,0:T(8,128)(2,1)S(1)}, u32[]{:S(2)}, u32[]{:S(2)}) collective-permute-start(bf16[32,8,128]{2,1,0:T(8,128)(2,1)S(1)} %get-tuple-element.34.refs_3_), channel_id=1, source_target_pairs={{0,2},{1,3},{2,0},{3,1},{4,6},{5,7},{6,4},{7,5},{8,10},{9,11},{10,... | collective-permute-start | bytes 196616 | tf_op jit(solution)/shard_map/ppermute | solution.py:381
  9.3 6.2 %collective-permute-start.3 = (bf16[32,8,128]{2,1,0:T(8,128)(2,1)S(1)}, bf16[32,8,128]{2,1,0:T(8,128)(2,1)S(1)}, u32[]{:S(2)}, u32[]{:S(2)}) collective-permute-start(bf16[32,8,128]{2,1,0:T(8,128)(2,1)S(1)} %get-tuple-element.34.refs_3_), channel_id=1, source_target_pairs={{0,3},{1,2},{2,1},{3,0},{4,7},{5,6},{6,5},{7,4},{8,11},{9,10},{10,... | collective-permute-start | bytes 196616 | tf_op jit(solution)/shard_map/ppermute | solution.py:381
  10.6 5.0 %collective-permute-start.2 = (bf16[32,8,128]{2,1,0:T(8,128)(2,1)S(1)}, bf16[32,8,128]{2,1,0:T(8,128)(2,1)S(1)}, u32[]{:S(2)}, u32[]{:S(2)}) collective-permute-start(bf16[32,8,128]{2,1,0:T(8,128)(2,1)S(1)} %get-tuple-element.34.refs_3_), channel_id=1, source_target_pairs={{0,1},{1,0},{2,3},{3,2},{4,5},{5,4},{6,7},{7,6},{8,9},{9,8},{10,11... | collective-permute-start | bytes 196616 | tf_op jit(solution)/shard_map/ppermute | solution.py:381
  16.6 6.0 %collective-permute-start.5 = (bf16[304,128]{1,0:T(8,128)(2,1)S(1)}, bf16[304,128]{1,0:T(8,128)(2,1)S(1)}, u32[]{:S(2)}, u32[]{:S(2)}) collective-permute-start(bf16[304,128]{1,0:T(8,128)(2,1)S(1)} %get-tuple-element.38), channel_id=1, source_target_pairs={{0,1},{1,0},{2,3},{3,2},{4,5},{5,4},{6,7},{7,6},{8,9},{9,8},{10,11... | collective-permute-start | bytes 233480 | tf_op jit(solution)/shard_map/ppermute | solution.py:381
  16.7 7.7 %collective-permute-start.6 = (bf16[304,128]{1,0:T(8,128)(2,1)S(1)}, bf16[304,128]{1,0:T(8,128)(2,1)S(1)}, u32[]{:S(2)}, u32[]{:S(2)}) collective-permute-start(bf16[304,128]{1,0:T(8,128)(2,1)S(1)} %get-tuple-element.39), channel_id=1, source_target_pairs={{0,3},{1,2},{2,1},{3,0},{4,7},{5,6},{6,5},{7,4},{8,11},{9,10},{10,... | collective-permute-start | bytes 233480 | tf_op jit(solution)/shard_map/ppermute | solution.py:381
  20.0 6.4 %collective-permute-start.7 = (bf16[256,128]{1,0:T(8,128)(2,1)S(1)}, bf16[256,128]{1,0:T(8,128)(2,1)S(1)}, u32[]{:S(2)}, u32[]{:S(2)}) collective-permute-start(bf16[256,128]{1,0:T(8,128)(2,1)S(1)} %get-tuple-element.41), channel_id=1, source_target_pairs={{0,2},{1,3},{2,0},{3,1},{4,6},{5,7},{6,4},{7,5},{8,10},{9,11},{10,... | collective-permute-start | bytes 196616 | tf_op jit(solution)/shard_map/ppermute | solution.py:381

commit v9 on v8

--- a/solution.py
+++ b/solution.py
@@ -108,7 +108,7 @@
     return north, south
 
 
-def pack_columns(rows_a, rows_o, atm, ocean, rate, out, spread):
+def pack_columns(rows_a, rows_o, atm, ocean, rate, out, lined, spread):
     tile_parity = lax.rem(lax.axis_index("tile"), 2)
     lanes = atm.shape[1]
     row = lax.broadcasted_iota(jnp.int32, (8, lanes), 0)
@@ -130,6 +130,7 @@
             square = rho * rho
             q = [ref[pl.ds(c * rows + r, 8, stride=rows), :] for r in range(rows)]
             for r in range(rows):
+                lined[r, at + c : at + c + 8, :] = q[r]
                 far = square * q[r]
                 beside = q[1] if r == 0 else q[r - 1]
                 if 0 < r < rows - 1:
@@ -177,6 +178,12 @@
     out_b[behind:, :] = joined[1].astype(BF16)
 
 
+def quotient(number, divisor):
+    if divisor & (divisor - 1) == 0:
+        return lax.shift_right_logical(number, divisor.bit_length() - 1)
+    return lax.div(number, divisor)
+
+
 def remap(tile_count, rows_a, rows_o, *refs):
     table, number, weights, own = refs[:4]
     got = refs[4 : 3 + tile_count]
@@ -199,8 +206,8 @@
     def picked(k):
         a = table[0, k]
         o = table[1, k]
-        at_a = lax.div(a, rows_a) * block + lax.rem(a, rows_a)
-        at_o = lax.div(o, rows_o) * block + rows_a + lax.rem(o, rows_o)
+        at_a = a + quotient(a, rows_a) * rows_o
+        at_o = o + rows_a + quotient(o, rows_o) * rows_a
         live = k < live_count
         ta = band[at_a]
         to = band[at_o]
@@ -231,22 +238,22 @@
         ref[0 : block * SURF, :] = part.reshape(block * SURF, lanes)
 
 
-def stencil(rows_a, rows_o, atm, ocean, rate, even_in, odd_in, atm_out, ocean_out):
+def stencil(rows_a, rows_o, lined, rate, even_in, odd_in, atm_out, ocean_out):
     comp = lax.axis_index("comp")
-    lanes = atm.shape[1]
+    lanes = lined.shape[2]
     lane = lax.broadcasted_iota(jnp.int32, (8, lanes), 1)
     at_west = lane == 0
     at_east = lane == lanes - 1
     keep_north = jnp.where(comp == 0, 0.0, 1.0).astype(F32)
     keep_south = jnp.where(comp == lax.axis_size("comp") - 1, 0.0, 1.0).astype(F32)
     at = 0
-    for ref, rows, out in ((atm, rows_a, atm_out), (ocean, rows_o, ocean_out)):
-        channels = ref.shape[0] // rows
+    for rows, out in ((rows_a, atm_out), (rows_o, ocean_out)):
+        channels = out.shape[0] // rows
         for c in range(0, channels, 8):
             rho = rate[at + c : at + c + 8, :]
             own = 1.0 - 4.0 * rho
             north, south = halo_rows(comp, even_in, odd_in, at + c)
-            q = north + [ref[pl.ds(c * rows + r, 8, stride=rows), :] for r in range(rows)] + south
+            q = north + [lined[r, at + c : at + c + 8, :] for r in range(rows)] + south
             p = []
             for i in range(1, rows + 3):
                 west = jnp.where(at_west, 0.0, pltpu.roll(q[i], 1, 1))
@@ -455,13 +462,16 @@
     even_in = lax.ppermute(even_rows, "comp", even_pairs)
     odd_in = lax.ppermute(odd_rows, "comp", odd_pairs)
 
-    stage = call(
+    stage, lined = call(
         functools.partial(pack_columns, rows_a, rows_o),
         1.1,
         8 << 20,
         in_specs=[VMEM] * 3,
-        out_specs=VMEM,
-        out_shape=pltpu.VMEM((2, extra, lanes), F32),
+        out_specs=[VMEM, VMEM],
+        out_shape=[
+            pltpu.VMEM((2, extra, lanes), F32),
+            pltpu.VMEM((max(rows_a, rows_o), channels, lanes), F32),
+        ],
         scratch_shapes=[pltpu.VMEM((channels_a * rows_a + channels_o * rows_o, lanes), F32)],
         name="pack_columns",
     )(atm, ocean, rate)
@@ -498,14 +508,14 @@
         functools.partial(stencil, rows_a, rows_o),
         2.5,
         8 << 20,
-        in_specs=[VMEM] * 5,
+        in_specs=[VMEM] * 4,
         out_specs=[VMEM, VMEM],
         out_shape=[
             jax.ShapeDtypeStruct(atm.shape, F32),
             jax.ShapeDtypeStruct(ocean.shape, F32),
         ],
         name="stencil",
-    )(atm, ocean, rate, even_in, odd_in)
+    )(lined, rate, even_in, odd_in)
 
     result = [pltpu.HBM(atm.shape, F32), pltpu.HBM(ocean.shape, F32)]
     atm_next, ocean_next, base = call(

time: 27.3 us -> 27.5 us (level)
  no operation moved by 1% of the time
where the time goes in v9:
time: 27.5 us; the launch traced here: 27.3 us
  starting transfers between devices  11.8 us (43%)
  Pallas kernels  7.97 us (29%)
  waiting for transfers between devices  6.02 us (22%)
  between operations  1.5 us (5%)
    ppermute x6, starting transfers between devices, exchange(): out.append(lax.ppermute(block, 'tile', route))  7.7 us
    ppermute x6, waiting for transfers between devices, exchange(): out.append(lax.ppermute(block, 'tile', route))  6.02 us
    ppermute x1, starting transfers between devices, interval(): odd_in = lax.ppermute(odd_rows, 'comp', odd_pairs)  3.54 us
    pallas_call x1, Pallas kernels, interval(): call(functools.partial(stencil, rows_a, rows_o), 2.5, 8 << 20, in_specs=[...  2.44 us
    pallas_call x1, Pallas kernels, interval(): call(functools.partial(edges, rows_a, rows_o), 1.5, 12 << 20, in_specs=[S...  1.54 us
    pallas_call x1, Pallas kernels, interval(): call(functools.partial(pack_columns, rows_a, rows_o), 1.1, 8 << 20, in_sp...  1.18 us
    pallas_call x1, Pallas kernels, interval(): call(functools.partial(pack_surface, rows_a, rows_o), 0.8, 4 << 20, in_sp...  0.98 us
    pallas_call x1, Pallas kernels, interval(): call(functools.partial(remap, tile_count, rows_a, rows_o), 2.0, 12 << 20,...  0.82 us
  transfers between devices with their start and end apart: 8, of which 4 were waited for; matrix products, arithmetic and copies ran while one was open for 0% of the time, Pallas kernels for 22%

profile of v9, /device:TPU:0, one launch (start us, length us, event | category | flops | bytes accessed | tf_op | source)
XLA Modules:
  0.0 27.3 jit_solution(12682045202554683911)
XLA Ops:
  0.6 0.0 copy-start
  0.6 0.0 copy-start.2
  1.4 1.0 %pack_surface.1 = (bf16[32,8,128]{2,1,0:T(8,128)(2,1)S(1)}, f32[1,128]{1,0:T(1,128)S(1)}, f32[1,48]{1,0:T(1,128)S(1)}, s32[2,48]{1,0:T(2,128)S(4)}, s32[1,16]{1,0:T(1,128)S(4)}) custom-call(f32[2048,128]{1,0:T(8,128)} %bitcast.8, f32[768,128]{1,0:T(8,128)} %bitcast.13, s32[1,16]{1,0:T(1,128)} %bitcast.18, s32[1,48]{1,0:T(1,128)} %refs_3_.1, ...), custom_call_target="tpu_custom_call" | custom-call | bytes 2400000 | tf_op jit(solution)/shard_map/pack_surface/pallas_call | solution.py:417
  2.4 0.0 copy-done
  2.4 0.0 copy-done.2
  2.4 0.0 copy-start.1
  2.4 0.1 prepare.1
  2.6 0.6 %collective-permute-start = (bf16[2,176,128]{2,1,0:T(8,128)(2,1)S(1)}, bf16[2,176,128]{2,1,0:T(8,128)(2,1)S(1)}, u32[]{:S(2)}, u32[]{:S(2)}) collective-permute-start(bf16[2,176,128]{2,1,0:T(8,128)(2,1)S(1)} %get-tuple-element.31), channel_id=1, source_target_pairs={{0,4},{4,0},{8,12},{12,8},{16,20},{20,16},{24,28},{28,24},{1,5},{5... | collective-permute-start | bytes 270344 | tf_op jit(solution)/shard_map/ppermute | solution.py:462
  3.1 3.5 %collective-permute-start.1 = (bf16[2,176,128]{2,1,0:T(8,128)(2,1)S(1)}, bf16[2,176,128]{2,1,0:T(8,128)(2,1)S(1)}, u32[]{:S(2)}, u32[]{:S(2)}) collective-permute-start(bf16[2,176,128]{2,1,0:T(8,128)(2,1)S(1)} %get-tuple-element.32), channel_id=1, source_target_pairs={{0,28},{4,8},{8,4},{12,16},{16,12},{20,24},{24,20},{28,0},{1,29},{... | collective-permute-start | bytes 270344 | tf_op jit(solution)/shard_map/ppermute | solution.py:463
  6.7 1.6 %collective-permute-start.2 = (bf16[32,8,128]{2,1,0:T(8,128)(2,1)S(1)}, bf16[32,8,128]{2,1,0:T(8,128)(2,1)S(1)}, u32[]{:S(2)}, u32[]{:S(2)}) collective-permute-start(bf16[32,8,128]{2,1,0:T(8,128)(2,1)S(1)} %get-tuple-element.37.refs_3_), channel_id=1, source_target_pairs={{0,1},{1,0},{2,3},{3,2},{4,5},{5,4},{6,7},{7,6},{8,9},{9,8},{10,11... | collective-permute-start | bytes 196616 | tf_op jit(solution)/shard_map/ppermute | solution.py:388
  8.3 2.5 %collective-permute-start.3 = (bf16[32,8,128]{2,1,0:T(8,128)(2,1)S(1)}, bf16[32,8,128]{2,1,0:T(8,128)(2,1)S(1)}, u32[]{:S(2)}, u32[]{:S(2)}) collective-permute-start(bf16[32,8,128]{2,1,0:T(8,128)(2,1)S(1)} %get-tuple-element.37.refs_3_), channel_id=1, source_target_pairs={{0,3},{1,2},{2,1},{3,0},{4,7},{5,6},{6,5},{7,4},{8,11},{9,10},{10,... | collective-permute-start | bytes 196616 | tf_op jit(solution)/shard_map/ppermute | solution.py:388
  10.7 0.1 collective-permute-start.4
  10.8 1.2 %pack_columns.1 = (f32[2,48,128]{2,1,0:T(8,128)S(1)}, f32[16,176,128]{2,1,0:T(8,128)S(1)}) custom-call(f32[2048,128]{1,0:T(8,128)S(1)} %bitcast.10, f32[768,128]{1,0:T(8,128)S(1)} %bitcast.15, f32[176,128]{1,0:T(8,128)S(1)} %get-tuple-element.29.rate), custom_call_target="tpu_custom_call" | custom-call | bytes 3300000 | tf_op jit(solution)/shard_map/pack_columns/pallas_call | solution.py:465
  12.0 0.0 collective-permute-done.2.refs_4_
  12.0 2.4 %collective-permute-done.3.refs_5_ = bf16[32,8,128]{2,1,0:T(8,128)(2,1)S(1)} collective-permute-done((bf16[32,8,128]{2,1,0:T(8,128)(2,1)S(1)}, bf16[32,8,128]{2,1,0:T(8,128)(2,1)S(1)}, u32[]{:S(2)}, u32[]{:S(2)}) %collective-permute-start.3) | collective-permute-done | bytes 65568 | tf_op jit(solution)/shard_map/ppermute | solution.py:388
  14.5 2.1 %collective-permute-done.4.refs_6_ = bf16[32,8,128]{2,1,0:T(8,128)(2,1)S(1)} collective-permute-done((bf16[32,8,128]{2,1,0:T(8,128)(2,1)S(1)}, bf16[32,8,128]{2,1,0:T(8,128)(2,1)S(1)}, u32[]{:S(2)}, u32[]{:S(2)}) %collective-permute-start.4) | collective-permute-done | bytes 65568 | tf_op jit(solution)/shard_map/ppermute | solution.py:388
  16.6 0.0 copy-done.1
  16.6 0.8 %remap.1 = (f32[32,8,128]{2,1,0:T(8,128)S(1)}, bf16[304,128]{1,0:T(8,128)(2,1)S(1)}, bf16[304,128]{1,0:T(8,128)(2,1)S(1)}, bf16[256,128]{1,0:T(8,128)(2,1)S(1)}) custom-call(s32[2,48]{1,0:T(2,128)S(4)} %get-tuple-element.35.refs_0_, s32[1,48]{1,0:T(1,128)S(4)} %get-tuple-element.36.refs_1_, bf16[48,128,128]{2,1,0:T(8,128)(2,1)S(1)} %bitcast.12, ...), custom_call_target="tpu_custom_call" | custom-call | bytes 6000000 | tf_op jit(solution)/shard_map/remap/pallas_call | solution.py:481
  17.4 0.0 collective-permute-done.even_in
  17.4 0.0 collective-permute-done.1.odd_in
  17.4 0.2 corners.1
  17.6 0.1 collective-permute-start.5
  17.7 2.4 %collective-permute-start.6 = (bf16[304,128]{1,0:T(8,128)(2,1)S(1)}, bf16[304,128]{1,0:T(8,128)(2,1)S(1)}, u32[]{:S(2)}, u32[]{:S(2)}) collective-permute-start(bf16[304,128]{1,0:T(8,128)(2,1)S(1)} %get-tuple-element.43), channel_id=1, source_target_pairs={{0,3},{1,2},{2,1},{3,0},{4,7},{5,6},{6,5},{7,4},{8,11},{9,10},{10,... | collective-permute-start | bytes 233480 | tf_op jit(solution)/shard_map/ppermute | solution.py:388
  20.2 1.0 %collective-permute-start.7 = (bf16[256,128]{1,0:T(8,128)(2,1)S(1)}, bf16[256,128]{1,0:T(8,128)(2,1)S(1)}, u32[]{:S(2)}, u32[]{:S(2)}) collective-permute-start(bf16[256,128]{1,0:T(8,128)(2,1)S(1)} %get-tuple-element.45), channel_id=1, source_target_pairs={{0,2},{1,3},{2,0},{3,1},{4,6},{5,7},{6,4},{7,5},{8,10},{9,11},{10,... | collective-permute-start | bytes 196616 | tf_op jit(solution)/shard_map/ppermute | solution.py:388
  21.2 2.4 %stencil.1 = (f32[2048,128]{1,0:T(8,128)S(1)}, f32[768,128]{1,0:T(8,128)S(1)}) custom-call(f32[16,176,128]{2,1,0:T(8,128)S(1)} %get-tuple-element.30.lined, f32[176,128]{1,0:T(8,128)S(1)} %get-tuple-element.29.rate, bf16[2,176,128]{2,1,0:T(8,128)(2,1)S(1)} %collective-permute-done.even_in, bf16[2,176,128]{2,1,0:T(8,128)(2,1)S(1)} %collective-permute-done.1.odd_in), custom_call_target="tpu_custom_call" | custom-call | bytes 7500000 | tf_op jit(solution)/shard_map/stencil/pallas_call | solution.py:507
  23.6 0.0 collective-permute-done.5.got_a
  23.6 0.5 %collective-permute-done.6.got_b = bf16[304,128]{1,0:T(8,128)(2,1)S(1)} collective-permute-done((bf16[304,128]{1,0:T(8,128)(2,1)S(1)}, bf16[304,128]{1,0:T(8,128)(2,1)S(1)}, u32[]{:S(2)}, u32[]{:S(2)}) %collective-permute-start.6) | collective-permute-done | bytes 77856 | tf_op jit(solution)/shard_map/ppermute | solution.py:388
  24.1 1.5 %edges.1 = (f32[2048,128]{1,0:T(8,128)}, f32[768,128]{1,0:T(8,128)}, f32[256,128]{1,0:T(8,128)S(1)}) custom-call(s32[1,16]{1,0:T(1,128)S(4)} %get-tuple-element.26.mask, f32[176,128]{1,0:T(8,128)S(1)} %get-tuple-element.29.rate, f32[2048,128]{1,0:T(8,128)S(1)} %get-tuple-element.33.atm, f32[768,128]{1,0:T(8,128)S(1)} %get-tuple-element.34.ocean, ...), custom_call_target="tpu_custom_call" | custom-call | bytes 4500000 | tf_op jit(solution)/shard_map/edges/pallas_call | solution.py:521
  25.6 1.0 %collective-permute-done.7.refs_0_ = bf16[256,128]{1,0:T(8,128)(2,1)S(1)} collective-permute-done((bf16[256,128]{1,0:T(8,128)(2,1)S(1)}, bf16[256,128]{1,0:T(8,128)(2,1)S(1)}, u32[]{:S(2)}, u32[]{:S(2)}) %collective-permute-start.7) | collective-permute-done | bytes 65568 | tf_op jit(solution)/shard_map/ppermute | solution.py:388
  26.6 0.7 %final.1 = (f32[2048,128]{1,0:T(8,128)}, f32[768,128]{1,0:T(8,128)}) custom-call(s32[1,16]{1,0:T(1,128)S(4)} %get-tuple-element.26.mask, f32[256,128]{1,0:T(8,128)S(1)} %get-tuple-element.44.surface, bf16[256,128]{1,0:T(8,128)(2,1)S(1)} %collective-permute-done.7.refs_0_, ...), custom_call_target="tpu_custom_call", output_to_operand_aliasing={{0}: (3, {}), {1}: (4, {})} | custom-call | bytes 2100000 | tf_op jit(solution)/shard_map/final/pallas_call | solution.py:539
Async XLA Ops:
  0.6 1.8 %copy-start = (f32[128,16,128]{2,1,0:T(8,128)S(1)}, f32[128,16,128]{2,1,0:T(8,128)}, u32[]{:S(2)}) copy-start(f32[128,16,128]{2,1,0:T(8,128)} %param.9) | copy-start | bytes 3145732
  0.6 1.8 %copy-start.2 = (f32[48,16,128]{2,1,0:T(8,128)S(1)}, f32[48,16,128]{2,1,0:T(8,128)}, u32[]{:S(2)}) copy-start(f32[48,16,128]{2,1,0:T(8,128)} %param.10) | copy-start | bytes 1179652
  2.4 14.2 %copy-start.1 = (bf16[1,48,128,128]{3,2,1,0:T(8,128)(2,1)S(1)}, bf16[1,48,128,128]{3,2,1,0:T(8,128)(2,1)}, u32[]{:S(2)}) copy-start(bf16[1,48,128,128]{3,2,1,0:T(8,128)(2,1)} %param.14) | copy-start | bytes 4718596
  2.6 14.9 %collective-permute-start = (bf16[2,176,128]{2,1,0:T(8,128)(2,1)S(1)}, bf16[2,176,128]{2,1,0:T(8,128)(2,1)S(1)}, u32[]{:S(2)}, u32[]{:S(2)}) collective-permute-start(bf16[2,176,128]{2,1,0:T(8,128)(2,1)S(1)} %get-tuple-element.31), channel_id=1, source_target_pairs={{0,4},{4,0},{8,12},{12,8},{16,20},{20,16},{24,28},{28,24},{1,5},{5... | collective-permute-start | bytes 270344 | tf_op jit(solution)/shard_map/ppermute | solution.py:462
  3.1 14.3 %collective-permute-start.1 = (bf16[2,176,128]{2,1,0:T(8,128)(2,1)S(1)}, bf16[2,176,128]{2,1,0:T(8,128)(2,1)S(1)}, u32[]{:S(2)}, u32[]{:S(2)}) collective-permute-start(bf16[2,176,128]{2,1,0:T(8,128)(2,1)S(1)} %get-tuple-element.32), channel_id=1, source_target_pairs={{0,28},{4,8},{8,4},{12,16},{16,12},{20,24},{24,20},{28,0},{1,29},{... | collective-permute-start | bytes 270344 | tf_op jit(solution)/shard_map/ppermute | solution.py:463
  6.7 5.4 %collective-permute-start.2 = (bf16[32,8,128]{2,1,0:T(8,128)(2,1)S(1)}, bf16[32,8,128]{2,1,0:T(8,128)(2,1)S(1)}, u32[]{:S(2)}, u32[]{:S(2)}) collective-permute-start(bf16[32,8,128]{2,1,0:T(8,128)(2,1)S(1)} %get-tuple-element.37.refs_3_), channel_id=1, source_target_pairs={{0,1},{1,0},{2,3},{3,2},{4,5},{5,4},{6,7},{7,6},{8,9},{9,8},{10,11... | collective-permute-start | bytes 196616 | tf_op jit(solution)/shard_map/ppermute | solution.py:388
  8.3 6.2 %collective-permute-start.3 = (bf16[32,8,128]{2,1,0:T(8,128)(2,1)S(1)}, bf16[32,8,128]{2,1,0:T(8,128)(2,1)S(1)}, u32[]{:S(2)}, u32[]{:S(2)}) collective-permute-start(bf16[32,8,128]{2,1,0:T(8,128)(2,1)S(1)} %get-tuple-element.37.refs_3_), channel_id=1, source_target_pairs={{0,3},{1,2},{2,1},{3,0},{4,7},{5,6},{6,5},{7,4},{8,11},{9,10},{10,... | collective-permute-start | bytes 196616 | tf_op jit(solution)/shard_map/ppermute | solution.py:388
  10.7 5.9 %collective-permute-start.4 = (bf16[32,8,128]{2,1,0:T(8,128)(2,1)S(1)}, bf16[32,8,128]{2,1,0:T(8,128)(2,1)S(1)}, u32[]{:S(2)}, u32[]{:S(2)}) collective-permute-start(bf16[32,8,128]{2,1,0:T(8,128)(2,1)S(1)} %get-tuple-element.37.refs_3_), channel_id=1, source_target_pairs={{0,2},{1,3},{2,0},{3,1},{4,6},{5,7},{6,4},{7,5},{8,10},{9,11},{10,... | collective-permute-start | bytes 196616 | tf_op jit(solution)/shard_map/ppermute | solution.py:388
  17.6 6.0 %collective-permute-start.5 = (bf16[304,128]{1,0:T(8,128)(2,1)S(1)}, bf16[304,128]{1,0:T(8,128)(2,1)S(1)}, u32[]{:S(2)}, u32[]{:S(2)}) collective-permute-start(bf16[304,128]{1,0:T(8,128)(2,1)S(1)} %get-tuple-element.42), channel_id=1, source_target_pairs={{0,1},{1,0},{2,3},{3,2},{4,5},{5,4},{6,7},{7,6},{8,9},{9,8},{10,11... | collective-permute-start | bytes 233480 | tf_op jit(solution)/shard_map/ppermute | solution.py:388
  17.7 6.4 %collective-permute-start.6 = (bf16[304,128]{1,0:T(8,128)(2,1)S(1)}, bf16[304,128]{1,0:T(8,128)(2,1)S(1)}, u32[]{:S(2)}, u32[]{:S(2)}) collective-permute-start(bf16[304,128]{1,0:T(8,128)(2,1)S(1)} %get-tuple-element.43), channel_id=1, source_target_pairs={{0,3},{1,2},{2,1},{3,0},{4,7},{5,6},{6,5},{7,4},{8,11},{9,10},{10,... | collective-permute-start | bytes 233480 | tf_op jit(solution)/shard_map/ppermute | solution.py:388
  20.2 6.4 %collective-permute-start.7 = (bf16[256,128]{1,0:T(8,128)(2,1)S(1)}, bf16[256,128]{1,0:T(8,128)(2,1)S(1)}, u32[]{:S(2)}, u32[]{:S(2)}) collective-permute-start(bf16[256,128]{1,0:T(8,128)(2,1)S(1)} %get-tuple-element.45), channel_id=1, source_target_pairs={{0,2},{1,3},{2,0},{3,1},{4,6},{5,7},{6,4},{7,5},{8,10},{9,11},{10,... | collective-permute-start | bytes 196616 | tf_op jit(solution)/shard_map/ppermute | solution.py:388
